TPU v7x, 256 devices: a whole 4x4x8 slice. The times are simulated.
256 devices in a mesh: segment: 16 (over z, core), node: 16 (over y, x).
Axes of the slice: x: 4, y: 4, z: 8, core: 2. Of those that a mesh axis runs over, the one named last changes fastest.
Arguments:
- features: bfloat16 [2, 8192, 256], P(None, 'node'), may hold values from -6 to 6
- tiles: bfloat16 [2, 64, 8, 128, 128], P(None, 'node'), may hold values from -0.25 to 0.25
- tile_cols: int32 [2, 64, 8], P(None, 'node'), may hold values from 0 to 63, as said below
- tile_count: int32 [2, 64], P(None, 'node'), may hold values from 1 to 8
- weights: bfloat16 [16, 256, 256], P('segment'), may hold values from -0.375 to 0.375
Outputs:
- layer_outputs: bfloat16 [16, 2, 8192, 256], P('segment', None, 'node')
Inputs may be any that keep to these rules, and one draw needn't show every extreme that they name: `tile_cols`: with P = 4 block rows per node group of 512 nodes, the block column of a tile in block row b lies in group g - 1, g or g + 1 (counted modulo 8192 / 512 groups) where g = b // P is the group of b. `tile_count`: slots from the count on are padding.
All inputs are finite; a program needn't handle non-finite values.
Results may differ from a plain program's by a relative error of at most 0.011.
Values may be sent and summed in bfloat16 or wider, within the bound.
No kernel may reach another device: no remote copies, remote signals or barrier semaphores. Data moves between devices by JAX's collectives and lax.ppermute only.
A program may use at most 64 MiB of HBM per device.

v0:
```python
import jax
import jax.numpy as jnp
from jax import lax
from jax.sharding import PartitionSpec as P


def with_halo(array, sides, width):
    for axis, dim in sides:
        count, length = (lax.axis_size(axis), array.shape[dim])
        up = [(i, (i + 1) % count) for i in range(count)]
        down = [(j, i) for i, j in up]
        last = lax.slice_in_dim(array, length - width, length, axis=dim)
        first = lax.slice_in_dim(array, 0, width, axis=dim)
        before = lax.ppermute(last, axis, up)
        after = lax.ppermute(first, axis, down)
        array = jnp.concatenate([before, array, after], axis=dim)
    return array


def passed_along(block, axis, distance):
    devices = range(lax.axis_size(axis))
    route = [(i - distance, i) for i in devices if i - distance in devices]
    return lax.ppermute(block, axis, route)


def layer_rows(window, masked, columns, initial, weight, beta_mix):
    tile_size = masked.shape[-1]
    feature_width = window.shape[-1]
    grouped = window.reshape(window.shape[0] // tile_size, tile_size, feature_width)
    picked = grouped[columns]
    aggregate = jnp.einsum("bkij,bkjd->bid", masked, picked, preferred_element_type=jnp.float32)
    aggregate = aggregate.reshape(-1, feature_width)
    support = (0.9 * aggregate + 0.1 * initial.astype(jnp.float32)).astype(jnp.bfloat16)
    branch = jnp.dot(support, weight, preferred_element_type=jnp.float32)
    combined = (1.0 - beta_mix) * support.astype(jnp.float32) + beta_mix * branch
    return jnp.maximum(combined, 0.0).astype(jnp.bfloat16)


def on_device(features, tiles, tile_cols, tile_count, weights):
    segments = lax.axis_size("segment")
    groups = lax.axis_size("node")
    segment_id = lax.axis_index("segment")
    group_id = lax.axis_index("node")
    spans = features.shape[0]
    per_group = tiles.shape[1]
    total_blocks = per_group * groups
    first_block = (group_id - 1) * per_group
    local_cols = (tile_cols - first_block + total_blocks) % total_blocks
    slot_ids = jnp.arange(tiles.shape[2], dtype=jnp.int32)
    live = (slot_ids[None, None, :] < tile_count[:, :, None]).astype(jnp.bfloat16)
    masked = tiles * live[:, :, :, None, None]
    beta_mix = jnp.log(0.5 / (segment_id.astype(jnp.float32) + 1.0) + 1.0)
    weight = weights[0]
    rows_here = features.shape[1]

    def step(step_no, state_pair):
        incoming, stored = state_pair
        offset_now = step_no - segment_id
        active = (offset_now >= 0) & (offset_now < spans)
        span_id = jnp.clip(offset_now, 0, spans - 1)
        initial = lax.dynamic_index_in_dim(features, span_id, 0, keepdims=False)
        layer_input = jnp.where(segment_id == 0, initial, incoming)
        window = with_halo(layer_input, (("node", 0),), rows_here)
        span_tiles = lax.dynamic_index_in_dim(masked, span_id, 0, keepdims=False)
        span_cols = lax.dynamic_index_in_dim(local_cols, span_id, 0, keepdims=False)
        result = layer_rows(window, span_tiles, span_cols, initial, weight, beta_mix)
        updated = lax.dynamic_update_index_in_dim(stored, result, span_id, 0)
        stored = jnp.where(active, updated, stored)
        incoming = passed_along(result, "segment", 1)
        return (incoming, stored)

    start_pair = (
        jnp.zeros(features.shape[1:], jnp.bfloat16),
        jnp.zeros(features.shape, jnp.bfloat16),
    )
    final_pair = lax.fori_loop(0, segments + spans - 1, step, start_pair)
    stored = final_pair[1]
    return stored[None]


def solution(mesh):
    in_specs = (
        P(None, "node", None),
        P(None, "node", None, None, None),
        P(None, "node", None),
        P(None, "node"),
        P("segment", None, None),
    )
    out_specs = P("segment", None, "node", None)
    return jax.shard_map(
        on_device, mesh=mesh, in_specs=in_specs, out_specs=out_specs, check_vma=False
    )
```

profile of v0, /device:TPU:1, one launch (start us, length us, event | category | flops | bytes accessed | tf_op | source)
XLA Modules:
  0.0 378.1 jit_solution(2263287651215544484)
XLA Ops:
  5.6 372.4 %while.16 = (s32[]{:T(128)}, bf16[512,256]{1,0:T(8,128)(2,1)S(1)}, bf16[2,512,256]{2,1,0:T(8,128)(2,1)}, f32[]{:T(128)}, s32[]{:T(128)}, /*index=5*/bf16[2,4,8,1...) while((s32[]{:T(128)}, bf16[512,256]{1,0:T(8,128)(2,1)S(1)}, ...), condition=%wide.region_1.2_spmd, body=%wide.region_0.1_spmd.sunk | while | flops 339608672 | bytes 20059276 | solution.py:76
  18.5 6.6 %collective-permute-start.2 = (bf16[512,256]{1,0:T(8,128)(2,1)S(1)}, bf16[512,256]{1,0:T(8,128)(2,1)S(1)}, u32[]{:S(2)}, u32[]{:S(2)}) collective-permute-start(bf16[512,256]{1,0:T(8,128)(2,1)S(1)} %get-tuple-element.298), channel_id=1, source_target_pairs={{0,16},{16,32},{32,48},{48,64},{64,80},{80,96},{96,112},{112,128},... | collective-permute-start | bytes 786440 | tf_op jit(solution)/shard_map/while/body/eval_jaxpr/ppermute | solution.py:23
  28.6 4.9 %collective-permute-start = (bf16[512,256]{1,0:T(8,128)(2,1)S(1)}, bf16[512,256]{1,0:T(8,128)(2,1)S(1)}, u32[]{:S(2)}, u32[]{:S(2)}) collective-permute-start(bf16[512,256]{1,0:T(8,128)(2,1)S(1)} %bitcast_select_fusion.3), channel_id=1, source_target_pairs={{1,0},{2,1},{3,2},{4,3},{5,4},{6,5},{7,6},{8,7},{9,8},{10,9},{11,1... | collective-permute-start | bytes 786440 | tf_op jit(solution)/shard_map/while/body/eval_jaxpr/ppermute | solution.py:15
  40.1 6.9 %collective-permute-start.2 = (bf16[512,256]{1,0:T(8,128)(2,1)S(1)}, bf16[512,256]{1,0:T(8,128)(2,1)S(1)}, u32[]{:S(2)}, u32[]{:S(2)}) collective-permute-start(bf16[512,256]{1,0:T(8,128)(2,1)S(1)} %get-tuple-element.298), channel_id=1, source_target_pairs={{0,16},{16,32},{32,48},{48,64},{64,80},{80,96},{96,112},{112,128},... | collective-permute-start | bytes 786440 | tf_op jit(solution)/shard_map/while/body/eval_jaxpr/ppermute | solution.py:23
  50.5 4.9 %collective-permute-start = (bf16[512,256]{1,0:T(8,128)(2,1)S(1)}, bf16[512,256]{1,0:T(8,128)(2,1)S(1)}, u32[]{:S(2)}, u32[]{:S(2)}) collective-permute-start(bf16[512,256]{1,0:T(8,128)(2,1)S(1)} %bitcast_select_fusion.3), channel_id=1, source_target_pairs={{1,0},{2,1},{3,2},{4,3},{5,4},{6,5},{7,6},{8,7},{9,8},{10,9},{11,1... | collective-permute-start | bytes 786440 | tf_op jit(solution)/shard_map/while/body/eval_jaxpr/ppermute | solution.py:15
  62.0 6.9 %collective-permute-start.2 = (bf16[512,256]{1,0:T(8,128)(2,1)S(1)}, bf16[512,256]{1,0:T(8,128)(2,1)S(1)}, u32[]{:S(2)}, u32[]{:S(2)}) collective-permute-start(bf16[512,256]{1,0:T(8,128)(2,1)S(1)} %get-tuple-element.298), channel_id=1, source_target_pairs={{0,16},{16,32},{32,48},{48,64},{64,80},{80,96},{96,112},{112,128},... | collective-permute-start | bytes 786440 | tf_op jit(solution)/shard_map/while/body/eval_jaxpr/ppermute | solution.py:23
  72.4 4.9 %collective-permute-start = (bf16[512,256]{1,0:T(8,128)(2,1)S(1)}, bf16[512,256]{1,0:T(8,128)(2,1)S(1)}, u32[]{:S(2)}, u32[]{:S(2)}) collective-permute-start(bf16[512,256]{1,0:T(8,128)(2,1)S(1)} %bitcast_select_fusion.3), channel_id=1, source_target_pairs={{1,0},{2,1},{3,2},{4,3},{5,4},{6,5},{7,6},{8,7},{9,8},{10,9},{11,1... | collective-permute-start | bytes 786440 | tf_op jit(solution)/shard_map/while/body/eval_jaxpr/ppermute | solution.py:15
  83.9 8.2 %collective-permute-start.2 = (bf16[512,256]{1,0:T(8,128)(2,1)S(1)}, bf16[512,256]{1,0:T(8,128)(2,1)S(1)}, u32[]{:S(2)}, u32[]{:S(2)}) collective-permute-start(bf16[512,256]{1,0:T(8,128)(2,1)S(1)} %get-tuple-element.298), channel_id=1, source_target_pairs={{0,16},{16,32},{32,48},{48,64},{64,80},{80,96},{96,112},{112,128},... | collective-permute-start | bytes 786440 | tf_op jit(solution)/shard_map/while/body/eval_jaxpr/ppermute | solution.py:23
  95.5 4.9 %collective-permute-start = (bf16[512,256]{1,0:T(8,128)(2,1)S(1)}, bf16[512,256]{1,0:T(8,128)(2,1)S(1)}, u32[]{:S(2)}, u32[]{:S(2)}) collective-permute-start(bf16[512,256]{1,0:T(8,128)(2,1)S(1)} %bitcast_select_fusion.3), channel_id=1, source_target_pairs={{1,0},{2,1},{3,2},{4,3},{5,4},{6,5},{7,6},{8,7},{9,8},{10,9},{11,1... | collective-permute-start | bytes 786440 | tf_op jit(solution)/shard_map/while/body/eval_jaxpr/ppermute | solution.py:15
  107.1 6.9 %collective-permute-start.2 = (bf16[512,256]{1,0:T(8,128)(2,1)S(1)}, bf16[512,256]{1,0:T(8,128)(2,1)S(1)}, u32[]{:S(2)}, u32[]{:S(2)}) collective-permute-start(bf16[512,256]{1,0:T(8,128)(2,1)S(1)} %get-tuple-element.298), channel_id=1, source_target_pairs={{0,16},{16,32},{32,48},{48,64},{64,80},{80,96},{96,112},{112,128},... | collective-permute-start | bytes 786440 | tf_op jit(solution)/shard_map/while/body/eval_jaxpr/ppermute | solution.py:23
  117.4 4.9 %collective-permute-start = (bf16[512,256]{1,0:T(8,128)(2,1)S(1)}, bf16[512,256]{1,0:T(8,128)(2,1)S(1)}, u32[]{:S(2)}, u32[]{:S(2)}) collective-permute-start(bf16[512,256]{1,0:T(8,128)(2,1)S(1)} %bitcast_select_fusion.3), channel_id=1, source_target_pairs={{1,0},{2,1},{3,2},{4,3},{5,4},{6,5},{7,6},{8,7},{9,8},{10,9},{11,1... | collective-permute-start | bytes 786440 | tf_op jit(solution)/shard_map/while/body/eval_jaxpr/ppermute | solution.py:15
  128.9 6.8 %collective-permute-start.2 = (bf16[512,256]{1,0:T(8,128)(2,1)S(1)}, bf16[512,256]{1,0:T(8,128)(2,1)S(1)}, u32[]{:S(2)}, u32[]{:S(2)}) collective-permute-start(bf16[512,256]{1,0:T(8,128)(2,1)S(1)} %get-tuple-element.298), channel_id=1, source_target_pairs={{0,16},{16,32},{32,48},{48,64},{64,80},{80,96},{96,112},{112,128},... | collective-permute-start | bytes 786440 | tf_op jit(solution)/shard_map/while/body/eval_jaxpr/ppermute | solution.py:23
  139.1 4.9 %collective-permute-start = (bf16[512,256]{1,0:T(8,128)(2,1)S(1)}, bf16[512,256]{1,0:T(8,128)(2,1)S(1)}, u32[]{:S(2)}, u32[]{:S(2)}) collective-permute-start(bf16[512,256]{1,0:T(8,128)(2,1)S(1)} %bitcast_select_fusion.3), channel_id=1, source_target_pairs={{1,0},{2,1},{3,2},{4,3},{5,4},{6,5},{7,6},{8,7},{9,8},{10,9},{11,1... | collective-permute-start | bytes 786440 | tf_op jit(solution)/shard_map/while/body/eval_jaxpr/ppermute | solution.py:15
  150.6 6.8 %collective-permute-start.2 = (bf16[512,256]{1,0:T(8,128)(2,1)S(1)}, bf16[512,256]{1,0:T(8,128)(2,1)S(1)}, u32[]{:S(2)}, u32[]{:S(2)}) collective-permute-start(bf16[512,256]{1,0:T(8,128)(2,1)S(1)} %get-tuple-element.298), channel_id=1, source_target_pairs={{0,16},{16,32},{32,48},{48,64},{64,80},{80,96},{96,112},{112,128},... | collective-permute-start | bytes 786440 | tf_op jit(solution)/shard_map/while/body/eval_jaxpr/ppermute | solution.py:23
  160.8 4.9 %collective-permute-start = (bf16[512,256]{1,0:T(8,128)(2,1)S(1)}, bf16[512,256]{1,0:T(8,128)(2,1)S(1)}, u32[]{:S(2)}, u32[]{:S(2)}) collective-permute-start(bf16[512,256]{1,0:T(8,128)(2,1)S(1)} %bitcast_select_fusion.3), channel_id=1, source_target_pairs={{1,0},{2,1},{3,2},{4,3},{5,4},{6,5},{7,6},{8,7},{9,8},{10,9},{11,1... | collective-permute-start | bytes 786440 | tf_op jit(solution)/shard_map/while/body/eval_jaxpr/ppermute | solution.py:15
  172.4 6.8 %collective-permute-start.2 = (bf16[512,256]{1,0:T(8,128)(2,1)S(1)}, bf16[512,256]{1,0:T(8,128)(2,1)S(1)}, u32[]{:S(2)}, u32[]{:S(2)}) collective-permute-start(bf16[512,256]{1,0:T(8,128)(2,1)S(1)} %get-tuple-element.298), channel_id=1, source_target_pairs={{0,16},{16,32},{32,48},{48,64},{64,80},{80,96},{96,112},{112,128},... | collective-permute-start | bytes 786440 | tf_op jit(solution)/shard_map/while/body/eval_jaxpr/ppermute | solution.py:23
  182.6 4.9 %collective-permute-start = (bf16[512,256]{1,0:T(8,128)(2,1)S(1)}, bf16[512,256]{1,0:T(8,128)(2,1)S(1)}, u32[]{:S(2)}, u32[]{:S(2)}) collective-permute-start(bf16[512,256]{1,0:T(8,128)(2,1)S(1)} %bitcast_select_fusion.3), channel_id=1, source_target_pairs={{1,0},{2,1},{3,2},{4,3},{5,4},{6,5},{7,6},{8,7},{9,8},{10,9},{11,1... | collective-permute-start | bytes 786440 | tf_op jit(solution)/shard_map/while/body/eval_jaxpr/ppermute | solution.py:15
  194.1 6.7 %collective-permute-start.2 = (bf16[512,256]{1,0:T(8,128)(2,1)S(1)}, bf16[512,256]{1,0:T(8,128)(2,1)S(1)}, u32[]{:S(2)}, u32[]{:S(2)}) collective-permute-start(bf16[512,256]{1,0:T(8,128)(2,1)S(1)} %get-tuple-element.298), channel_id=1, source_target_pairs={{0,16},{16,32},{32,48},{48,64},{64,80},{80,96},{96,112},{112,128},... | collective-permute-start | bytes 786440 | tf_op jit(solution)/shard_map/while/body/eval_jaxpr/ppermute | solution.py:23
  204.3 4.9 %collective-permute-start = (bf16[512,256]{1,0:T(8,128)(2,1)S(1)}, bf16[512,256]{1,0:T(8,128)(2,1)S(1)}, u32[]{:S(2)}, u32[]{:S(2)}) collective-permute-start(bf16[512,256]{1,0:T(8,128)(2,1)S(1)} %bitcast_select_fusion.3), channel_id=1, source_target_pairs={{1,0},{2,1},{3,2},{4,3},{5,4},{6,5},{7,6},{8,7},{9,8},{10,9},{11,1... | collective-permute-start | bytes 786440 | tf_op jit(solution)/shard_map/while/body/eval_jaxpr/ppermute | solution.py:15
  215.8 6.8 %collective-permute-start.2 = (bf16[512,256]{1,0:T(8,128)(2,1)S(1)}, bf16[512,256]{1,0:T(8,128)(2,1)S(1)}, u32[]{:S(2)}, u32[]{:S(2)}) collective-permute-start(bf16[512,256]{1,0:T(8,128)(2,1)S(1)} %get-tuple-element.298), channel_id=1, source_target_pairs={{0,16},{16,32},{32,48},{48,64},{64,80},{80,96},{96,112},{112,128},... | collective-permute-start | bytes 786440 | tf_op jit(solution)/shard_map/while/body/eval_jaxpr/ppermute | solution.py:23
  226.0 4.9 %collective-permute-start = (bf16[512,256]{1,0:T(8,128)(2,1)S(1)}, bf16[512,256]{1,0:T(8,128)(2,1)S(1)}, u32[]{:S(2)}, u32[]{:S(2)}) collective-permute-start(bf16[512,256]{1,0:T(8,128)(2,1)S(1)} %bitcast_select_fusion.3), channel_id=1, source_target_pairs={{1,0},{2,1},{3,2},{4,3},{5,4},{6,5},{7,6},{8,7},{9,8},{10,9},{11,1... | collective-permute-start | bytes 786440 | tf_op jit(solution)/shard_map/while/body/eval_jaxpr/ppermute | solution.py:15
  237.6 6.8 %collective-permute-start.2 = (bf16[512,256]{1,0:T(8,128)(2,1)S(1)}, bf16[512,256]{1,0:T(8,128)(2,1)S(1)}, u32[]{:S(2)}, u32[]{:S(2)}) collective-permute-start(bf16[512,256]{1,0:T(8,128)(2,1)S(1)} %get-tuple-element.298), channel_id=1, source_target_pairs={{0,16},{16,32},{32,48},{48,64},{64,80},{80,96},{96,112},{112,128},... | collective-permute-start | bytes 786440 | tf_op jit(solution)/shard_map/while/body/eval_jaxpr/ppermute | solution.py:23
  247.8 4.9 %collective-permute-start = (bf16[512,256]{1,0:T(8,128)(2,1)S(1)}, bf16[512,256]{1,0:T(8,128)(2,1)S(1)}, u32[]{:S(2)}, u32[]{:S(2)}) collective-permute-start(bf16[512,256]{1,0:T(8,128)(2,1)S(1)} %bitcast_select_fusion.3), channel_id=1, source_target_pairs={{1,0},{2,1},{3,2},{4,3},{5,4},{6,5},{7,6},{8,7},{9,8},{10,9},{11,1... | collective-permute-start | bytes 786440 | tf_op jit(solution)/shard_map/while/body/eval_jaxpr/ppermute | solution.py:15
  259.3 6.8 %collective-permute-start.2 = (bf16[512,256]{1,0:T(8,128)(2,1)S(1)}, bf16[512,256]{1,0:T(8,128)(2,1)S(1)}, u32[]{:S(2)}, u32[]{:S(2)}) collective-permute-start(bf16[512,256]{1,0:T(8,128)(2,1)S(1)} %get-tuple-element.298), channel_id=1, source_target_pairs={{0,16},{16,32},{32,48},{48,64},{64,80},{80,96},{96,112},{112,128},... | collective-permute-start | bytes 786440 | tf_op jit(solution)/shard_map/while/body/eval_jaxpr/ppermute | solution.py:23
  269.5 4.9 %collective-permute-start = (bf16[512,256]{1,0:T(8,128)(2,1)S(1)}, bf16[512,256]{1,0:T(8,128)(2,1)S(1)}, u32[]{:S(2)}, u32[]{:S(2)}) collective-permute-start(bf16[512,256]{1,0:T(8,128)(2,1)S(1)} %bitcast_select_fusion.3), channel_id=1, source_target_pairs={{1,0},{2,1},{3,2},{4,3},{5,4},{6,5},{7,6},{8,7},{9,8},{10,9},{11,1... | collective-permute-start | bytes 786440 | tf_op jit(solution)/shard_map/while/body/eval_jaxpr/ppermute | solution.py:15
  281.1 6.7 %collective-permute-start.2 = (bf16[512,256]{1,0:T(8,128)(2,1)S(1)}, bf16[512,256]{1,0:T(8,128)(2,1)S(1)}, u32[]{:S(2)}, u32[]{:S(2)}) collective-permute-start(bf16[512,256]{1,0:T(8,128)(2,1)S(1)} %get-tuple-element.298), channel_id=1, source_target_pairs={{0,16},{16,32},{32,48},{48,64},{64,80},{80,96},{96,112},{112,128},... | collective-permute-start | bytes 786440 | tf_op jit(solution)/shard_map/while/body/eval_jaxpr/ppermute | solution.py:23
  291.2 4.9 %collective-permute-start = (bf16[512,256]{1,0:T(8,128)(2,1)S(1)}, bf16[512,256]{1,0:T(8,128)(2,1)S(1)}, u32[]{:S(2)}, u32[]{:S(2)}) collective-permute-start(bf16[512,256]{1,0:T(8,128)(2,1)S(1)} %bitcast_select_fusion.3), channel_id=1, source_target_pairs={{1,0},{2,1},{3,2},{4,3},{5,4},{6,5},{7,6},{8,7},{9,8},{10,9},{11,1... | collective-permute-start | bytes 786440 | tf_op jit(solution)/shard_map/while/body/eval_jaxpr/ppermute | solution.py:15
  302.8 6.8 %collective-permute-start.2 = (bf16[512,256]{1,0:T(8,128)(2,1)S(1)}, bf16[512,256]{1,0:T(8,128)(2,1)S(1)}, u32[]{:S(2)}, u32[]{:S(2)}) collective-permute-start(bf16[512,256]{1,0:T(8,128)(2,1)S(1)} %get-tuple-element.298), channel_id=1, source_target_pairs={{0,16},{16,32},{32,48},{48,64},{64,80},{80,96},{96,112},{112,128},... | collective-permute-start | bytes 786440 | tf_op jit(solution)/shard_map/while/body/eval_jaxpr/ppermute | solution.py:23
  324.5 6.8 %collective-permute-start.2 = (bf16[512,256]{1,0:T(8,128)(2,1)S(1)}, bf16[512,256]{1,0:T(8,128)(2,1)S(1)}, u32[]{:S(2)}, u32[]{:S(2)}) collective-permute-start(bf16[512,256]{1,0:T(8,128)(2,1)S(1)} %get-tuple-element.298), channel_id=1, source_target_pairs={{0,16},{16,32},{32,48},{48,64},{64,80},{80,96},{96,112},{112,128},... | collective-permute-start | bytes 786440 | tf_op jit(solution)/shard_map/while/body/eval_jaxpr/ppermute | solution.py:23
  346.3 6.8 %collective-permute-start.2 = (bf16[512,256]{1,0:T(8,128)(2,1)S(1)}, bf16[512,256]{1,0:T(8,128)(2,1)S(1)}, u32[]{:S(2)}, u32[]{:S(2)}) collective-permute-start(bf16[512,256]{1,0:T(8,128)(2,1)S(1)} %get-tuple-element.298), channel_id=1, source_target_pairs={{0,16},{16,32},{32,48},{48,64},{64,80},{80,96},{96,112},{112,128},... | collective-permute-start | bytes 786440 | tf_op jit(solution)/shard_map/while/body/eval_jaxpr/ppermute | solution.py:23
  356.5 4.9 %collective-permute-start = (bf16[512,256]{1,0:T(8,128)(2,1)S(1)}, bf16[512,256]{1,0:T(8,128)(2,1)S(1)}, u32[]{:S(2)}, u32[]{:S(2)}) collective-permute-start(bf16[512,256]{1,0:T(8,128)(2,1)S(1)} %bitcast_select_fusion.3), channel_id=1, source_target_pairs={{1,0},{2,1},{3,2},{4,3},{5,4},{6,5},{7,6},{8,7},{9,8},{10,9},{11,1... | collective-permute-start | bytes 786440 | tf_op jit(solution)/shard_map/while/body/eval_jaxpr/ppermute | solution.py:15
  368.0 6.7 %collective-permute-start.2 = (bf16[512,256]{1,0:T(8,128)(2,1)S(1)}, bf16[512,256]{1,0:T(8,128)(2,1)S(1)}, u32[]{:S(2)}, u32[]{:S(2)}) collective-permute-start(bf16[512,256]{1,0:T(8,128)(2,1)S(1)} %get-tuple-element.298), channel_id=1, source_target_pairs={{0,16},{16,32},{32,48},{48,64},{64,80},{80,96},{96,112},{112,128},... | collective-permute-start | bytes 786440 | tf_op jit(solution)/shard_map/while/body/eval_jaxpr/ppermute | solution.py:23
  (301 shorter events, 190.8 us)
Async XLA Ops:
  5.7 9.9 %collective-permute-start.1 = (bf16[512,256]{1,0:T(8,128)(2,1)S(1)}, bf16[512,256]{1,0:T(8,128)(2,1)S(1)}, u32[]{:S(2)}, u32[]{:S(2)}) collective-permute-start(bf16[512,256]{1,0:T(8,128)(2,1)S(1)} %bitcast_select_fusion.3), channel_id=1, source_target_pairs={{0,1},{1,2},{2,3},{3,4},{4,5},{5,6},{6,7},{7,8},{8,9},{9,10},{10,1... | collective-permute-start | bytes 786440 | tf_op jit(solution)/shard_map/while/body/eval_jaxpr/ppermute | solution.py:14
  18.5 9.9 %collective-permute-start.2 = (bf16[512,256]{1,0:T(8,128)(2,1)S(1)}, bf16[512,256]{1,0:T(8,128)(2,1)S(1)}, u32[]{:S(2)}, u32[]{:S(2)}) collective-permute-start(bf16[512,256]{1,0:T(8,128)(2,1)S(1)} %get-tuple-element.298), channel_id=1, source_target_pairs={{0,16},{16,32},{32,48},{48,64},{64,80},{80,96},{96,112},{112,128},... | collective-permute-start | bytes 786440 | tf_op jit(solution)/shard_map/while/body/eval_jaxpr/ppermute | solution.py:23
  28.5 8.7 %collective-permute-start.1 = (bf16[512,256]{1,0:T(8,128)(2,1)S(1)}, bf16[512,256]{1,0:T(8,128)(2,1)S(1)}, u32[]{:S(2)}, u32[]{:S(2)}) collective-permute-start(bf16[512,256]{1,0:T(8,128)(2,1)S(1)} %bitcast_select_fusion.3), channel_id=1, source_target_pairs={{0,1},{1,2},{2,3},{3,4},{4,5},{5,6},{6,7},{7,8},{8,9},{9,10},{10,1... | collective-permute-start | bytes 786440 | tf_op jit(solution)/shard_map/while/body/eval_jaxpr/ppermute | solution.py:14
  40.1 10.2 %collective-permute-start.2 = (bf16[512,256]{1,0:T(8,128)(2,1)S(1)}, bf16[512,256]{1,0:T(8,128)(2,1)S(1)}, u32[]{:S(2)}, u32[]{:S(2)}) collective-permute-start(bf16[512,256]{1,0:T(8,128)(2,1)S(1)} %get-tuple-element.298), channel_id=1, source_target_pairs={{0,16},{16,32},{32,48},{48,64},{64,80},{80,96},{96,112},{112,128},... | collective-permute-start | bytes 786440 | tf_op jit(solution)/shard_map/while/body/eval_jaxpr/ppermute | solution.py:23
  50.4 8.7 %collective-permute-start.1 = (bf16[512,256]{1,0:T(8,128)(2,1)S(1)}, bf16[512,256]{1,0:T(8,128)(2,1)S(1)}, u32[]{:S(2)}, u32[]{:S(2)}) collective-permute-start(bf16[512,256]{1,0:T(8,128)(2,1)S(1)} %bitcast_select_fusion.3), channel_id=1, source_target_pairs={{0,1},{1,2},{2,3},{3,4},{4,5},{5,6},{6,7},{7,8},{8,9},{9,10},{10,1... | collective-permute-start | bytes 786440 | tf_op jit(solution)/shard_map/while/body/eval_jaxpr/ppermute | solution.py:14
  62.0 10.2 %collective-permute-start.2 = (bf16[512,256]{1,0:T(8,128)(2,1)S(1)}, bf16[512,256]{1,0:T(8,128)(2,1)S(1)}, u32[]{:S(2)}, u32[]{:S(2)}) collective-permute-start(bf16[512,256]{1,0:T(8,128)(2,1)S(1)} %get-tuple-element.298), channel_id=1, source_target_pairs={{0,16},{16,32},{32,48},{48,64},{64,80},{80,96},{96,112},{112,128},... | collective-permute-start | bytes 786440 | tf_op jit(solution)/shard_map/while/body/eval_jaxpr/ppermute | solution.py:23
  72.3 8.7 %collective-permute-start.1 = (bf16[512,256]{1,0:T(8,128)(2,1)S(1)}, bf16[512,256]{1,0:T(8,128)(2,1)S(1)}, u32[]{:S(2)}, u32[]{:S(2)}) collective-permute-start(bf16[512,256]{1,0:T(8,128)(2,1)S(1)} %bitcast_select_fusion.3), channel_id=1, source_target_pairs={{0,1},{1,2},{2,3},{3,4},{4,5},{5,6},{6,7},{7,8},{8,9},{9,10},{10,1... | collective-permute-start | bytes 786440 | tf_op jit(solution)/shard_map/while/body/eval_jaxpr/ppermute | solution.py:14
  83.9 11.5 %collective-permute-start.2 = (bf16[512,256]{1,0:T(8,128)(2,1)S(1)}, bf16[512,256]{1,0:T(8,128)(2,1)S(1)}, u32[]{:S(2)}, u32[]{:S(2)}) collective-permute-start(bf16[512,256]{1,0:T(8,128)(2,1)S(1)} %get-tuple-element.298), channel_id=1, source_target_pairs={{0,16},{16,32},{32,48},{48,64},{64,80},{80,96},{96,112},{112,128},... | collective-permute-start | bytes 786440 | tf_op jit(solution)/shard_map/while/body/eval_jaxpr/ppermute | solution.py:23
  95.4 8.7 %collective-permute-start.1 = (bf16[512,256]{1,0:T(8,128)(2,1)S(1)}, bf16[512,256]{1,0:T(8,128)(2,1)S(1)}, u32[]{:S(2)}, u32[]{:S(2)}) collective-permute-start(bf16[512,256]{1,0:T(8,128)(2,1)S(1)} %bitcast_select_fusion.3), channel_id=1, source_target_pairs={{0,1},{1,2},{2,3},{3,4},{4,5},{5,6},{6,7},{7,8},{8,9},{9,10},{10,1... | collective-permute-start | bytes 786440 | tf_op jit(solution)/shard_map/while/body/eval_jaxpr/ppermute | solution.py:14
  107.1 10.2 %collective-permute-start.2 = (bf16[512,256]{1,0:T(8,128)(2,1)S(1)}, bf16[512,256]{1,0:T(8,128)(2,1)S(1)}, u32[]{:S(2)}, u32[]{:S(2)}) collective-permute-start(bf16[512,256]{1,0:T(8,128)(2,1)S(1)} %get-tuple-element.298), channel_id=1, source_target_pairs={{0,16},{16,32},{32,48},{48,64},{64,80},{80,96},{96,112},{112,128},... | collective-permute-start | bytes 786440 | tf_op jit(solution)/shard_map/while/body/eval_jaxpr/ppermute | solution.py:23
  117.3 8.7 %collective-permute-start.1 = (bf16[512,256]{1,0:T(8,128)(2,1)S(1)}, bf16[512,256]{1,0:T(8,128)(2,1)S(1)}, u32[]{:S(2)}, u32[]{:S(2)}) collective-permute-start(bf16[512,256]{1,0:T(8,128)(2,1)S(1)} %bitcast_select_fusion.3), channel_id=1, source_target_pairs={{0,1},{1,2},{2,3},{3,4},{4,5},{5,6},{6,7},{7,8},{8,9},{9,10},{10,1... | collective-permute-start | bytes 786440 | tf_op jit(solution)/shard_map/while/body/eval_jaxpr/ppermute | solution.py:14
  128.9 10.1 %collective-permute-start.2 = (bf16[512,256]{1,0:T(8,128)(2,1)S(1)}, bf16[512,256]{1,0:T(8,128)(2,1)S(1)}, u32[]{:S(2)}, u32[]{:S(2)}) collective-permute-start(bf16[512,256]{1,0:T(8,128)(2,1)S(1)} %get-tuple-element.298), channel_id=1, source_target_pairs={{0,16},{16,32},{32,48},{48,64},{64,80},{80,96},{96,112},{112,128},... | collective-permute-start | bytes 786440 | tf_op jit(solution)/shard_map/while/body/eval_jaxpr/ppermute | solution.py:23
  139.0 8.7 %collective-permute-start.1 = (bf16[512,256]{1,0:T(8,128)(2,1)S(1)}, bf16[512,256]{1,0:T(8,128)(2,1)S(1)}, u32[]{:S(2)}, u32[]{:S(2)}) collective-permute-start(bf16[512,256]{1,0:T(8,128)(2,1)S(1)} %bitcast_select_fusion.3), channel_id=1, source_target_pairs={{0,1},{1,2},{2,3},{3,4},{4,5},{5,6},{6,7},{7,8},{8,9},{9,10},{10,1... | collective-permute-start | bytes 786440 | tf_op jit(solution)/shard_map/while/body/eval_jaxpr/ppermute | solution.py:14
  150.6 10.1 %collective-permute-start.2 = (bf16[512,256]{1,0:T(8,128)(2,1)S(1)}, bf16[512,256]{1,0:T(8,128)(2,1)S(1)}, u32[]{:S(2)}, u32[]{:S(2)}) collective-permute-start(bf16[512,256]{1,0:T(8,128)(2,1)S(1)} %get-tuple-element.298), channel_id=1, source_target_pairs={{0,16},{16,32},{32,48},{48,64},{64,80},{80,96},{96,112},{112,128},... | collective-permute-start | bytes 786440 | tf_op jit(solution)/shard_map/while/body/eval_jaxpr/ppermute | solution.py:23
  160.7 8.7 %collective-permute-start.1 = (bf16[512,256]{1,0:T(8,128)(2,1)S(1)}, bf16[512,256]{1,0:T(8,128)(2,1)S(1)}, u32[]{:S(2)}, u32[]{:S(2)}) collective-permute-start(bf16[512,256]{1,0:T(8,128)(2,1)S(1)} %bitcast_select_fusion.3), channel_id=1, source_target_pairs={{0,1},{1,2},{2,3},{3,4},{4,5},{5,6},{6,7},{7,8},{8,9},{9,10},{10,1... | collective-permute-start | bytes 786440 | tf_op jit(solution)/shard_map/while/body/eval_jaxpr/ppermute | solution.py:14
  172.4 10.1 %collective-permute-start.2 = (bf16[512,256]{1,0:T(8,128)(2,1)S(1)}, bf16[512,256]{1,0:T(8,128)(2,1)S(1)}, u32[]{:S(2)}, u32[]{:S(2)}) collective-permute-start(bf16[512,256]{1,0:T(8,128)(2,1)S(1)} %get-tuple-element.298), channel_id=1, source_target_pairs={{0,16},{16,32},{32,48},{48,64},{64,80},{80,96},{96,112},{112,128},... | collective-permute-start | bytes 786440 | tf_op jit(solution)/shard_map/while/body/eval_jaxpr/ppermute | solution.py:23
  182.5 8.7 %collective-permute-start.1 = (bf16[512,256]{1,0:T(8,128)(2,1)S(1)}, bf16[512,256]{1,0:T(8,128)(2,1)S(1)}, u32[]{:S(2)}, u32[]{:S(2)}) collective-permute-start(bf16[512,256]{1,0:T(8,128)(2,1)S(1)} %bitcast_select_fusion.3), channel_id=1, source_target_pairs={{0,1},{1,2},{2,3},{3,4},{4,5},{5,6},{6,7},{7,8},{8,9},{9,10},{10,1... | collective-permute-start | bytes 786440 | tf_op jit(solution)/shard_map/while/body/eval_jaxpr/ppermute | solution.py:14
  194.1 10.0 %collective-permute-start.2 = (bf16[512,256]{1,0:T(8,128)(2,1)S(1)}, bf16[512,256]{1,0:T(8,128)(2,1)S(1)}, u32[]{:S(2)}, u32[]{:S(2)}) collective-permute-start(bf16[512,256]{1,0:T(8,128)(2,1)S(1)} %get-tuple-element.298), channel_id=1, source_target_pairs={{0,16},{16,32},{32,48},{48,64},{64,80},{80,96},{96,112},{112,128},... | collective-permute-start | bytes 786440 | tf_op jit(solution)/shard_map/while/body/eval_jaxpr/ppermute | solution.py:23
  204.2 8.7 %collective-permute-start.1 = (bf16[512,256]{1,0:T(8,128)(2,1)S(1)}, bf16[512,256]{1,0:T(8,128)(2,1)S(1)}, u32[]{:S(2)}, u32[]{:S(2)}) collective-permute-start(bf16[512,256]{1,0:T(8,128)(2,1)S(1)} %bitcast_select_fusion.3), channel_id=1, source_target_pairs={{0,1},{1,2},{2,3},{3,4},{4,5},{5,6},{6,7},{7,8},{8,9},{9,10},{10,1... | collective-permute-start | bytes 786440 | tf_op jit(solution)/shard_map/while/body/eval_jaxpr/ppermute | solution.py:14
  215.8 10.1 %collective-permute-start.2 = (bf16[512,256]{1,0:T(8,128)(2,1)S(1)}, bf16[512,256]{1,0:T(8,128)(2,1)S(1)}, u32[]{:S(2)}, u32[]{:S(2)}) collective-permute-start(bf16[512,256]{1,0:T(8,128)(2,1)S(1)} %get-tuple-element.298), channel_id=1, source_target_pairs={{0,16},{16,32},{32,48},{48,64},{64,80},{80,96},{96,112},{112,128},... | collective-permute-start | bytes 786440 | tf_op jit(solution)/shard_map/while/body/eval_jaxpr/ppermute | solution.py:23
  237.6 10.1 %collective-permute-start.2 = (bf16[512,256]{1,0:T(8,128)(2,1)S(1)}, bf16[512,256]{1,0:T(8,128)(2,1)S(1)}, u32[]{:S(2)}, u32[]{:S(2)}) collective-permute-start(bf16[512,256]{1,0:T(8,128)(2,1)S(1)} %get-tuple-element.298), channel_id=1, source_target_pairs={{0,16},{16,32},{32,48},{48,64},{64,80},{80,96},{96,112},{112,128},... | collective-permute-start | bytes 786440 | tf_op jit(solution)/shard_map/while/body/eval_jaxpr/ppermute | solution.py:23
  247.7 8.7 %collective-permute-start.1 = (bf16[512,256]{1,0:T(8,128)(2,1)S(1)}, bf16[512,256]{1,0:T(8,128)(2,1)S(1)}, u32[]{:S(2)}, u32[]{:S(2)}) collective-permute-start(bf16[512,256]{1,0:T(8,128)(2,1)S(1)} %bitcast_select_fusion.3), channel_id=1, source_target_pairs={{0,1},{1,2},{2,3},{3,4},{4,5},{5,6},{6,7},{7,8},{8,9},{9,10},{10,1... | collective-permute-start | bytes 786440 | tf_op jit(solution)/shard_map/while/body/eval_jaxpr/ppermute | solution.py:14
  259.3 10.1 %collective-permute-start.2 = (bf16[512,256]{1,0:T(8,128)(2,1)S(1)}, bf16[512,256]{1,0:T(8,128)(2,1)S(1)}, u32[]{:S(2)}, u32[]{:S(2)}) collective-permute-start(bf16[512,256]{1,0:T(8,128)(2,1)S(1)} %get-tuple-element.298), channel_id=1, source_target_pairs={{0,16},{16,32},{32,48},{48,64},{64,80},{80,96},{96,112},{112,128},... | collective-permute-start | bytes 786440 | tf_op jit(solution)/shard_map/while/body/eval_jaxpr/ppermute | solution.py:23
  269.4 8.7 %collective-permute-start.1 = (bf16[512,256]{1,0:T(8,128)(2,1)S(1)}, bf16[512,256]{1,0:T(8,128)(2,1)S(1)}, u32[]{:S(2)}, u32[]{:S(2)}) collective-permute-start(bf16[512,256]{1,0:T(8,128)(2,1)S(1)} %bitcast_select_fusion.3), channel_id=1, source_target_pairs={{0,1},{1,2},{2,3},{3,4},{4,5},{5,6},{6,7},{7,8},{8,9},{9,10},{10,1... | collective-permute-start | bytes 786440 | tf_op jit(solution)/shard_map/while/body/eval_jaxpr/ppermute | solution.py:14
  281.1 10.0 %collective-permute-start.2 = (bf16[512,256]{1,0:T(8,128)(2,1)S(1)}, bf16[512,256]{1,0:T(8,128)(2,1)S(1)}, u32[]{:S(2)}, u32[]{:S(2)}) collective-permute-start(bf16[512,256]{1,0:T(8,128)(2,1)S(1)} %get-tuple-element.298), channel_id=1, source_target_pairs={{0,16},{16,32},{32,48},{48,64},{64,80},{80,96},{96,112},{112,128},... | collective-permute-start | bytes 786440 | tf_op jit(solution)/shard_map/while/body/eval_jaxpr/ppermute | solution.py:23
  291.2 8.7 %collective-permute-start.1 = (bf16[512,256]{1,0:T(8,128)(2,1)S(1)}, bf16[512,256]{1,0:T(8,128)(2,1)S(1)}, u32[]{:S(2)}, u32[]{:S(2)}) collective-permute-start(bf16[512,256]{1,0:T(8,128)(2,1)S(1)} %bitcast_select_fusion.3), channel_id=1, source_target_pairs={{0,1},{1,2},{2,3},{3,4},{4,5},{5,6},{6,7},{7,8},{8,9},{9,10},{10,1... | collective-permute-start | bytes 786440 | tf_op jit(solution)/shard_map/while/body/eval_jaxpr/ppermute | solution.py:14
  302.8 10.1 %collective-permute-start.2 = (bf16[512,256]{1,0:T(8,128)(2,1)S(1)}, bf16[512,256]{1,0:T(8,128)(2,1)S(1)}, u32[]{:S(2)}, u32[]{:S(2)}) collective-permute-start(bf16[512,256]{1,0:T(8,128)(2,1)S(1)} %get-tuple-element.298), channel_id=1, source_target_pairs={{0,16},{16,32},{32,48},{48,64},{64,80},{80,96},{96,112},{112,128},... | collective-permute-start | bytes 786440 | tf_op jit(solution)/shard_map/while/body/eval_jaxpr/ppermute | solution.py:23
  312.9 8.7 %collective-permute-start.1 = (bf16[512,256]{1,0:T(8,128)(2,1)S(1)}, bf16[512,256]{1,0:T(8,128)(2,1)S(1)}, u32[]{:S(2)}, u32[]{:S(2)}) collective-permute-start(bf16[512,256]{1,0:T(8,128)(2,1)S(1)} %bitcast_select_fusion.3), channel_id=1, source_target_pairs={{0,1},{1,2},{2,3},{3,4},{4,5},{5,6},{6,7},{7,8},{8,9},{9,10},{10,1... | collective-permute-start | bytes 786440 | tf_op jit(solution)/shard_map/while/body/eval_jaxpr/ppermute | solution.py:14
  324.5 10.1 %collective-permute-start.2 = (bf16[512,256]{1,0:T(8,128)(2,1)S(1)}, bf16[512,256]{1,0:T(8,128)(2,1)S(1)}, u32[]{:S(2)}, u32[]{:S(2)}) collective-permute-start(bf16[512,256]{1,0:T(8,128)(2,1)S(1)} %get-tuple-element.298), channel_id=1, source_target_pairs={{0,16},{16,32},{32,48},{48,64},{64,80},{80,96},{96,112},{112,128},... | collective-permute-start | bytes 786440 | tf_op jit(solution)/shard_map/while/body/eval_jaxpr/ppermute | solution.py:23
  346.3 10.1 %collective-permute-start.2 = (bf16[512,256]{1,0:T(8,128)(2,1)S(1)}, bf16[512,256]{1,0:T(8,128)(2,1)S(1)}, u32[]{:S(2)}, u32[]{:S(2)}) collective-permute-start(bf16[512,256]{1,0:T(8,128)(2,1)S(1)} %get-tuple-element.298), channel_id=1, source_target_pairs={{0,16},{16,32},{32,48},{48,64},{64,80},{80,96},{96,112},{112,128},... | collective-permute-start | bytes 786440 | tf_op jit(solution)/shard_map/while/body/eval_jaxpr/ppermute | solution.py:23
  356.4 8.7 %collective-permute-start.1 = (bf16[512,256]{1,0:T(8,128)(2,1)S(1)}, bf16[512,256]{1,0:T(8,128)(2,1)S(1)}, u32[]{:S(2)}, u32[]{:S(2)}) collective-permute-start(bf16[512,256]{1,0:T(8,128)(2,1)S(1)} %bitcast_select_fusion.3), channel_id=1, source_target_pairs={{0,1},{1,2},{2,3},{3,4},{4,5},{5,6},{6,7},{7,8},{8,9},{9,10},{10,1... | collective-permute-start | bytes 786440 | tf_op jit(solution)/shard_map/while/body/eval_jaxpr/ppermute | solution.py:14
  368.0 10.0 %collective-permute-start.2 = (bf16[512,256]{1,0:T(8,128)(2,1)S(1)}, bf16[512,256]{1,0:T(8,128)(2,1)S(1)}, u32[]{:S(2)}, u32[]{:S(2)}) collective-permute-start(bf16[512,256]{1,0:T(8,128)(2,1)S(1)} %get-tuple-element.298), channel_id=1, source_target_pairs={{0,16},{16,32},{32,48},{48,64},{64,80},{80,96},{96,112},{112,128},... | collective-permute-start | bytes 786440 | tf_op jit(solution)/shard_map/while/body/eval_jaxpr/ppermute | solution.py:23
  (55 other events, 376.2 us)
where the time goes:
time: 379 us; the launch traced here: 378 us
  starting transfers between devices  203 us (54%)
  waiting for transfers between devices  117 us (31%)
  matrix products  35.1 us (9%)
  local copies, waits for them, and re-layouts  14.1 us (4%)
  other arithmetic  7.48 us (2%)
    ppermute x17, starting transfers between devices, passed_along(): return lax.ppermute(block, axis, route)  117 us
    ppermute x17, starting transfers between devices, with_halo(): after = lax.ppermute(first, axis, down)  82.8 us
    ppermute x17, waiting for transfers between devices, with_halo(): before = lax.ppermute(last, axis, up)  61 us
    ppermute x17, waiting for transfers between devices, passed_along(): return lax.ppermute(block, axis, route)  55.9 us
    dot_general x17, matrix products, layer_rows(): jnp.einsum('bkij,bkjd->bid', masked, picked, preferred_element_type=jnp.f...  30.4 us
    gather x17, local copies, waits for them, and re-layouts, layer_rows(): picked = grouped[columns]  11.6 us
  transfers between devices with their start and end apart: 51, of which 34 were waited for; matrix products, arithmetic and copies ran while one was open for 0% of the time, Pallas kernels for 0%

commit v1 on v0

v1 whole, which is shorter than its diff:
```python
import math

import jax
import jax.numpy as jnp
from jax import lax
from jax.experimental import pallas as pl
from jax.experimental.pallas import tpu as pltpu
from jax.sharding import PartitionSpec as P

BLOCK = 128
HALF = 256
VMEM = pl.BlockSpec(memory_space=pltpu.VMEM)
SMEM = pl.BlockSpec(memory_space=pltpu.SMEM)


def dense_kernel(places_ref, tiles_ref, dense_ref, total_ref):
    total_ref[...] = jnp.zeros_like(total_ref)
    blocks, slots = places_ref.shape
    for b in range(blocks):
        rows = pl.ds(b * BLOCK, BLOCK)
        for k in range(slots):
            place = places_ref[b, k]
            chunk = place // 2
            tile = tiles_ref[pl.ds((b * slots + k) * BLOCK, BLOCK), :].astype(jnp.float32)

            @pl.when((place < 12) & (place % 2 == 0))
            def _():
                total_ref[chunk, rows, 0:BLOCK] += tile

            @pl.when((place < 12) & (place % 2 == 1))
            def _():
                total_ref[chunk, rows, BLOCK:HALF] += tile

    dense_ref[...] = total_ref[...].astype(jnp.bfloat16)


def dense_adjacency(places, tiles):
    rows = places.shape[0] * BLOCK
    return pl.pallas_call(
        dense_kernel,
        out_shape=jax.ShapeDtypeStruct((6, rows, HALF), jnp.bfloat16),
        in_specs=[SMEM, VMEM],
        out_specs=VMEM,
        scratch_shapes=[pltpu.VMEM((6, rows, HALF), jnp.float32)],
        compiler_params=pltpu.CompilerParams(vmem_limit_bytes=16 << 20),
    )(places, tiles)


def product(dense_ref, chunk, rows_ref):
    first = jnp.dot(dense_ref[chunk], rows_ref[0:HALF, :], preferred_element_type=jnp.float32)
    second = jnp.dot(dense_ref[chunk + 1], rows_ref[HALF:, :], preferred_element_type=jnp.float32)
    return first + second


def own_kernel(dense_ref, own_ref, part_ref):
    part_ref[...] = product(dense_ref, 0, own_ref)


def own_part(dense, own):
    return pl.pallas_call(
        own_kernel,
        out_shape=jax.ShapeDtypeStruct(own.shape, jnp.float32),
        in_specs=[VMEM, VMEM],
        out_specs=VMEM,
        cost_estimate=pl.CostEstimate(flops=2 * 512 * 512 * 256, bytes_accessed=1 << 20, transcendentals=0),
    )(dense, own)


def layer_kernel(beta, dense_ref, part_ref, beside_ref, across_ref, initial_ref, weight_ref, out_ref):
    aggregate = part_ref[...] + product(dense_ref, 2, beside_ref)
    aggregate = aggregate + product(dense_ref, 4, across_ref)
    support = (0.9 * aggregate + 0.1 * initial_ref[...].astype(jnp.float32)).astype(jnp.bfloat16)
    branch = jnp.dot(support, weight_ref[...], preferred_element_type=jnp.float32)
    combined = (1.0 - beta) * support.astype(jnp.float32) + beta * branch
    out_ref[...] = jnp.maximum(combined, 0.0).astype(jnp.bfloat16)


def layer(beta, dense, part, beside, across, initial, weight):
    return pl.pallas_call(
        lambda *refs: layer_kernel(beta, *refs),
        out_shape=jax.ShapeDtypeStruct(initial.shape, jnp.bfloat16),
        in_specs=[VMEM] * 6,
        out_specs=VMEM,
        cost_estimate=pl.CostEstimate(flops=2 * 512 * 1280 * 256, bytes_accessed=2 << 20, transcendentals=0),
    )(dense, part, beside, across, initial, weight)


def on_device(features, tiles, tile_cols, tile_count, weights):
    groups = lax.axis_size("node")
    layers = lax.axis_size("segment")
    seg = lax.axis_index("segment")
    node = lax.axis_index("node")
    per_group, slots = tile_cols.shape[1:]
    core = seg % 2
    both = ("segment", "node")
    turn = [(s * groups + n, n * groups + s) for s in range(layers) for n in range(groups)]
    pairs_beside = [(s, s ^ 1) for s in range(layers)]
    pairs_across = [(s, (s + 1) % layers if s % 2 else (s - 1) % layers) for s in range(layers)]

    all_weights = lax.all_gather(weights[0], "segment", axis=0, tiled=False)

    cols = lax.dynamic_index_in_dim(tile_cols, core, 0, keepdims=False)
    count = lax.dynamic_index_in_dim(tile_count, core, 0, keepdims=False)
    relative = (cols - (node - 1) * per_group) % (per_group * groups)
    side = relative // per_group
    odd = node % 2
    part_of = jnp.where(side == 1, 0, jnp.where((side == 2) == (odd == 0), 1, 2))
    places = part_of * per_group + relative % per_group
    places = jnp.where(jnp.arange(slots, dtype=jnp.int32)[None, :] < count[:, None], places, 12)
    note = jnp.zeros((16, BLOCK), jnp.bfloat16).at[0:per_group, 0:slots].set(places.astype(jnp.bfloat16))

    mine = lax.dynamic_index_in_dim(features, core, 0, keepdims=False)
    mine_tiles = lax.dynamic_index_in_dim(tiles, core, 0, keepdims=False).reshape(-1, BLOCK)
    bundle = jnp.concatenate([mine_tiles, mine[:, :BLOCK], mine[:, BLOCK:], note], axis=0)
    bundle = lax.ppermute(bundle, both, turn)

    tile_rows = mine_tiles.shape[0]
    rows = mine.shape[0]
    held_tiles = bundle[:tile_rows]
    initial = jnp.concatenate(
        [bundle[tile_rows : tile_rows + rows], bundle[tile_rows + rows : tile_rows + 2 * rows]], axis=1
    )
    held_places = bundle[tile_rows + 2 * rows :][0:per_group, 0:slots].astype(jnp.int32)
    dense = dense_adjacency(held_places, held_tiles)

    hidden = initial
    kept = [initial, initial]
    low = node - node % 2
    for step in range(layers):
        beta = math.log(0.5 / (step + 1) + 1.0)
        across = lax.ppermute(hidden, "segment", pairs_across)
        beside = lax.ppermute(hidden, "segment", pairs_beside)
        part = own_part(dense, hidden)
        hidden = layer(beta, dense, part, beside, across, initial, all_weights[step])
        kept[step % 2] = jnp.where(low == step - step % 2, hidden, kept[step % 2])

    arrived = lax.ppermute(jnp.stack(kept), both, turn)
    mine_out = lax.dynamic_index_in_dim(arrived, core, 0, keepdims=False)
    give = lax.dynamic_index_in_dim(arrived, 1 - core, 0, keepdims=False)
    other = lax.ppermute(give, "segment", pairs_beside)
    first = jnp.where(core == 0, mine_out, other)
    second = jnp.where(core == 0, other, mine_out)
    return jnp.stack([first, second])[None]


def solution(mesh):
    in_specs = (
        P(None, "node", None),
        P(None, "node", None, None, None),
        P(None, "node", None),
        P(None, "node"),
        P("segment", None, None),
    )
    out_specs = P("segment", None, "node", None)
    return jax.shard_map(
        on_device, mesh=mesh, in_specs=in_specs, out_specs=out_specs, check_vma=False
    )
```

time: 379 us -> 393 us (1.037); the launches traced: 378 us -> 387 us
  starting transfers between devices: 203 us -> 46.4 us
  waiting for transfers between devices: 117 us -> 214 us
  Pallas kernels: 0 us -> 91.5 us
  matrix products: 35.1 us -> 0 us
  between operations: 0.11 us -> 13.8 us
    ppermute x51 -> x35, starting transfers between devices: 203 us -> 46.4 us  [the longest x16 39.3 us: on_device(): beside = lax.ppermute(hidden, 'segment', pairs_beside)]
    pallas_call x0 -> x33, Pallas kernels: none -> 91.5 us  [the longest x16 49.7 us: layer(): pl.pallas_call(lambda *refs: layer_kernel(beta, *refs), out_shape=jax.Sha...]
    ppermute x51 -> x35, waiting for transfers between devices: 117 us -> 206 us  [the longest x1 103 us: on_device(): bundle = lax.ppermute(bundle, both, turn)]
    dot_general x34 -> x0, matrix products: 35.1 us -> none  [the longest x17 30.4 us: layer_rows(): jnp.einsum('bkij,bkjd->bid', masked, picked, preferred_element_type=jnp.f...]
    unnamed x4 -> x92, local copies, waits for them, and re-layouts: 0.01 us -> 11.9 us
    gather x17 -> x0, local copies, waits for them, and re-layouts: 11.6 us -> none  [layer_rows(): picked = grouped[columns]]
    all_gather x0 -> x1, waiting for transfers between devices: none -> 7.7 us  [on_device(): all_weights = lax.all_gather(weights[0], 'segment', axis=0, tiled=False)]
  transfers between devices with their start and end apart: 51 -> 36, of which waited for: 34 -> 19; matrix products, arithmetic and copies ran while one was open for 0% -> 2% of each run, Pallas kernels for 0% -> 10%
where the time goes in v1:
time: 393 us; the launch traced here: 387 us
  waiting for transfers between devices  214 us (54%)
  Pallas kernels  91.5 us (23%)
  starting transfers between devices  46.4 us (12%)
  local copies, waits for them, and re-layouts  16.7 us (4%)
  between operations  13.8 us (4%)
  other arithmetic  4.34 us (1%)
    ppermute x1, waiting for transfers between devices, on_device(): bundle = lax.ppermute(bundle, both, turn)  103 us
    ppermute x16, waiting for transfers between devices, on_device(): across = lax.ppermute(hidden, 'segment', pairs_across)  56.3 us
    pallas_call x16, Pallas kernels, layer(): pl.pallas_call(lambda *refs: layer_kernel(beta, *refs), out_shape=jax.Sha...  49.7 us
    ppermute x1, waiting for transfers between devices, on_device(): arrived = lax.ppermute(jnp.stack(kept), both, turn)  44.7 us
    pallas_call x16, Pallas kernels, own_part(): pl.pallas_call(own_kernel, out_shape=jax.ShapeDtypeStruct(own.shape, jnp....  40.2 us
    ppermute x16, starting transfers between devices, on_device(): beside = lax.ppermute(hidden, 'segment', pairs_beside)  39.3 us
    unnamed x92, local copies, waits for them, and re-layouts  11.9 us
  transfers between devices with their start and end apart: 36, of which 19 were waited for; matrix products, arithmetic and copies ran while one was open for 2% of the time, Pallas kernels for 10%

profile of v1, /device:TPU:1, one launch (start us, length us, event | category | flops | bytes accessed | tf_op | source)
XLA Modules:
  0.0 386.8 jit_solution(4818718298344719836)
XLA Ops:
  9.2 4.5 %collective-permute-start = (bf16[5136,128]{1,0:T(8,128)(2,1)S(1)}, bf16[5136,128]{1,0:T(8,128)(2,1)S(1)}, u32[]{:S(2)}, u32[]{:S(2)}) collective-permute-start(bf16[5136,128]{1,0:T(8,128)(2,1)S(1)} %fusion.1), channel_id=1, source_target_pairs={{0,0},{1,16},{2,32},{3,48},{4,64},{5,80},{6,96},{7,112},{8,128},{9... | collective-permute-start | bytes 3944456 | tf_op jit(solution)/shard_map/ppermute | solution.py:115
  13.8 103.0 %collective-permute-done = bf16[5136,128]{1,0:T(8,128)(2,1)S(1)} collective-permute-done((bf16[5136,128]{1,0:T(8,128)(2,1)S(1)}, bf16[5136,128]{1,0:T(8,128)(2,1)S(1)}, u32[]{:S(2)}, u32[]{:S(2)}) %collective-permute-start) | collective-permute-done | bytes 1314848 | tf_op jit(solution)/shard_map/ppermute | solution.py:115
  122.4 7.7 %all-gather.2.cloned.1.call-done = bf16[16,256,256]{2,1,0:T(8,128)(2,1)} async-done(((bf16[1,256,256]{2,1,0:T(8,128)(2,1)}), bf16[16,256,256]{2,1,0:T(8,128)(2,1)}) %all-gather.2.cloned.1.call-update) | async-done | bytes 2097168 | tf_op jit(solution)/shard_map/all_gather | solution.py:100
  137.0 25.3 %collective-permute-start.3 = (bf16[512,256]{1,0:T(8,128)(2,1)}, bf16[512,256]{1,0:T(8,128)(2,1)S(1)}, u32[]{:S(2)}, u32[]{:S(2)}) collective-permute-start(bf16[512,256]{1,0:T(8,128)(2,1)} %shard_map.57.own_ref), channel_id=1, source_target_pairs={{0,16},{16,0},{32,48},{48,32},{64,80},{80,64},{96,112},{112,96},{1... | collective-permute-start | bytes 786440 | tf_op jit(solution)/shard_map/ppermute | solution.py:132
  164.8 3.8 collective-permute-done.4.refs_3_
  169.3 3.1 shard_map.59.own_ref
  175.8 3.8 collective-permute-done.6.refs_3_
  180.3 3.1 shard_map.61.own_ref
  186.9 3.8 collective-permute-done.8.refs_3_
  191.4 3.1 shard_map.63.own_ref
  201.6 3.1 shard_map.65.own_ref
  209.0 3.8 collective-permute-done.12.refs_3_
  213.5 3.1 shard_map.67.own_ref
  220.1 3.8 collective-permute-done.14.refs_3_
  224.6 3.1 shard_map.69.own_ref
  231.1 3.8 collective-permute-done.16.refs_3_
  235.6 3.1 shard_map.71.own_ref
  242.2 3.8 collective-permute-done.18.refs_3_
  246.6 3.1 shard_map.73.own_ref
  253.2 3.8 collective-permute-done.20.refs_3_
  257.6 3.1 shard_map.75.own_ref
  264.2 3.8 collective-permute-done.22.refs_3_
  268.7 3.1 shard_map.77.own_ref
  275.2 3.8 collective-permute-done.24.refs_3_
  279.7 3.1 shard_map.79.own_ref
  286.2 3.8 collective-permute-done.26.refs_3_
  290.7 3.1 shard_map.81.own_ref
  297.3 3.8 collective-permute-done.28.refs_3_
  308.3 3.8 collective-permute-done.30.refs_3_
  312.8 3.2 shard_map.85.own_ref
  321.5 4.4 %collective-permute-done.32.refs_3_ = bf16[512,256]{1,0:T(8,128)(2,1)} collective-permute-done((bf16[512,256]{1,0:T(8,128)(2,1)}, bf16[512,256]{1,0:T(8,128)(2,1)}, u32[]{:S(2)}, u32[]{:S(2)}) %collective-permute-start.32) | collective-permute-done | bytes 262176 | tf_op jit(solution)/shard_map/ppermute | solution.py:131
  332.7 44.7 %collective-permute-done.33 = bf16[2,512,256]{2,1,0:T(8,128)(2,1)S(1)} collective-permute-done((bf16[2,512,256]{2,1,0:T(8,128)(2,1)S(1)}, bf16[2,512,256]{2,1,0:T(8,128)(2,1)S(1)}, u32[]{:S(2)}, u32[]{:S(2)}) %collective-permute-start.33) | collective-permute-done | bytes 524320 | tf_op jit(solution)/shard_map/ppermute | solution.py:137
  (183 shorter events, 93.7 us)
Async XLA Ops:
  6.5 123.6 %all-gather.2.cloned.1.call-start = ((), (), s32[]{:S(2)}) async-start(), calls=%async_computation | async-start | bytes 2228224 | tf_op jit(solution)/shard_map/all_gather | solution.py:100
  9.2 107.5 %collective-permute-start = (bf16[5136,128]{1,0:T(8,128)(2,1)S(1)}, bf16[5136,128]{1,0:T(8,128)(2,1)S(1)}, u32[]{:S(2)}, u32[]{:S(2)}) collective-permute-start(bf16[5136,128]{1,0:T(8,128)(2,1)S(1)} %fusion.1), channel_id=1, source_target_pairs={{0,0},{1,16},{2,32},{3,48},{4,64},{5,80},{6,96},{7,112},{8,128},{9... | collective-permute-start | bytes 3944456 | tf_op jit(solution)/shard_map/ppermute | solution.py:115
  116.8 16.2 %collective-permute-start.1 = (bf16[512,256]{1,0:T(8,128)(2,1)S(1)}, bf16[512,256]{1,0:T(8,128)(2,1)S(1)}, u32[]{:S(2)}, u32[]{:S(2)}) collective-permute-start(bf16[512,256]{1,0:T(8,128)(2,1)S(1)} %pad_maximum_fusion.1.own_ref.refs_4_), channel_id=1, source_target_pairs={{0,16},{16,0},{32,48},{48,32},{64,80},{80,64},{96,112},{112,96},{1... | collective-permute-start | bytes 786440 | tf_op jit(solution)/shard_map/ppermute | solution.py:132
  116.9 16.2 %collective-permute-start.2 = (bf16[512,256]{1,0:T(8,128)(2,1)S(1)}, bf16[512,256]{1,0:T(8,128)(2,1)S(1)}, u32[]{:S(2)}, u32[]{:S(2)}) collective-permute-start(bf16[512,256]{1,0:T(8,128)(2,1)S(1)} %pad_maximum_fusion.1.own_ref.refs_4_), channel_id=1, source_target_pairs={{0,240},{16,32},{32,16},{48,64},{64,48},{80,96},{96,80},{112,128},... | collective-permute-start | bytes 786440 | tf_op jit(solution)/shard_map/ppermute | solution.py:131
  137.0 27.9 %collective-permute-start.3 = (bf16[512,256]{1,0:T(8,128)(2,1)}, bf16[512,256]{1,0:T(8,128)(2,1)S(1)}, u32[]{:S(2)}, u32[]{:S(2)}) collective-permute-start(bf16[512,256]{1,0:T(8,128)(2,1)} %shard_map.57.own_ref), channel_id=1, source_target_pairs={{0,16},{16,0},{32,48},{48,32},{64,80},{80,64},{96,112},{112,96},{1... | collective-permute-start | bytes 786440 | tf_op jit(solution)/shard_map/ppermute | solution.py:132
  162.3 6.3 %collective-permute-start.4 = (bf16[512,256]{1,0:T(8,128)(2,1)}, bf16[512,256]{1,0:T(8,128)(2,1)S(1)}, u32[]{:S(2)}, u32[]{:S(2)}) collective-permute-start(bf16[512,256]{1,0:T(8,128)(2,1)} %shard_map.57.own_ref), channel_id=1, source_target_pairs={{0,240},{16,32},{32,16},{48,64},{64,48},{80,96},{96,80},{112,128},... | collective-permute-start | bytes 786440 | tf_op jit(solution)/shard_map/ppermute | solution.py:131
  172.4 3.4 collective-permute-start.5
  173.3 6.3 %collective-permute-start.6 = (bf16[512,256]{1,0:T(8,128)(2,1)}, bf16[512,256]{1,0:T(8,128)(2,1)S(1)}, u32[]{:S(2)}, u32[]{:S(2)}) collective-permute-start(bf16[512,256]{1,0:T(8,128)(2,1)} %shard_map.59.own_ref), channel_id=1, source_target_pairs={{0,240},{16,32},{32,16},{48,64},{64,48},{80,96},{96,80},{112,128},... | collective-permute-start | bytes 786440 | tf_op jit(solution)/shard_map/ppermute | solution.py:131
  184.4 6.3 %collective-permute-start.8 = (bf16[512,256]{1,0:T(8,128)(2,1)}, bf16[512,256]{1,0:T(8,128)(2,1)S(1)}, u32[]{:S(2)}, u32[]{:S(2)}) collective-permute-start(bf16[512,256]{1,0:T(8,128)(2,1)} %shard_map.61.own_ref), channel_id=1, source_target_pairs={{0,240},{16,32},{32,16},{48,64},{64,48},{80,96},{96,80},{112,128},... | collective-permute-start | bytes 786440 | tf_op jit(solution)/shard_map/ppermute | solution.py:131
  194.5 6.3 %collective-permute-start.10 = (bf16[512,256]{1,0:T(8,128)(2,1)}, bf16[512,256]{1,0:T(8,128)(2,1)S(1)}, u32[]{:S(2)}, u32[]{:S(2)}) collective-permute-start(bf16[512,256]{1,0:T(8,128)(2,1)} %shard_map.63.own_ref), channel_id=1, source_target_pairs={{0,240},{16,32},{32,16},{48,64},{64,48},{80,96},{96,80},{112,128},... | collective-permute-start | bytes 786440 | tf_op jit(solution)/shard_map/ppermute | solution.py:131
  194.5 6.3 %collective-permute-start.9 = (bf16[512,256]{1,0:T(8,128)(2,1)}, bf16[512,256]{1,0:T(8,128)(2,1)S(1)}, u32[]{:S(2)}, u32[]{:S(2)}) collective-permute-start(bf16[512,256]{1,0:T(8,128)(2,1)} %shard_map.63.own_ref), channel_id=1, source_target_pairs={{0,16},{16,0},{32,48},{48,32},{64,80},{80,64},{96,112},{112,96},{1... | collective-permute-start | bytes 786440 | tf_op jit(solution)/shard_map/ppermute | solution.py:132
  204.7 4.4 %collective-permute-start.11 = (bf16[512,256]{1,0:T(8,128)(2,1)}, bf16[512,256]{1,0:T(8,128)(2,1)S(1)}, u32[]{:S(2)}, u32[]{:S(2)}) collective-permute-start(bf16[512,256]{1,0:T(8,128)(2,1)} %shard_map.65.own_ref), channel_id=1, source_target_pairs={{0,16},{16,0},{32,48},{48,32},{64,80},{80,64},{96,112},{112,96},{1... | collective-permute-start | bytes 786440 | tf_op jit(solution)/shard_map/ppermute | solution.py:132
  206.5 6.3 %collective-permute-start.12 = (bf16[512,256]{1,0:T(8,128)(2,1)}, bf16[512,256]{1,0:T(8,128)(2,1)S(1)}, u32[]{:S(2)}, u32[]{:S(2)}) collective-permute-start(bf16[512,256]{1,0:T(8,128)(2,1)} %shard_map.65.own_ref), channel_id=1, source_target_pairs={{0,240},{16,32},{32,16},{48,64},{64,48},{80,96},{96,80},{112,128},... | collective-permute-start | bytes 786440 | tf_op jit(solution)/shard_map/ppermute | solution.py:131
  216.6 3.4 collective-permute-start.13
  217.6 6.3 %collective-permute-start.14 = (bf16[512,256]{1,0:T(8,128)(2,1)}, bf16[512,256]{1,0:T(8,128)(2,1)S(1)}, u32[]{:S(2)}, u32[]{:S(2)}) collective-permute-start(bf16[512,256]{1,0:T(8,128)(2,1)} %shard_map.67.own_ref), channel_id=1, source_target_pairs={{0,240},{16,32},{32,16},{48,64},{64,48},{80,96},{96,80},{112,128},... | collective-permute-start | bytes 786440 | tf_op jit(solution)/shard_map/ppermute | solution.py:131
  227.7 3.4 collective-permute-start.15
  228.6 6.3 %collective-permute-start.16 = (bf16[512,256]{1,0:T(8,128)(2,1)}, bf16[512,256]{1,0:T(8,128)(2,1)S(1)}, u32[]{:S(2)}, u32[]{:S(2)}) collective-permute-start(bf16[512,256]{1,0:T(8,128)(2,1)} %shard_map.69.own_ref), channel_id=1, source_target_pairs={{0,240},{16,32},{32,16},{48,64},{64,48},{80,96},{96,80},{112,128},... | collective-permute-start | bytes 786440 | tf_op jit(solution)/shard_map/ppermute | solution.py:131
  238.7 3.4 collective-permute-start.17
  239.6 6.3 %collective-permute-start.18 = (bf16[512,256]{1,0:T(8,128)(2,1)}, bf16[512,256]{1,0:T(8,128)(2,1)S(1)}, u32[]{:S(2)}, u32[]{:S(2)}) collective-permute-start(bf16[512,256]{1,0:T(8,128)(2,1)} %shard_map.71.own_ref), channel_id=1, source_target_pairs={{0,240},{16,32},{32,16},{48,64},{64,48},{80,96},{96,80},{112,128},... | collective-permute-start | bytes 786440 | tf_op jit(solution)/shard_map/ppermute | solution.py:131
  249.7 3.4 collective-permute-start.19
  250.7 6.3 %collective-permute-start.20 = (bf16[512,256]{1,0:T(8,128)(2,1)}, bf16[512,256]{1,0:T(8,128)(2,1)S(1)}, u32[]{:S(2)}, u32[]{:S(2)}) collective-permute-start(bf16[512,256]{1,0:T(8,128)(2,1)} %shard_map.73.own_ref), channel_id=1, source_target_pairs={{0,240},{16,32},{32,16},{48,64},{64,48},{80,96},{96,80},{112,128},... | collective-permute-start | bytes 786440 | tf_op jit(solution)/shard_map/ppermute | solution.py:131
  260.8 3.4 collective-permute-start.21
  261.7 6.3 %collective-permute-start.22 = (bf16[512,256]{1,0:T(8,128)(2,1)}, bf16[512,256]{1,0:T(8,128)(2,1)S(1)}, u32[]{:S(2)}, u32[]{:S(2)}) collective-permute-start(bf16[512,256]{1,0:T(8,128)(2,1)} %shard_map.75.own_ref), channel_id=1, source_target_pairs={{0,240},{16,32},{32,16},{48,64},{64,48},{80,96},{96,80},{112,128},... | collective-permute-start | bytes 786440 | tf_op jit(solution)/shard_map/ppermute | solution.py:131
  271.8 3.4 collective-permute-start.23
  272.7 6.3 %collective-permute-start.24 = (bf16[512,256]{1,0:T(8,128)(2,1)}, bf16[512,256]{1,0:T(8,128)(2,1)S(1)}, u32[]{:S(2)}, u32[]{:S(2)}) collective-permute-start(bf16[512,256]{1,0:T(8,128)(2,1)} %shard_map.77.own_ref), channel_id=1, source_target_pairs={{0,240},{16,32},{32,16},{48,64},{64,48},{80,96},{96,80},{112,128},... | collective-permute-start | bytes 786440 | tf_op jit(solution)/shard_map/ppermute | solution.py:131
  283.7 6.3 %collective-permute-start.26 = (bf16[512,256]{1,0:T(8,128)(2,1)}, bf16[512,256]{1,0:T(8,128)(2,1)S(1)}, u32[]{:S(2)}, u32[]{:S(2)}) collective-permute-start(bf16[512,256]{1,0:T(8,128)(2,1)} %shard_map.79.own_ref), channel_id=1, source_target_pairs={{0,240},{16,32},{32,16},{48,64},{64,48},{80,96},{96,80},{112,128},... | collective-permute-start | bytes 786440 | tf_op jit(solution)/shard_map/ppermute | solution.py:131
  293.8 3.4 collective-permute-start.27
  294.8 6.3 %collective-permute-start.28 = (bf16[512,256]{1,0:T(8,128)(2,1)}, bf16[512,256]{1,0:T(8,128)(2,1)S(1)}, u32[]{:S(2)}, u32[]{:S(2)}) collective-permute-start(bf16[512,256]{1,0:T(8,128)(2,1)} %shard_map.81.own_ref), channel_id=1, source_target_pairs={{0,240},{16,32},{32,16},{48,64},{64,48},{80,96},{96,80},{112,128},... | collective-permute-start | bytes 786440 | tf_op jit(solution)/shard_map/ppermute | solution.py:131
  304.9 3.4 collective-permute-start.29
  305.8 6.3 %collective-permute-start.30 = (bf16[512,256]{1,0:T(8,128)(2,1)}, bf16[512,256]{1,0:T(8,128)(2,1)S(1)}, u32[]{:S(2)}, u32[]{:S(2)}) collective-permute-start(bf16[512,256]{1,0:T(8,128)(2,1)} %shard_map.83.own_ref), channel_id=1, source_target_pairs={{0,240},{16,32},{32,16},{48,64},{64,48},{80,96},{96,80},{112,128},... | collective-permute-start | bytes 786440 | tf_op jit(solution)/shard_map/ppermute | solution.py:131
  319.5 6.4 %collective-permute-start.32 = (bf16[512,256]{1,0:T(8,128)(2,1)}, bf16[512,256]{1,0:T(8,128)(2,1)}, u32[]{:S(2)}, u32[]{:S(2)}) collective-permute-start(bf16[512,256]{1,0:T(8,128)(2,1)} %shard_map.85.own_ref), channel_id=1, source_target_pairs={{0,240},{16,32},{32,16},{48,64},{64,48},{80,96},{96,80},{112,128},... | collective-permute-start | bytes 786440 | tf_op jit(solution)/shard_map/ppermute | solution.py:131
  330.3 47.1 %collective-permute-start.33 = (bf16[2,512,256]{2,1,0:T(8,128)(2,1)S(1)}, bf16[2,512,256]{2,1,0:T(8,128)(2,1)S(1)}, u32[]{:S(2)}, u32[]{:S(2)}) collective-permute-start(bf16[2,512,256]{2,1,0:T(8,128)(2,1)S(1)} %pad_maximum_fusion), channel_id=1, source_target_pairs={{0,0},{1,16},{2,32},{3,48},{4,64},{5,80},{6,96},{7,112},{8,128},{9... | collective-permute-start | bytes 1572872 | tf_op jit(solution)/shard_map/ppermute | solution.py:137
  (50 other events, 155.0 us)
Sparse Core Ops, SparseCore 0:
  9.2 120.8 all-gather.1

commit v2 on v1

v2 whole, which is shorter than its diff:
```python
import math

import jax
import jax.numpy as jnp
from jax import lax
from jax.experimental import pallas as pl
from jax.experimental.pallas import tpu as pltpu
from jax.sharding import PartitionSpec as P

BLOCK = 128
HALF = 256
VMEM = pl.BlockSpec(memory_space=pltpu.VMEM)
SMEM = pl.BlockSpec(memory_space=pltpu.SMEM)


def dense_kernel(places_ref, tiles_ref, own_ref, before_ref, after_ref, total_ref):
    total_ref[...] = jnp.zeros_like(total_ref)
    blocks, slots = places_ref.shape
    for b in range(blocks):
        rows = pl.ds(b * BLOCK, BLOCK)

        @pl.loop(0, slots)
        def _(k):
            place = places_ref[b, k]
            chunk = place // 2
            tile = tiles_ref[b * slots + k].astype(jnp.float32)

            @pl.when((place < 12) & (place % 2 == 0))
            def _():
                total_ref[chunk, rows, 0:BLOCK] += tile

            @pl.when((place < 12) & (place % 2 == 1))
            def _():
                total_ref[chunk, rows, BLOCK:HALF] += tile

    own_ref[...] = total_ref[0:2].astype(jnp.bfloat16)
    before_ref[...] = total_ref[2:4].astype(jnp.bfloat16)
    after_ref[...] = total_ref[4:6].astype(jnp.bfloat16)


def dense_adjacency(places, tiles):
    rows = places.shape[0] * BLOCK
    part = jax.ShapeDtypeStruct((2, rows, HALF), jnp.bfloat16)
    return pl.pallas_call(
        dense_kernel,
        out_shape=(part, part, part),
        in_specs=[SMEM, VMEM],
        out_specs=(VMEM, VMEM, VMEM),
        scratch_shapes=[pltpu.VMEM((6, rows, HALF), jnp.float32)],
        compiler_params=pltpu.CompilerParams(vmem_limit_bytes=16 << 20),
    )(places, tiles)


def product(dense_ref, rows_ref, rows=slice(None)):
    first = jnp.dot(dense_ref[0, rows, :], rows_ref[0:HALF, :], preferred_element_type=jnp.float32)
    second = jnp.dot(dense_ref[1, rows, :], rows_ref[HALF:, :], preferred_element_type=jnp.float32)
    return first + second


def own_kernel(dense_ref, own_ref, part_ref):
    @pl.loop(0, 4)
    def _(r):
        rows = pl.ds(pl.multiple_of(r * BLOCK, BLOCK), BLOCK)
        part_ref[rows, :] = product(dense_ref, own_ref, rows)


def own_part(dense, own):
    return pl.pallas_call(
        own_kernel,
        out_shape=jax.ShapeDtypeStruct(own.shape, jnp.float32),
        in_specs=[VMEM, VMEM],
        out_specs=VMEM,
        compiler_params=pltpu.CompilerParams(vmem_limit_bytes=12 << 20),
        cost_estimate=pl.CostEstimate(flops=2 * 512 * 512 * 256, bytes_accessed=1 << 20, transcendentals=0),
    )(dense, own)


def layer_kernel(beta, to_before_ref, to_after_ref, part_ref, before_ref, after_ref, initial_ref, weight_ref, out_ref):
    aggregate = part_ref[...] + product(to_before_ref, before_ref)
    aggregate = aggregate + product(to_after_ref, after_ref)
    support = (0.9 * aggregate + 0.1 * initial_ref[...].astype(jnp.float32)).astype(jnp.bfloat16)
    branch = jnp.dot(support, weight_ref[...], preferred_element_type=jnp.float32)
    combined = (1.0 - beta) * support.astype(jnp.float32) + beta * branch
    out_ref[...] = jnp.maximum(combined, 0.0).astype(jnp.bfloat16)


def layer(beta, to_before, to_after, part, before, after, initial, weight):
    return pl.pallas_call(
        lambda *refs: layer_kernel(beta, *refs),
        out_shape=jax.ShapeDtypeStruct(initial.shape, jnp.bfloat16),
        in_specs=[VMEM] * 7,
        out_specs=VMEM,
        compiler_params=pltpu.CompilerParams(vmem_limit_bytes=12 << 20),
        cost_estimate=pl.CostEstimate(flops=2 * 512 * 1280 * 256, bytes_accessed=2 << 20, transcendentals=0),
    )(to_before, to_after, part, before, after, initial, weight)


def on_device(features, tiles, tile_cols, tile_count, weights):
    groups = lax.axis_size("node")
    layers = lax.axis_size("segment")
    seg = lax.axis_index("segment")
    node = lax.axis_index("node")
    per_group, slots = tile_cols.shape[1:]
    core = seg % 2
    up = [(n, (n + 1) % groups) for n in range(groups)]
    down = [(n, (n - 1) % groups) for n in range(groups)]
    swap = [(s, s ^ 1) for s in range(layers)]

    all_weights = lax.all_gather(weights[0], "segment", axis=0, tiled=False)

    cols = lax.dynamic_index_in_dim(tile_cols, core, 0, keepdims=False)
    count = lax.dynamic_index_in_dim(tile_count, core, 0, keepdims=False)
    relative = (cols - (node - 1) * per_group) % (per_group * groups)
    places = jnp.where(relative < per_group, relative + per_group, jnp.where(relative < 2 * per_group, relative - per_group, relative))
    places = jnp.where(jnp.arange(slots, dtype=jnp.int32)[None, :] < count[:, None], places, 12)

    initial = lax.dynamic_index_in_dim(features, core, 0, keepdims=False)
    held = lax.dynamic_index_in_dim(tiles, core, 0, keepdims=False).reshape(-1, BLOCK, BLOCK)
    to_own, to_before, to_after = dense_adjacency(places, held)

    hidden = initial
    kept = [initial, initial]
    low = seg - core
    for step in range(layers):
        beta = math.log(0.5 / (step + 1) + 1.0)
        before = lax.ppermute(hidden, "node", up)
        after = lax.ppermute(hidden, "node", down)
        part = own_part(to_own, hidden)
        hidden = layer(beta, to_before, to_after, part, before, after, initial, all_weights[step])
        kept[step % 2] = jnp.where(low == step - step % 2, hidden, kept[step % 2])

    mine = jnp.where(core == 0, kept[0], kept[1])
    give = jnp.where(core == 0, kept[1], kept[0])
    other = lax.ppermute(give, "segment", swap)
    first = jnp.where(core == 0, mine, other)
    second = jnp.where(core == 0, other, mine)
    return jnp.stack([first, second])[None]


def solution(mesh):
    in_specs = (
        P(None, "node", None),
        P(None, "node", None, None, None),
        P(None, "node", None),
        P(None, "node"),
        P("segment", None, None),
    )
    out_specs = P("segment", None, "node", None)
    return jax.shard_map(
        on_device, mesh=mesh, in_specs=in_specs, out_specs=out_specs, check_vma=False
    )
```

time: 393 us -> 241 us (0.61); the launches traced: 387 us -> 240 us
  waiting for transfers between devices: 214 us -> 92.6 us
  Pallas kernels: 91.5 us -> 28.1 us
  starting transfers between devices: 46.4 us -> 96.7 us
  local copies, waits for them, and re-layouts: 16.7 us -> 6.36 us
    ppermute x35 -> x33, waiting for transfers between devices: 206 us -> 58 us  [the longest x16 56.8 us: on_device(): before = lax.ppermute(hidden, 'node', up)]
    ppermute x35 -> x33, starting transfers between devices: 46.4 us -> 96.7 us  [the longest x16 76.4 us: on_device(): after = lax.ppermute(hidden, 'node', down)]
    pallas_call x16, Pallas kernels: 49.7 us -> 13.1 us  [layer(): pl.pallas_call(lambda *refs: layer_kernel(beta, *refs), out_shape=jax.Sha...]
    pallas_call x16, Pallas kernels: 40.2 us -> 13.2 us  [own_part(): pl.pallas_call(own_kernel, out_shape=jax.ShapeDtypeStruct(own.shape, jnp....]
    all_gather x1, waiting for transfers between devices: 7.7 us -> 33.9 us  [on_device(): all_weights = lax.all_gather(weights[0], 'segment', axis=0, tiled=False)]
    unnamed x92 -> x70, local copies, waits for them, and re-layouts: 11.9 us -> 2.81 us
  transfers between devices with their start and end apart: 36 -> 34, of which waited for: 19 -> 17; matrix products, arithmetic and copies ran while one was open for 2% -> 2% of each run, Pallas kernels for 10% -> 6%
where the time goes in v2:
time: 241 us; the launch traced here: 240 us
  starting transfers between devices  96.7 us (40%)
  waiting for transfers between devices  92.6 us (38%)
  Pallas kernels  28.1 us (12%)
  between operations  14.2 us (6%)
  local copies, waits for them, and re-layouts  6.36 us (3%)
    ppermute x16, starting transfers between devices, on_device(): after = lax.ppermute(hidden, 'node', down)  76.4 us
    ppermute x16, waiting for transfers between devices, on_device(): before = lax.ppermute(hidden, 'node', up)  56.8 us
    all_gather x1, waiting for transfers between devices, on_device(): all_weights = lax.all_gather(weights[0], 'segment', axis=0, tiled=False)  33.9 us
    ppermute x1, starting transfers between devices, on_device(): other = lax.ppermute(give, 'segment', swap)  15.6 us
    pallas_call x16, Pallas kernels, own_part(): pl.pallas_call(own_kernel, out_shape=jax.ShapeDtypeStruct(own.shape, jnp....  13.2 us
    pallas_call x16, Pallas kernels, layer(): pl.pallas_call(lambda *refs: layer_kernel(beta, *refs), out_shape=jax.Sha...  13.1 us
  transfers between devices with their start and end apart: 34, of which 17 were waited for; matrix products, arithmetic and copies ran while one was open for 2% of the time, Pallas kernels for 6%

profile of v2, /device:TPU:1, one launch (start us, length us, event | category | flops | bytes accessed | tf_op | source)
XLA Modules:
  0.0 240.3 jit_solution(10361173552129662441)
XLA Ops:
  10.4 3.8 %collective-permute-start.1 = (bf16[512,256]{1,0:T(8,128)(2,1)S(1)}, bf16[512,256]{1,0:T(8,128)(2,1)}, u32[]{:S(2)}, u32[]{:S(2)}) collective-permute-start(bf16[512,256]{1,0:T(8,128)(2,1)S(1)} %dynamic-slice_bitcast_fusion.own_ref.refs_5_), channel_id=1, source_target_pairs={{0,15},{1,0},{2,1},{3,2},{4,3},{5,4},{6,5},{7,6},{8,7},{9,8},{10,9... | collective-permute-start | bytes 786440 | tf_op jit(solution)/shard_map/ppermute | solution.py:127
  19.2 33.9 %all-gather.2.cloned.1.call-done = bf16[16,256,256]{2,1,0:T(8,128)(2,1)} async-done(((bf16[1,256,256]{2,1,0:T(8,128)(2,1)}), bf16[16,256,256]{2,1,0:T(8,128)(2,1)}) %all-gather.2.cloned.1.call-update) | async-done | bytes 2097168 | tf_op jit(solution)/shard_map/all_gather | solution.py:109
  58.0 3.6 %collective-permute-start.3 = (bf16[512,256]{1,0:T(8,128)(2,1)S(1)}, bf16[512,256]{1,0:T(8,128)(2,1)S(1)}, u32[]{:S(2)}, u32[]{:S(2)}) collective-permute-start(bf16[512,256]{1,0:T(8,128)(2,1)S(1)} %shard_map.57.own_ref), channel_id=1, source_target_pairs={{0,15},{1,0},{2,1},{3,2},{4,3},{5,4},{6,5},{7,6},{8,7},{9,8},{10,9... | collective-permute-start | bytes 786440 | tf_op jit(solution)/shard_map/ppermute | solution.py:127
  62.4 5.4 %collective-permute-done.2.refs_3_ = bf16[512,256]{1,0:T(8,128)(2,1)S(1)} collective-permute-done((bf16[512,256]{1,0:T(8,128)(2,1)S(1)}, bf16[512,256]{1,0:T(8,128)(2,1)S(1)}, u32[]{:S(2)}, u32[]{:S(2)}) %collective-permute-start.2) | collective-permute-done | bytes 262176 | tf_op jit(solution)/shard_map/ppermute | solution.py:126
  68.6 4.8 %collective-permute-start.5 = (bf16[512,256]{1,0:T(8,128)(2,1)S(1)}, bf16[512,256]{1,0:T(8,128)(2,1)S(1)}, u32[]{:S(2)}, u32[]{:S(2)}) collective-permute-start(bf16[512,256]{1,0:T(8,128)(2,1)S(1)} %shard_map.59.own_ref), channel_id=1, source_target_pairs={{0,15},{1,0},{2,1},{3,2},{4,3},{5,4},{6,5},{7,6},{8,7},{9,8},{10,9... | collective-permute-start | bytes 786440 | tf_op jit(solution)/shard_map/ppermute | solution.py:127
  74.1 4.5 %collective-permute-done.4.refs_3_ = bf16[512,256]{1,0:T(8,128)(2,1)S(1)} collective-permute-done((bf16[512,256]{1,0:T(8,128)(2,1)S(1)}, bf16[512,256]{1,0:T(8,128)(2,1)S(1)}, u32[]{:S(2)}, u32[]{:S(2)}) %collective-permute-start.4) | collective-permute-done | bytes 262176 | tf_op jit(solution)/shard_map/ppermute | solution.py:126
  79.4 4.8 %collective-permute-start.7 = (bf16[512,256]{1,0:T(8,128)(2,1)S(1)}, bf16[512,256]{1,0:T(8,128)(2,1)S(1)}, u32[]{:S(2)}, u32[]{:S(2)}) collective-permute-start(bf16[512,256]{1,0:T(8,128)(2,1)S(1)} %shard_map.61.own_ref), channel_id=1, source_target_pairs={{0,15},{1,0},{2,1},{3,2},{4,3},{5,4},{6,5},{7,6},{8,7},{9,8},{10,9... | collective-permute-start | bytes 786440 | tf_op jit(solution)/shard_map/ppermute | solution.py:127
  84.9 3.6 %collective-permute-done.6.refs_3_ = bf16[512,256]{1,0:T(8,128)(2,1)S(1)} collective-permute-done((bf16[512,256]{1,0:T(8,128)(2,1)S(1)}, bf16[512,256]{1,0:T(8,128)(2,1)S(1)}, u32[]{:S(2)}, u32[]{:S(2)}) %collective-permute-start.6) | collective-permute-done | bytes 262176 | tf_op jit(solution)/shard_map/ppermute | solution.py:126
  89.2 4.8 %collective-permute-start.9 = (bf16[512,256]{1,0:T(8,128)(2,1)S(1)}, bf16[512,256]{1,0:T(8,128)(2,1)S(1)}, u32[]{:S(2)}, u32[]{:S(2)}) collective-permute-start(bf16[512,256]{1,0:T(8,128)(2,1)S(1)} %shard_map.63.own_ref), channel_id=1, source_target_pairs={{0,15},{1,0},{2,1},{3,2},{4,3},{5,4},{6,5},{7,6},{8,7},{9,8},{10,9... | collective-permute-start | bytes 786440 | tf_op jit(solution)/shard_map/ppermute | solution.py:127
  94.8 3.0 %collective-permute-done.8.refs_3_ = bf16[512,256]{1,0:T(8,128)(2,1)S(1)} collective-permute-done((bf16[512,256]{1,0:T(8,128)(2,1)S(1)}, bf16[512,256]{1,0:T(8,128)(2,1)S(1)}, u32[]{:S(2)}, u32[]{:S(2)}) %collective-permute-start.8) | collective-permute-done | bytes 262176 | tf_op jit(solution)/shard_map/ppermute | solution.py:126
  98.7 4.9 %collective-permute-start.11 = (bf16[512,256]{1,0:T(8,128)(2,1)S(1)}, bf16[512,256]{1,0:T(8,128)(2,1)S(1)}, u32[]{:S(2)}, u32[]{:S(2)}) collective-permute-start(bf16[512,256]{1,0:T(8,128)(2,1)S(1)} %shard_map.65.own_ref), channel_id=1, source_target_pairs={{0,15},{1,0},{2,1},{3,2},{4,3},{5,4},{6,5},{7,6},{8,7},{9,8},{10,9... | collective-permute-start | bytes 786440 | tf_op jit(solution)/shard_map/ppermute | solution.py:127
  104.3 2.9 %collective-permute-done.10.refs_3_ = bf16[512,256]{1,0:T(8,128)(2,1)S(1)} collective-permute-done((bf16[512,256]{1,0:T(8,128)(2,1)S(1)}, bf16[512,256]{1,0:T(8,128)(2,1)S(1)}, u32[]{:S(2)}, u32[]{:S(2)}) %collective-permute-start.10) | collective-permute-done | bytes 262176 | tf_op jit(solution)/shard_map/ppermute | solution.py:126
  107.9 4.9 %collective-permute-start.13 = (bf16[512,256]{1,0:T(8,128)(2,1)S(1)}, bf16[512,256]{1,0:T(8,128)(2,1)S(1)}, u32[]{:S(2)}, u32[]{:S(2)}) collective-permute-start(bf16[512,256]{1,0:T(8,128)(2,1)S(1)} %shard_map.67.own_ref), channel_id=1, source_target_pairs={{0,15},{1,0},{2,1},{3,2},{4,3},{5,4},{6,5},{7,6},{8,7},{9,8},{10,9... | collective-permute-start | bytes 786440 | tf_op jit(solution)/shard_map/ppermute | solution.py:127
  113.7 2.9 %collective-permute-done.12.refs_3_ = bf16[512,256]{1,0:T(8,128)(2,1)S(1)} collective-permute-done((bf16[512,256]{1,0:T(8,128)(2,1)S(1)}, bf16[512,256]{1,0:T(8,128)(2,1)S(1)}, u32[]{:S(2)}, u32[]{:S(2)}) %collective-permute-start.12) | collective-permute-done | bytes 262176 | tf_op jit(solution)/shard_map/ppermute | solution.py:126
  117.3 4.9 %collective-permute-start.15 = (bf16[512,256]{1,0:T(8,128)(2,1)S(1)}, bf16[512,256]{1,0:T(8,128)(2,1)S(1)}, u32[]{:S(2)}, u32[]{:S(2)}) collective-permute-start(bf16[512,256]{1,0:T(8,128)(2,1)S(1)} %shard_map.69.own_ref), channel_id=1, source_target_pairs={{0,15},{1,0},{2,1},{3,2},{4,3},{5,4},{6,5},{7,6},{8,7},{9,8},{10,9... | collective-permute-start | bytes 786440 | tf_op jit(solution)/shard_map/ppermute | solution.py:127
  123.0 2.9 %collective-permute-done.14.refs_3_ = bf16[512,256]{1,0:T(8,128)(2,1)S(1)} collective-permute-done((bf16[512,256]{1,0:T(8,128)(2,1)S(1)}, bf16[512,256]{1,0:T(8,128)(2,1)S(1)}, u32[]{:S(2)}, u32[]{:S(2)}) %collective-permute-start.14) | collective-permute-done | bytes 262176 | tf_op jit(solution)/shard_map/ppermute | solution.py:126
  126.7 4.9 %collective-permute-start.17 = (bf16[512,256]{1,0:T(8,128)(2,1)S(1)}, bf16[512,256]{1,0:T(8,128)(2,1)S(1)}, u32[]{:S(2)}, u32[]{:S(2)}) collective-permute-start(bf16[512,256]{1,0:T(8,128)(2,1)S(1)} %shard_map.71.own_ref), channel_id=1, source_target_pairs={{0,15},{1,0},{2,1},{3,2},{4,3},{5,4},{6,5},{7,6},{8,7},{9,8},{10,9... | collective-permute-start | bytes 786440 | tf_op jit(solution)/shard_map/ppermute | solution.py:127
  132.4 3.2 %collective-permute-done.16.refs_3_ = bf16[512,256]{1,0:T(8,128)(2,1)S(1)} collective-permute-done((bf16[512,256]{1,0:T(8,128)(2,1)S(1)}, bf16[512,256]{1,0:T(8,128)(2,1)S(1)}, u32[]{:S(2)}, u32[]{:S(2)}) %collective-permute-start.16) | collective-permute-done | bytes 262176 | tf_op jit(solution)/shard_map/ppermute | solution.py:126
  136.3 5.2 %collective-permute-start.19 = (bf16[512,256]{1,0:T(8,128)(2,1)S(1)}, bf16[512,256]{1,0:T(8,128)(2,1)S(1)}, u32[]{:S(2)}, u32[]{:S(2)}) collective-permute-start(bf16[512,256]{1,0:T(8,128)(2,1)S(1)} %shard_map.73.own_ref), channel_id=1, source_target_pairs={{0,15},{1,0},{2,1},{3,2},{4,3},{5,4},{6,5},{7,6},{8,7},{9,8},{10,9... | collective-permute-start | bytes 786440 | tf_op jit(solution)/shard_map/ppermute | solution.py:127
  142.3 4.2 %collective-permute-done.18.refs_3_ = bf16[512,256]{1,0:T(8,128)(2,1)S(1)} collective-permute-done((bf16[512,256]{1,0:T(8,128)(2,1)S(1)}, bf16[512,256]{1,0:T(8,128)(2,1)S(1)}, u32[]{:S(2)}, u32[]{:S(2)}) %collective-permute-start.18) | collective-permute-done | bytes 262176 | tf_op jit(solution)/shard_map/ppermute | solution.py:126
  147.3 5.4 %collective-permute-start.21 = (bf16[512,256]{1,0:T(8,128)(2,1)S(1)}, bf16[512,256]{1,0:T(8,128)(2,1)S(1)}, u32[]{:S(2)}, u32[]{:S(2)}) collective-permute-start(bf16[512,256]{1,0:T(8,128)(2,1)S(1)} %shard_map.75.own_ref), channel_id=1, source_target_pairs={{0,15},{1,0},{2,1},{3,2},{4,3},{5,4},{6,5},{7,6},{8,7},{9,8},{10,9... | collective-permute-start | bytes 786440 | tf_op jit(solution)/shard_map/ppermute | solution.py:127
  153.5 5.2 %collective-permute-done.20.refs_3_ = bf16[512,256]{1,0:T(8,128)(2,1)S(1)} collective-permute-done((bf16[512,256]{1,0:T(8,128)(2,1)S(1)}, bf16[512,256]{1,0:T(8,128)(2,1)S(1)}, u32[]{:S(2)}, u32[]{:S(2)}) %collective-permute-start.20) | collective-permute-done | bytes 262176 | tf_op jit(solution)/shard_map/ppermute | solution.py:126
  159.4 5.3 %collective-permute-start.23 = (bf16[512,256]{1,0:T(8,128)(2,1)S(1)}, bf16[512,256]{1,0:T(8,128)(2,1)S(1)}, u32[]{:S(2)}, u32[]{:S(2)}) collective-permute-start(bf16[512,256]{1,0:T(8,128)(2,1)S(1)} %shard_map.77.own_ref), channel_id=1, source_target_pairs={{0,15},{1,0},{2,1},{3,2},{4,3},{5,4},{6,5},{7,6},{8,7},{9,8},{10,9... | collective-permute-start | bytes 786440 | tf_op jit(solution)/shard_map/ppermute | solution.py:127
  165.5 5.5 %collective-permute-done.22.refs_3_ = bf16[512,256]{1,0:T(8,128)(2,1)S(1)} collective-permute-done((bf16[512,256]{1,0:T(8,128)(2,1)S(1)}, bf16[512,256]{1,0:T(8,128)(2,1)S(1)}, u32[]{:S(2)}, u32[]{:S(2)}) %collective-permute-start.22) | collective-permute-done | bytes 262176 | tf_op jit(solution)/shard_map/ppermute | solution.py:126
  171.7 4.8 %collective-permute-start.25 = (bf16[512,256]{1,0:T(8,128)(2,1)S(1)}, bf16[512,256]{1,0:T(8,128)(2,1)S(1)}, u32[]{:S(2)}, u32[]{:S(2)}) collective-permute-start(bf16[512,256]{1,0:T(8,128)(2,1)S(1)} %shard_map.79.own_ref), channel_id=1, source_target_pairs={{0,15},{1,0},{2,1},{3,2},{4,3},{5,4},{6,5},{7,6},{8,7},{9,8},{10,9... | collective-permute-start | bytes 786440 | tf_op jit(solution)/shard_map/ppermute | solution.py:127
  177.2 4.7 %collective-permute-done.24.refs_3_ = bf16[512,256]{1,0:T(8,128)(2,1)S(1)} collective-permute-done((bf16[512,256]{1,0:T(8,128)(2,1)S(1)}, bf16[512,256]{1,0:T(8,128)(2,1)S(1)}, u32[]{:S(2)}, u32[]{:S(2)}) %collective-permute-start.24) | collective-permute-done | bytes 262176 | tf_op jit(solution)/shard_map/ppermute | solution.py:126
  182.6 4.8 %collective-permute-start.27 = (bf16[512,256]{1,0:T(8,128)(2,1)S(1)}, bf16[512,256]{1,0:T(8,128)(2,1)S(1)}, u32[]{:S(2)}, u32[]{:S(2)}) collective-permute-start(bf16[512,256]{1,0:T(8,128)(2,1)S(1)} %shard_map.81.own_ref), channel_id=1, source_target_pairs={{0,15},{1,0},{2,1},{3,2},{4,3},{5,4},{6,5},{7,6},{8,7},{9,8},{10,9... | collective-permute-start | bytes 786440 | tf_op jit(solution)/shard_map/ppermute | solution.py:127
  188.2 3.7 %collective-permute-done.26.refs_3_ = bf16[512,256]{1,0:T(8,128)(2,1)S(1)} collective-permute-done((bf16[512,256]{1,0:T(8,128)(2,1)S(1)}, bf16[512,256]{1,0:T(8,128)(2,1)S(1)}, u32[]{:S(2)}, u32[]{:S(2)}) %collective-permute-start.26) | collective-permute-done | bytes 262176 | tf_op jit(solution)/shard_map/ppermute | solution.py:126
  192.7 4.8 %collective-permute-start.29 = (bf16[512,256]{1,0:T(8,128)(2,1)S(1)}, bf16[512,256]{1,0:T(8,128)(2,1)S(1)}, u32[]{:S(2)}, u32[]{:S(2)}) collective-permute-start(bf16[512,256]{1,0:T(8,128)(2,1)S(1)} %shard_map.83.own_ref), channel_id=1, source_target_pairs={{0,15},{1,0},{2,1},{3,2},{4,3},{5,4},{6,5},{7,6},{8,7},{9,8},{10,9... | collective-permute-start | bytes 786440 | tf_op jit(solution)/shard_map/ppermute | solution.py:127
  198.2 3.0 %collective-permute-done.28.refs_3_ = bf16[512,256]{1,0:T(8,128)(2,1)S(1)} collective-permute-done((bf16[512,256]{1,0:T(8,128)(2,1)S(1)}, bf16[512,256]{1,0:T(8,128)(2,1)S(1)}, u32[]{:S(2)}, u32[]{:S(2)}) %collective-permute-start.28) | collective-permute-done | bytes 262176 | tf_op jit(solution)/shard_map/ppermute | solution.py:126
  202.6 4.8 %collective-permute-start.31 = (bf16[512,256]{1,0:T(8,128)(2,1)}, bf16[512,256]{1,0:T(8,128)(2,1)}, u32[]{:S(2)}, u32[]{:S(2)}) collective-permute-start(bf16[512,256]{1,0:T(8,128)(2,1)} %shard_map.85.own_ref), channel_id=1, source_target_pairs={{0,15},{1,0},{2,1},{3,2},{4,3},{5,4},{6,5},{7,6},{8,7},{9,8},{10,9... | collective-permute-start | bytes 786440 | tf_op jit(solution)/shard_map/ppermute | solution.py:127
  215.8 15.6 %collective-permute-start.32 = (bf16[512,256]{1,0:T(8,128)(2,1)S(1)}, bf16[512,256]{1,0:T(8,128)(2,1)S(1)}, u32[]{:S(2)}, u32[]{:S(2)}) collective-permute-start(bf16[512,256]{1,0:T(8,128)(2,1)S(1)} %get-tuple-element.11), channel_id=1, source_target_pairs={{0,16},{16,0},{32,48},{48,32},{64,80},{80,64},{96,112},{112,96},{1... | collective-permute-start | bytes 786440 | tf_op jit(solution)/shard_map/ppermute | solution.py:134
  (148 shorter events, 45.5 us)
Async XLA Ops:
  6.5 46.6 %all-gather.2.cloned.1.call-start = ((), (), s32[]{:S(2)}) async-start(), calls=%async_computation | async-start | bytes 2228224 | tf_op jit(solution)/shard_map/all_gather | solution.py:109
  8.3 46.8 %collective-permute-start = (bf16[512,256]{1,0:T(8,128)(2,1)S(1)}, bf16[512,256]{1,0:T(8,128)(2,1)}, u32[]{:S(2)}, u32[]{:S(2)}) collective-permute-start(bf16[512,256]{1,0:T(8,128)(2,1)S(1)} %dynamic-slice_bitcast_fusion.own_ref.refs_5_), channel_id=1, source_target_pairs={{0,1},{1,2},{2,3},{3,4},{4,5},{5,6},{6,7},{7,8},{8,9},{9,10},{10,1... | collective-permute-start | bytes 786440 | tf_op jit(solution)/shard_map/ppermute | solution.py:126
  10.4 44.7 %collective-permute-start.1 = (bf16[512,256]{1,0:T(8,128)(2,1)S(1)}, bf16[512,256]{1,0:T(8,128)(2,1)}, u32[]{:S(2)}, u32[]{:S(2)}) collective-permute-start(bf16[512,256]{1,0:T(8,128)(2,1)S(1)} %dynamic-slice_bitcast_fusion.own_ref.refs_5_), channel_id=1, source_target_pairs={{0,15},{1,0},{2,1},{3,2},{4,3},{5,4},{6,5},{7,6},{8,7},{9,8},{10,9... | collective-permute-start | bytes 786440 | tf_op jit(solution)/shard_map/ppermute | solution.py:127
  56.8 11.0 %collective-permute-start.2 = (bf16[512,256]{1,0:T(8,128)(2,1)S(1)}, bf16[512,256]{1,0:T(8,128)(2,1)S(1)}, u32[]{:S(2)}, u32[]{:S(2)}) collective-permute-start(bf16[512,256]{1,0:T(8,128)(2,1)S(1)} %shard_map.57.own_ref), channel_id=1, source_target_pairs={{0,1},{1,2},{2,3},{3,4},{4,5},{5,6},{6,7},{7,8},{8,9},{9,10},{10,1... | collective-permute-start | bytes 786440 | tf_op jit(solution)/shard_map/ppermute | solution.py:126
  58.0 9.8 %collective-permute-start.3 = (bf16[512,256]{1,0:T(8,128)(2,1)S(1)}, bf16[512,256]{1,0:T(8,128)(2,1)S(1)}, u32[]{:S(2)}, u32[]{:S(2)}) collective-permute-start(bf16[512,256]{1,0:T(8,128)(2,1)S(1)} %shard_map.57.own_ref), channel_id=1, source_target_pairs={{0,15},{1,0},{2,1},{3,2},{4,3},{5,4},{6,5},{7,6},{8,7},{9,8},{10,9... | collective-permute-start | bytes 786440 | tf_op jit(solution)/shard_map/ppermute | solution.py:127
  68.5 10.1 %collective-permute-start.4 = (bf16[512,256]{1,0:T(8,128)(2,1)S(1)}, bf16[512,256]{1,0:T(8,128)(2,1)S(1)}, u32[]{:S(2)}, u32[]{:S(2)}) collective-permute-start(bf16[512,256]{1,0:T(8,128)(2,1)S(1)} %shard_map.59.own_ref), channel_id=1, source_target_pairs={{0,1},{1,2},{2,3},{3,4},{4,5},{5,6},{6,7},{7,8},{8,9},{9,10},{10,1... | collective-permute-start | bytes 786440 | tf_op jit(solution)/shard_map/ppermute | solution.py:126
  68.6 10.0 %collective-permute-start.5 = (bf16[512,256]{1,0:T(8,128)(2,1)S(1)}, bf16[512,256]{1,0:T(8,128)(2,1)S(1)}, u32[]{:S(2)}, u32[]{:S(2)}) collective-permute-start(bf16[512,256]{1,0:T(8,128)(2,1)S(1)} %shard_map.59.own_ref), channel_id=1, source_target_pairs={{0,15},{1,0},{2,1},{3,2},{4,3},{5,4},{6,5},{7,6},{8,7},{9,8},{10,9... | collective-permute-start | bytes 786440 | tf_op jit(solution)/shard_map/ppermute | solution.py:127
  79.3 9.2 %collective-permute-start.6 = (bf16[512,256]{1,0:T(8,128)(2,1)S(1)}, bf16[512,256]{1,0:T(8,128)(2,1)S(1)}, u32[]{:S(2)}, u32[]{:S(2)}) collective-permute-start(bf16[512,256]{1,0:T(8,128)(2,1)S(1)} %shard_map.61.own_ref), channel_id=1, source_target_pairs={{0,1},{1,2},{2,3},{3,4},{4,5},{5,6},{6,7},{7,8},{8,9},{9,10},{10,1... | collective-permute-start | bytes 786440 | tf_op jit(solution)/shard_map/ppermute | solution.py:126
  79.4 9.1 %collective-permute-start.7 = (bf16[512,256]{1,0:T(8,128)(2,1)S(1)}, bf16[512,256]{1,0:T(8,128)(2,1)S(1)}, u32[]{:S(2)}, u32[]{:S(2)}) collective-permute-start(bf16[512,256]{1,0:T(8,128)(2,1)S(1)} %shard_map.61.own_ref), channel_id=1, source_target_pairs={{0,15},{1,0},{2,1},{3,2},{4,3},{5,4},{6,5},{7,6},{8,7},{9,8},{10,9... | collective-permute-start | bytes 786440 | tf_op jit(solution)/shard_map/ppermute | solution.py:127
  89.1 8.6 %collective-permute-start.8 = (bf16[512,256]{1,0:T(8,128)(2,1)S(1)}, bf16[512,256]{1,0:T(8,128)(2,1)S(1)}, u32[]{:S(2)}, u32[]{:S(2)}) collective-permute-start(bf16[512,256]{1,0:T(8,128)(2,1)S(1)} %shard_map.63.own_ref), channel_id=1, source_target_pairs={{0,1},{1,2},{2,3},{3,4},{4,5},{5,6},{6,7},{7,8},{8,9},{9,10},{10,1... | collective-permute-start | bytes 786440 | tf_op jit(solution)/shard_map/ppermute | solution.py:126
  98.4 8.8 %collective-permute-start.10 = (bf16[512,256]{1,0:T(8,128)(2,1)S(1)}, bf16[512,256]{1,0:T(8,128)(2,1)S(1)}, u32[]{:S(2)}, u32[]{:S(2)}) collective-permute-start(bf16[512,256]{1,0:T(8,128)(2,1)S(1)} %shard_map.65.own_ref), channel_id=1, source_target_pairs={{0,1},{1,2},{2,3},{3,4},{4,5},{5,6},{6,7},{7,8},{8,9},{9,10},{10,1... | collective-permute-start | bytes 786440 | tf_op jit(solution)/shard_map/ppermute | solution.py:126
  98.7 8.5 %collective-permute-start.11 = (bf16[512,256]{1,0:T(8,128)(2,1)S(1)}, bf16[512,256]{1,0:T(8,128)(2,1)S(1)}, u32[]{:S(2)}, u32[]{:S(2)}) collective-permute-start(bf16[512,256]{1,0:T(8,128)(2,1)S(1)} %shard_map.65.own_ref), channel_id=1, source_target_pairs={{0,15},{1,0},{2,1},{3,2},{4,3},{5,4},{6,5},{7,6},{8,7},{9,8},{10,9... | collective-permute-start | bytes 786440 | tf_op jit(solution)/shard_map/ppermute | solution.py:127
  107.9 8.7 %collective-permute-start.12 = (bf16[512,256]{1,0:T(8,128)(2,1)S(1)}, bf16[512,256]{1,0:T(8,128)(2,1)S(1)}, u32[]{:S(2)}, u32[]{:S(2)}) collective-permute-start(bf16[512,256]{1,0:T(8,128)(2,1)S(1)} %shard_map.67.own_ref), channel_id=1, source_target_pairs={{0,1},{1,2},{2,3},{3,4},{4,5},{5,6},{6,7},{7,8},{8,9},{9,10},{10,1... | collective-permute-start | bytes 786440 | tf_op jit(solution)/shard_map/ppermute | solution.py:126
  107.9 8.6 %collective-permute-start.13 = (bf16[512,256]{1,0:T(8,128)(2,1)S(1)}, bf16[512,256]{1,0:T(8,128)(2,1)S(1)}, u32[]{:S(2)}, u32[]{:S(2)}) collective-permute-start(bf16[512,256]{1,0:T(8,128)(2,1)S(1)} %shard_map.67.own_ref), channel_id=1, source_target_pairs={{0,15},{1,0},{2,1},{3,2},{4,3},{5,4},{6,5},{7,6},{8,7},{9,8},{10,9... | collective-permute-start | bytes 786440 | tf_op jit(solution)/shard_map/ppermute | solution.py:127
  117.2 8.7 %collective-permute-start.14 = (bf16[512,256]{1,0:T(8,128)(2,1)S(1)}, bf16[512,256]{1,0:T(8,128)(2,1)S(1)}, u32[]{:S(2)}, u32[]{:S(2)}) collective-permute-start(bf16[512,256]{1,0:T(8,128)(2,1)S(1)} %shard_map.69.own_ref), channel_id=1, source_target_pairs={{0,1},{1,2},{2,3},{3,4},{4,5},{5,6},{6,7},{7,8},{8,9},{9,10},{10,1... | collective-permute-start | bytes 786440 | tf_op jit(solution)/shard_map/ppermute | solution.py:126
  117.3 8.6 %collective-permute-start.15 = (bf16[512,256]{1,0:T(8,128)(2,1)S(1)}, bf16[512,256]{1,0:T(8,128)(2,1)S(1)}, u32[]{:S(2)}, u32[]{:S(2)}) collective-permute-start(bf16[512,256]{1,0:T(8,128)(2,1)S(1)} %shard_map.69.own_ref), channel_id=1, source_target_pairs={{0,15},{1,0},{2,1},{3,2},{4,3},{5,4},{6,5},{7,6},{8,7},{9,8},{10,9... | collective-permute-start | bytes 786440 | tf_op jit(solution)/shard_map/ppermute | solution.py:127
  126.6 9.0 %collective-permute-start.16 = (bf16[512,256]{1,0:T(8,128)(2,1)S(1)}, bf16[512,256]{1,0:T(8,128)(2,1)S(1)}, u32[]{:S(2)}, u32[]{:S(2)}) collective-permute-start(bf16[512,256]{1,0:T(8,128)(2,1)S(1)} %shard_map.71.own_ref), channel_id=1, source_target_pairs={{0,1},{1,2},{2,3},{3,4},{4,5},{5,6},{6,7},{7,8},{8,9},{9,10},{10,1... | collective-permute-start | bytes 786440 | tf_op jit(solution)/shard_map/ppermute | solution.py:126
  126.7 8.9 %collective-permute-start.17 = (bf16[512,256]{1,0:T(8,128)(2,1)S(1)}, bf16[512,256]{1,0:T(8,128)(2,1)S(1)}, u32[]{:S(2)}, u32[]{:S(2)}) collective-permute-start(bf16[512,256]{1,0:T(8,128)(2,1)S(1)} %shard_map.71.own_ref), channel_id=1, source_target_pairs={{0,15},{1,0},{2,1},{3,2},{4,3},{5,4},{6,5},{7,6},{8,7},{9,8},{10,9... | collective-permute-start | bytes 786440 | tf_op jit(solution)/shard_map/ppermute | solution.py:127
  136.2 10.3 %collective-permute-start.18 = (bf16[512,256]{1,0:T(8,128)(2,1)S(1)}, bf16[512,256]{1,0:T(8,128)(2,1)S(1)}, u32[]{:S(2)}, u32[]{:S(2)}) collective-permute-start(bf16[512,256]{1,0:T(8,128)(2,1)S(1)} %shard_map.73.own_ref), channel_id=1, source_target_pairs={{0,1},{1,2},{2,3},{3,4},{4,5},{5,6},{6,7},{7,8},{8,9},{9,10},{10,1... | collective-permute-start | bytes 786440 | tf_op jit(solution)/shard_map/ppermute | solution.py:126
  136.3 10.3 %collective-permute-start.19 = (bf16[512,256]{1,0:T(8,128)(2,1)S(1)}, bf16[512,256]{1,0:T(8,128)(2,1)S(1)}, u32[]{:S(2)}, u32[]{:S(2)}) collective-permute-start(bf16[512,256]{1,0:T(8,128)(2,1)S(1)} %shard_map.73.own_ref), channel_id=1, source_target_pairs={{0,15},{1,0},{2,1},{3,2},{4,3},{5,4},{6,5},{7,6},{8,7},{9,8},{10,9... | collective-permute-start | bytes 786440 | tf_op jit(solution)/shard_map/ppermute | solution.py:127
  147.2 11.5 %collective-permute-start.20 = (bf16[512,256]{1,0:T(8,128)(2,1)S(1)}, bf16[512,256]{1,0:T(8,128)(2,1)S(1)}, u32[]{:S(2)}, u32[]{:S(2)}) collective-permute-start(bf16[512,256]{1,0:T(8,128)(2,1)S(1)} %shard_map.75.own_ref), channel_id=1, source_target_pairs={{0,1},{1,2},{2,3},{3,4},{4,5},{5,6},{6,7},{7,8},{8,9},{9,10},{10,1... | collective-permute-start | bytes 786440 | tf_op jit(solution)/shard_map/ppermute | solution.py:126
  147.3 11.4 %collective-permute-start.21 = (bf16[512,256]{1,0:T(8,128)(2,1)S(1)}, bf16[512,256]{1,0:T(8,128)(2,1)S(1)}, u32[]{:S(2)}, u32[]{:S(2)}) collective-permute-start(bf16[512,256]{1,0:T(8,128)(2,1)S(1)} %shard_map.75.own_ref), channel_id=1, source_target_pairs={{0,15},{1,0},{2,1},{3,2},{4,3},{5,4},{6,5},{7,6},{8,7},{9,8},{10,9... | collective-permute-start | bytes 786440 | tf_op jit(solution)/shard_map/ppermute | solution.py:127
  159.3 11.6 %collective-permute-start.22 = (bf16[512,256]{1,0:T(8,128)(2,1)S(1)}, bf16[512,256]{1,0:T(8,128)(2,1)S(1)}, u32[]{:S(2)}, u32[]{:S(2)}) collective-permute-start(bf16[512,256]{1,0:T(8,128)(2,1)S(1)} %shard_map.77.own_ref), channel_id=1, source_target_pairs={{0,1},{1,2},{2,3},{3,4},{4,5},{5,6},{6,7},{7,8},{8,9},{9,10},{10,1... | collective-permute-start | bytes 786440 | tf_op jit(solution)/shard_map/ppermute | solution.py:126
  159.4 11.5 %collective-permute-start.23 = (bf16[512,256]{1,0:T(8,128)(2,1)S(1)}, bf16[512,256]{1,0:T(8,128)(2,1)S(1)}, u32[]{:S(2)}, u32[]{:S(2)}) collective-permute-start(bf16[512,256]{1,0:T(8,128)(2,1)S(1)} %shard_map.77.own_ref), channel_id=1, source_target_pairs={{0,15},{1,0},{2,1},{3,2},{4,3},{5,4},{6,5},{7,6},{8,7},{9,8},{10,9... | collective-permute-start | bytes 786440 | tf_op jit(solution)/shard_map/ppermute | solution.py:127
  171.6 10.3 %collective-permute-start.24 = (bf16[512,256]{1,0:T(8,128)(2,1)S(1)}, bf16[512,256]{1,0:T(8,128)(2,1)S(1)}, u32[]{:S(2)}, u32[]{:S(2)}) collective-permute-start(bf16[512,256]{1,0:T(8,128)(2,1)S(1)} %shard_map.79.own_ref), channel_id=1, source_target_pairs={{0,1},{1,2},{2,3},{3,4},{4,5},{5,6},{6,7},{7,8},{8,9},{9,10},{10,1... | collective-permute-start | bytes 786440 | tf_op jit(solution)/shard_map/ppermute | solution.py:126
  171.7 10.2 %collective-permute-start.25 = (bf16[512,256]{1,0:T(8,128)(2,1)S(1)}, bf16[512,256]{1,0:T(8,128)(2,1)S(1)}, u32[]{:S(2)}, u32[]{:S(2)}) collective-permute-start(bf16[512,256]{1,0:T(8,128)(2,1)S(1)} %shard_map.79.own_ref), channel_id=1, source_target_pairs={{0,15},{1,0},{2,1},{3,2},{4,3},{5,4},{6,5},{7,6},{8,7},{9,8},{10,9... | collective-permute-start | bytes 786440 | tf_op jit(solution)/shard_map/ppermute | solution.py:127
  182.6 9.4 %collective-permute-start.26 = (bf16[512,256]{1,0:T(8,128)(2,1)S(1)}, bf16[512,256]{1,0:T(8,128)(2,1)S(1)}, u32[]{:S(2)}, u32[]{:S(2)}) collective-permute-start(bf16[512,256]{1,0:T(8,128)(2,1)S(1)} %shard_map.81.own_ref), channel_id=1, source_target_pairs={{0,1},{1,2},{2,3},{3,4},{4,5},{5,6},{6,7},{7,8},{8,9},{9,10},{10,1... | collective-permute-start | bytes 786440 | tf_op jit(solution)/shard_map/ppermute | solution.py:126
  182.6 9.3 %collective-permute-start.27 = (bf16[512,256]{1,0:T(8,128)(2,1)S(1)}, bf16[512,256]{1,0:T(8,128)(2,1)S(1)}, u32[]{:S(2)}, u32[]{:S(2)}) collective-permute-start(bf16[512,256]{1,0:T(8,128)(2,1)S(1)} %shard_map.81.own_ref), channel_id=1, source_target_pairs={{0,15},{1,0},{2,1},{3,2},{4,3},{5,4},{6,5},{7,6},{8,7},{9,8},{10,9... | collective-permute-start | bytes 786440 | tf_op jit(solution)/shard_map/ppermute | solution.py:127
  192.6 8.6 %collective-permute-start.28 = (bf16[512,256]{1,0:T(8,128)(2,1)S(1)}, bf16[512,256]{1,0:T(8,128)(2,1)S(1)}, u32[]{:S(2)}, u32[]{:S(2)}) collective-permute-start(bf16[512,256]{1,0:T(8,128)(2,1)S(1)} %shard_map.83.own_ref), channel_id=1, source_target_pairs={{0,1},{1,2},{2,3},{3,4},{4,5},{5,6},{6,7},{7,8},{8,9},{9,10},{10,1... | collective-permute-start | bytes 786440 | tf_op jit(solution)/shard_map/ppermute | solution.py:126
  202.6 8.9 %collective-permute-start.30 = (bf16[512,256]{1,0:T(8,128)(2,1)}, bf16[512,256]{1,0:T(8,128)(2,1)}, u32[]{:S(2)}, u32[]{:S(2)}) collective-permute-start(bf16[512,256]{1,0:T(8,128)(2,1)} %shard_map.85.own_ref), channel_id=1, source_target_pairs={{0,1},{1,2},{2,3},{3,4},{4,5},{5,6},{6,7},{7,8},{8,9},{9,10},{10,1... | collective-permute-start | bytes 786440 | tf_op jit(solution)/shard_map/ppermute | solution.py:126
  202.6 8.9 %collective-permute-start.31 = (bf16[512,256]{1,0:T(8,128)(2,1)}, bf16[512,256]{1,0:T(8,128)(2,1)}, u32[]{:S(2)}, u32[]{:S(2)}) collective-permute-start(bf16[512,256]{1,0:T(8,128)(2,1)} %shard_map.85.own_ref), channel_id=1, source_target_pairs={{0,15},{1,0},{2,1},{3,2},{4,3},{5,4},{6,5},{7,6},{8,7},{9,8},{10,9... | collective-permute-start | bytes 786440 | tf_op jit(solution)/shard_map/ppermute | solution.py:127
  215.8 16.8 %collective-permute-start.32 = (bf16[512,256]{1,0:T(8,128)(2,1)S(1)}, bf16[512,256]{1,0:T(8,128)(2,1)S(1)}, u32[]{:S(2)}, u32[]{:S(2)}) collective-permute-start(bf16[512,256]{1,0:T(8,128)(2,1)S(1)} %get-tuple-element.11), channel_id=1, source_target_pairs={{0,16},{16,0},{32,48},{48,32},{64,80},{80,64},{96,112},{112,96},{1... | collective-permute-start | bytes 786440 | tf_op jit(solution)/shard_map/ppermute | solution.py:134
  (37 other events, 314.5 us)
Sparse Core Ops, SparseCore 0:
  9.2 43.9 all-gather.1

commit v3 on v2

--- a/solution.py
+++ b/solution.py
@@ -95,6 +95,14 @@
     )(to_before, to_after, part, before, after, initial, weight)
 
 
+RING = ((0, 0), (0, 1), (1, 1), (2, 1), (3, 1), (3, 0), (2, 0), (1, 0))
+
+
+def ring_node(span, pair):
+    y, x = RING[pair % len(RING)]
+    return y * 4 + x + 2 * span
+
+
 def on_device(features, tiles, tile_cols, tile_count, weights):
     groups = lax.axis_size("node")
     layers = lax.axis_size("segment")
@@ -102,38 +110,61 @@
     node = lax.axis_index("node")
     per_group, slots = tile_cols.shape[1:]
     core = seg % 2
-    up = [(n, (n + 1) % groups) for n in range(groups)]
-    down = [(n, (n - 1) % groups) for n in range(groups)]
+    both = ("segment", "node")
     swap = [(s, s ^ 1) for s in range(layers)]
+    gather, across_pairs = [], []
+    for plane in range(0, layers, 2):
+        for span in range(2):
+            for g in range(groups):
+                held_at = (plane + g % 2) * groups + ring_node(span, g // 2)
+                gather.append(((plane + span) * groups + g, held_at))
+                beyond = g + 1 if g % 2 else g + groups - 1
+                beyond_at = (plane + beyond % 2) * groups + ring_node(span, beyond % groups // 2)
+                across_pairs.append((held_at, beyond_at))
+    scatter = [(b, a) for a, b in gather]
 
     all_weights = lax.all_gather(weights[0], "segment", axis=0, tiled=False)
 
     cols = lax.dynamic_index_in_dim(tile_cols, core, 0, keepdims=False)
     count = lax.dynamic_index_in_dim(tile_count, core, 0, keepdims=False)
     relative = (cols - (node - 1) * per_group) % (per_group * groups)
-    places = jnp.where(relative < per_group, relative + per_group, jnp.where(relative < 2 * per_group, relative - per_group, relative))
+    side = relative // per_group
+    part_of = jnp.where(side == 1, 0, jnp.where((side == 2) == (node % 2 == 0), 1, 2))
+    places = part_of * per_group + relative % per_group
     places = jnp.where(jnp.arange(slots, dtype=jnp.int32)[None, :] < count[:, None], places, 12)
+    note = jnp.zeros((16, BLOCK), jnp.bfloat16).at[0:per_group, 0:slots].set(places.astype(jnp.bfloat16))
 
-    initial = lax.dynamic_index_in_dim(features, core, 0, keepdims=False)
-    held = lax.dynamic_index_in_dim(tiles, core, 0, keepdims=False).reshape(-1, BLOCK, BLOCK)
-    to_own, to_before, to_after = dense_adjacency(places, held)
+    mine = lax.dynamic_index_in_dim(features, core, 0, keepdims=False)
+    mine_tiles = lax.dynamic_index_in_dim(tiles, core, 0, keepdims=False).reshape(-1, BLOCK)
+    bundle = jnp.concatenate([mine_tiles, mine[:, :BLOCK], mine[:, BLOCK:], note], axis=0)
+    bundle = lax.ppermute(bundle, both, gather)
+
+    tile_rows = mine_tiles.shape[0]
+    rows = mine.shape[0]
+    held_tiles = bundle[:tile_rows].reshape(-1, BLOCK, BLOCK)
+    initial = jnp.concatenate(
+        [bundle[tile_rows : tile_rows + rows], bundle[tile_rows + rows : tile_rows + 2 * rows]], axis=1
+    )
+    held_places = bundle[tile_rows + 2 * rows :][0:per_group, 0:slots].astype(jnp.int32)
+    to_own, to_beside, to_across = dense_adjacency(held_places, held_tiles)
 
     hidden = initial
     kept = [initial, initial]
     low = seg - core
     for step in range(layers):
         beta = math.log(0.5 / (step + 1) + 1.0)
-        before = lax.ppermute(hidden, "node", up)
-        after = lax.ppermute(hidden, "node", down)
+        across = lax.ppermute(hidden, both, across_pairs)
+        beside = lax.ppermute(hidden, "segment", swap)
         part = own_part(to_own, hidden)
-        hidden = layer(beta, to_before, to_after, part, before, after, initial, all_weights[step])
+        hidden = layer(beta, to_beside, to_across, part, beside, across, initial, all_weights[step])
         kept[step % 2] = jnp.where(low == step - step % 2, hidden, kept[step % 2])
 
-    mine = jnp.where(core == 0, kept[0], kept[1])
-    give = jnp.where(core == 0, kept[1], kept[0])
+    arrived = [lax.ppermute(value, both, scatter) for value in kept]
+    mine_out = jnp.where(core == 0, arrived[0], arrived[1])
+    give = jnp.where(core == 0, arrived[1], arrived[0])
     other = lax.ppermute(give, "segment", swap)
-    first = jnp.where(core == 0, mine, other)
-    second = jnp.where(core == 0, other, mine)
+    first = jnp.where(core == 0, mine_out, other)
+    second = jnp.where(core == 0, other, mine_out)
     return jnp.stack([first, second])[None]
 
 

time: 241 us -> 212 us (0.88)
  starting transfers between devices: 96.7 us -> 62.1 us
    ppermute x32 -> x35, waiting for transfers between devices: 56.8 us -> 87.9 us  [the longest x16 61.6 us: on_device(): across = lax.ppermute(hidden, both, across_pairs)]
    all_gather x1, waiting for transfers between devices: 33.9 us -> 3.08 us  [on_device(): all_weights = lax.all_gather(weights[0], 'segment', axis=0, tiled=False)]
    ppermute x32 -> x35, starting transfers between devices: 81.1 us -> 62 us  [the longest x16 32.3 us: on_device(): beside = lax.ppermute(hidden, 'segment', swap)]
    ppermute x1, starting transfers between devices: 15.6 us -> 0.09 us  [on_device(): other = lax.ppermute(give, 'segment', swap)]
  transfers between devices with their start and end apart: 34 -> 37, of which waited for: 17 -> 32; matrix products, arithmetic and copies ran while one was open for 2% -> 3% of each run, Pallas kernels for 6% -> 8%
where the time goes in v3:
time: 212 us; the launch traced here: 209 us
  waiting for transfers between devices  93.2 us (44%)
  starting transfers between devices  62.1 us (29%)
  Pallas kernels  28.1 us (13%)
  between operations  14.3 us (7%)
  local copies, waits for them, and re-layouts  8.04 us (4%)
  other arithmetic  3.39 us (2%)
    ppermute x16, waiting for transfers between devices, on_device(): across = lax.ppermute(hidden, both, across_pairs)  61.6 us
    ppermute x16, starting transfers between devices, on_device(): beside = lax.ppermute(hidden, 'segment', swap)  32.3 us
    ppermute x16, starting transfers between devices, on_device(): across = lax.ppermute(hidden, both, across_pairs)  15.8 us
    ppermute x1, waiting for transfers between devices, on_device(): bundle = lax.ppermute(bundle, both, gather)  14.6 us
    pallas_call x16, Pallas kernels, own_part(): pl.pallas_call(own_kernel, out_shape=jax.ShapeDtypeStruct(own.shape, jnp....  13.2 us
    pallas_call x16, Pallas kernels, layer(): pl.pallas_call(lambda *refs: layer_kernel(beta, *refs), out_shape=jax.Sha...  13 us
    ppermute x2, starting transfers between devices, on_device(): arrived = [lax.ppermute(value, both, scatter) for value in kept]  7.88 us
    ppermute x1, starting transfers between devices, on_device(): bundle = lax.ppermute(bundle, both, gather)  6.04 us
  transfers between devices with their start and end apart: 37, of which 32 were waited for; matrix products, arithmetic and copies ran while one was open for 3% of the time, Pallas kernels for 8%

profile of v3, /device:TPU:1, one launch (start us, length us, event | category | flops | bytes accessed | tf_op | source)
XLA Modules:
  0.0 209.1 jit_solution(11349620201206328564)
XLA Ops:
  9.3 6.0 %collective-permute-start = (bf16[5136,128]{1,0:T(8,128)(2,1)S(1)}, bf16[5136,128]{1,0:T(8,128)(2,1)S(1)}, u32[]{:S(2)}, u32[]{:S(2)}) collective-permute-start(bf16[5136,128]{1,0:T(8,128)(2,1)S(1)} %fusion.1), channel_id=1, source_target_pairs={{0,0},{1,16},{2,1},{3,17},{4,5},{5,21},{6,9},{7,25},{8,13},{9,29},... | collective-permute-start | bytes 3944456 | tf_op jit(solution)/shard_map/ppermute | solution.py:140
  15.3 14.6 %collective-permute-done = bf16[5136,128]{1,0:T(8,128)(2,1)S(1)} collective-permute-done((bf16[5136,128]{1,0:T(8,128)(2,1)S(1)}, bf16[5136,128]{1,0:T(8,128)(2,1)S(1)}, u32[]{:S(2)}, u32[]{:S(2)}) %collective-permute-start) | collective-permute-done | bytes 1314848 | tf_op jit(solution)/shard_map/ppermute | solution.py:140
  30.1 15.7 %collective-permute-start.2 = (bf16[512,256]{1,0:T(8,128)(2,1)S(1)}, bf16[512,256]{1,0:T(8,128)(2,1)}, u32[]{:S(2)}, u32[]{:S(2)}) collective-permute-start(bf16[512,256]{1,0:T(8,128)(2,1)S(1)} %pad_maximum_fusion.own_ref.refs_5_), channel_id=1, source_target_pairs={{0,20},{16,1},{1,16},{17,5},{5,17},{21,9},{9,21},{25,13},{13,25},{... | collective-permute-start | bytes 786440 | tf_op jit(solution)/shard_map/ppermute | solution.py:156
  45.9 1.8 shard_map.55
  50.1 3.1 %all-gather.2.cloned.1.call-done = bf16[16,256,256]{2,1,0:T(8,128)(2,1)} async-done(((bf16[1,256,256]{2,1,0:T(8,128)(2,1)}), bf16[16,256,256]{2,1,0:T(8,128)(2,1)}) %all-gather.2.cloned.1.call-update) | async-done | bytes 2097168 | tf_op jit(solution)/shard_map/all_gather | solution.py:126
  53.2 2.5 %slice_bitcast_fusion = (bf16[256,256]{1,0:T(8,128)(2,1)S(1)}, bf16[256,256]{1,0:T(8,128)(2,1)}, bf16[256,256]{1,0:T(8,128)(2,1)S(1)}, bf16[256,256]{1,0:T(8,128...) fusion(bf16[16,256,256]{2,1,0:T(8,128)(2,1)} %all-gather.2.clon, ...), kind=kLoop, calls=%fused_computation.12 | loop fusion | bytes 4194304 | tf_op jit(solution)/shard_map/squeeze | solution.py:159
  55.7 1.7 shard_map.57.own_ref
  57.4 12.4 %collective-permute-start.3 = (bf16[512,256]{1,0:T(8,128)(2,1)S(1)}, bf16[512,256]{1,0:T(8,128)(2,1)S(1)}, u32[]{:S(2)}, u32[]{:S(2)}) collective-permute-start(bf16[512,256]{1,0:T(8,128)(2,1)S(1)} %shard_map.57.own_ref), channel_id=1, source_target_pairs={{0,16},{16,0},{32,48},{48,32},{64,80},{80,64},{96,112},{112,96},{1... | collective-permute-start | bytes 786440 | tf_op jit(solution)/shard_map/ppermute | solution.py:157
  71.0 4.6 %collective-permute-done.4.refs_4_ = bf16[512,256]{1,0:T(8,128)(2,1)S(1)} collective-permute-done((bf16[512,256]{1,0:T(8,128)(2,1)S(1)}, bf16[512,256]{1,0:T(8,128)(2,1)S(1)}, u32[]{:S(2)}, u32[]{:S(2)}) %collective-permute-start.4) | collective-permute-done | bytes 262176 | tf_op jit(solution)/shard_map/ppermute | solution.py:156
  76.3 13.3 %collective-permute-start.5 = (bf16[512,256]{1,0:T(8,128)(2,1)S(1)}, bf16[512,256]{1,0:T(8,128)(2,1)S(1)}, u32[]{:S(2)}, u32[]{:S(2)}) collective-permute-start(bf16[512,256]{1,0:T(8,128)(2,1)S(1)} %shard_map.59.own_ref), channel_id=1, source_target_pairs={{0,16},{16,0},{32,48},{48,32},{64,80},{80,64},{96,112},{112,96},{1... | collective-permute-start | bytes 786440 | tf_op jit(solution)/shard_map/ppermute | solution.py:157
  90.7 4.6 %collective-permute-done.6.refs_4_ = bf16[512,256]{1,0:T(8,128)(2,1)S(1)} collective-permute-done((bf16[512,256]{1,0:T(8,128)(2,1)S(1)}, bf16[512,256]{1,0:T(8,128)(2,1)S(1)}, u32[]{:S(2)}, u32[]{:S(2)}) %collective-permute-start.6) | collective-permute-done | bytes 262176 | tf_op jit(solution)/shard_map/ppermute | solution.py:156
  97.7 4.4 %collective-permute-done.8.refs_4_ = bf16[512,256]{1,0:T(8,128)(2,1)S(1)} collective-permute-done((bf16[512,256]{1,0:T(8,128)(2,1)S(1)}, bf16[512,256]{1,0:T(8,128)(2,1)S(1)}, u32[]{:S(2)}, u32[]{:S(2)}) %collective-permute-start.8) | collective-permute-done | bytes 262176 | tf_op jit(solution)/shard_map/ppermute | solution.py:156
  102.8 2.1 %collective-permute-start.9 = (bf16[512,256]{1,0:T(8,128)(2,1)S(1)}, bf16[512,256]{1,0:T(8,128)(2,1)S(1)}, u32[]{:S(2)}, u32[]{:S(2)}) collective-permute-start(bf16[512,256]{1,0:T(8,128)(2,1)S(1)} %shard_map.63.own_ref), channel_id=1, source_target_pairs={{0,16},{16,0},{32,48},{48,32},{64,80},{80,64},{96,112},{112,96},{1... | collective-permute-start | bytes 786440 | tf_op jit(solution)/shard_map/ppermute | solution.py:157
  105.7 2.9 %collective-permute-done.10.refs_4_ = bf16[512,256]{1,0:T(8,128)(2,1)S(1)} collective-permute-done((bf16[512,256]{1,0:T(8,128)(2,1)S(1)}, bf16[512,256]{1,0:T(8,128)(2,1)S(1)}, u32[]{:S(2)}, u32[]{:S(2)}) %collective-permute-start.10) | collective-permute-done | bytes 262176 | tf_op jit(solution)/shard_map/ppermute | solution.py:156
  110.9 4.6 %collective-permute-done.12.refs_4_ = bf16[512,256]{1,0:T(8,128)(2,1)S(1)} collective-permute-done((bf16[512,256]{1,0:T(8,128)(2,1)S(1)}, bf16[512,256]{1,0:T(8,128)(2,1)S(1)}, u32[]{:S(2)}, u32[]{:S(2)}) %collective-permute-start.12) | collective-permute-done | bytes 262176 | tf_op jit(solution)/shard_map/ppermute | solution.py:156
  118.0 4.4 %collective-permute-done.14.refs_4_ = bf16[512,256]{1,0:T(8,128)(2,1)S(1)} collective-permute-done((bf16[512,256]{1,0:T(8,128)(2,1)S(1)}, bf16[512,256]{1,0:T(8,128)(2,1)S(1)}, u32[]{:S(2)}, u32[]{:S(2)}) %collective-permute-start.14) | collective-permute-done | bytes 262176 | tf_op jit(solution)/shard_map/ppermute | solution.py:156
  124.6 4.6 %collective-permute-done.16.refs_4_ = bf16[512,256]{1,0:T(8,128)(2,1)S(1)} collective-permute-done((bf16[512,256]{1,0:T(8,128)(2,1)S(1)}, bf16[512,256]{1,0:T(8,128)(2,1)S(1)}, u32[]{:S(2)}, u32[]{:S(2)}) %collective-permute-start.16) | collective-permute-done | bytes 262176 | tf_op jit(solution)/shard_map/ppermute | solution.py:156
  131.5 4.4 %collective-permute-done.18.refs_4_ = bf16[512,256]{1,0:T(8,128)(2,1)S(1)} collective-permute-done((bf16[512,256]{1,0:T(8,128)(2,1)S(1)}, bf16[512,256]{1,0:T(8,128)(2,1)S(1)}, u32[]{:S(2)}, u32[]{:S(2)}) %collective-permute-start.18) | collective-permute-done | bytes 262176 | tf_op jit(solution)/shard_map/ppermute | solution.py:156
  138.2 4.6 %collective-permute-done.20.refs_4_ = bf16[512,256]{1,0:T(8,128)(2,1)S(1)} collective-permute-done((bf16[512,256]{1,0:T(8,128)(2,1)S(1)}, bf16[512,256]{1,0:T(8,128)(2,1)S(1)}, u32[]{:S(2)}, u32[]{:S(2)}) %collective-permute-start.20) | collective-permute-done | bytes 262176 | tf_op jit(solution)/shard_map/ppermute | solution.py:156
  145.1 4.4 %collective-permute-done.22.refs_4_ = bf16[512,256]{1,0:T(8,128)(2,1)S(1)} collective-permute-done((bf16[512,256]{1,0:T(8,128)(2,1)S(1)}, bf16[512,256]{1,0:T(8,128)(2,1)S(1)}, u32[]{:S(2)}, u32[]{:S(2)}) %collective-permute-start.22) | collective-permute-done | bytes 262176 | tf_op jit(solution)/shard_map/ppermute | solution.py:156
  151.8 4.6 %collective-permute-done.24.refs_4_ = bf16[512,256]{1,0:T(8,128)(2,1)S(1)} collective-permute-done((bf16[512,256]{1,0:T(8,128)(2,1)S(1)}, bf16[512,256]{1,0:T(8,128)(2,1)S(1)}, u32[]{:S(2)}, u32[]{:S(2)}) %collective-permute-start.24) | collective-permute-done | bytes 262176 | tf_op jit(solution)/shard_map/ppermute | solution.py:156
  158.7 4.4 %collective-permute-done.26.refs_4_ = bf16[512,256]{1,0:T(8,128)(2,1)S(1)} collective-permute-done((bf16[512,256]{1,0:T(8,128)(2,1)S(1)}, bf16[512,256]{1,0:T(8,128)(2,1)S(1)}, u32[]{:S(2)}, u32[]{:S(2)}) %collective-permute-start.26) | collective-permute-done | bytes 262176 | tf_op jit(solution)/shard_map/ppermute | solution.py:156
  165.6 4.6 %collective-permute-done.28.refs_4_ = bf16[512,256]{1,0:T(8,128)(2,1)S(1)} collective-permute-done((bf16[512,256]{1,0:T(8,128)(2,1)S(1)}, bf16[512,256]{1,0:T(8,128)(2,1)S(1)}, u32[]{:S(2)}, u32[]{:S(2)}) %collective-permute-start.28) | collective-permute-done | bytes 262176 | tf_op jit(solution)/shard_map/ppermute | solution.py:156
  170.2 1.4 shard_map.83.own_ref
  171.7 1.8 shard_map.84.refs_2_
  173.6 4.3 %collective-permute-done.30.refs_4_ = bf16[512,256]{1,0:T(8,128)(2,1)} collective-permute-done((bf16[512,256]{1,0:T(8,128)(2,1)}, bf16[512,256]{1,0:T(8,128)(2,1)}, u32[]{:S(2)}, u32[]{:S(2)}) %collective-permute-start.30) | collective-permute-done | bytes 262176 | tf_op jit(solution)/shard_map/ppermute | solution.py:156
  177.8 1.0 copy-done.3
  179.8 1.7 shard_map.85.own_ref
  183.1 3.8 %collective-permute-start.31 = (bf16[512,256]{1,0:T(8,128)(2,1)}, bf16[512,256]{1,0:T(8,128)(2,1)}, u32[]{:S(2)}, u32[]{:S(2)}) collective-permute-start(bf16[512,256]{1,0:T(8,128)(2,1)} %select_select_fusion.1), channel_id=1, source_target_pairs={{0,0},{16,1},{1,2},{17,3},{5,4},{21,5},{9,6},{25,7},{13,8},{29,9},... | collective-permute-start | bytes 786440 | tf_op jit(solution)/shard_map/ppermute | solution.py:162
  188.8 4.1 %collective-permute-start.34 = (bf16[512,256]{1,0:T(8,128)(2,1)S(1)}, bf16[512,256]{1,0:T(8,128)(2,1)S(1)}, u32[]{:S(2)}, u32[]{:S(2)}) collective-permute-start(bf16[512,256]{1,0:T(8,128)(2,1)S(1)} %select_select_fusion), channel_id=1, source_target_pairs={{0,0},{16,1},{1,2},{17,3},{5,4},{21,5},{9,6},{25,7},{13,8},{29,9},... | collective-permute-start | bytes 786440 | tf_op jit(solution)/shard_map/ppermute | solution.py:162
  193.6 5.1 %collective-permute-done.34 = bf16[512,256]{1,0:T(8,128)(2,1)S(1)} collective-permute-done((bf16[512,256]{1,0:T(8,128)(2,1)S(1)}, bf16[512,256]{1,0:T(8,128)(2,1)S(1)}, u32[]{:S(2)}, u32[]{:S(2)}) %collective-permute-start.34) | collective-permute-done | bytes 262176 | tf_op jit(solution)/shard_map/ppermute | solution.py:162
  199.8 1.5 collective-permute-done.35
  (170 shorter events, 39.6 us)
Async XLA Ops:
  6.5 46.6 %all-gather.2.cloned.1.call-start = ((), (), s32[]{:S(2)}) async-start(), calls=%async_computation | async-start | bytes 2228224 | tf_op jit(solution)/shard_map/all_gather | solution.py:126
  9.3 20.7 %collective-permute-start = (bf16[5136,128]{1,0:T(8,128)(2,1)S(1)}, bf16[5136,128]{1,0:T(8,128)(2,1)S(1)}, u32[]{:S(2)}, u32[]{:S(2)}) collective-permute-start(bf16[5136,128]{1,0:T(8,128)(2,1)S(1)} %fusion.1), channel_id=1, source_target_pairs={{0,0},{1,16},{2,1},{3,17},{4,5},{5,21},{6,9},{7,25},{8,13},{9,29},... | collective-permute-start | bytes 3944456 | tf_op jit(solution)/shard_map/ppermute | solution.py:140
  30.0 25.7 %collective-permute-start.1 = (bf16[512,256]{1,0:T(8,128)(2,1)S(1)}, bf16[512,256]{1,0:T(8,128)(2,1)}, u32[]{:S(2)}, u32[]{:S(2)}) collective-permute-start(bf16[512,256]{1,0:T(8,128)(2,1)S(1)} %pad_maximum_fusion.own_ref.refs_5_), channel_id=1, source_target_pairs={{0,16},{16,0},{32,48},{48,32},{64,80},{80,64},{96,112},{112,96},{1... | collective-permute-start | bytes 786440 | tf_op jit(solution)/shard_map/ppermute | solution.py:157
  30.1 25.6 %collective-permute-start.2 = (bf16[512,256]{1,0:T(8,128)(2,1)S(1)}, bf16[512,256]{1,0:T(8,128)(2,1)}, u32[]{:S(2)}, u32[]{:S(2)}) collective-permute-start(bf16[512,256]{1,0:T(8,128)(2,1)S(1)} %pad_maximum_fusion.own_ref.refs_5_), channel_id=1, source_target_pairs={{0,20},{16,1},{1,16},{17,5},{5,17},{21,9},{9,21},{25,13},{13,25},{... | collective-permute-start | bytes 786440 | tf_op jit(solution)/shard_map/ppermute | solution.py:156
  57.4 13.6 %collective-permute-start.3 = (bf16[512,256]{1,0:T(8,128)(2,1)S(1)}, bf16[512,256]{1,0:T(8,128)(2,1)S(1)}, u32[]{:S(2)}, u32[]{:S(2)}) collective-permute-start(bf16[512,256]{1,0:T(8,128)(2,1)S(1)} %shard_map.57.own_ref), channel_id=1, source_target_pairs={{0,16},{16,0},{32,48},{48,32},{64,80},{80,64},{96,112},{112,96},{1... | collective-permute-start | bytes 786440 | tf_op jit(solution)/shard_map/ppermute | solution.py:157
  69.9 5.8 %collective-permute-start.4 = (bf16[512,256]{1,0:T(8,128)(2,1)S(1)}, bf16[512,256]{1,0:T(8,128)(2,1)S(1)}, u32[]{:S(2)}, u32[]{:S(2)}) collective-permute-start(bf16[512,256]{1,0:T(8,128)(2,1)S(1)} %shard_map.57.own_ref), channel_id=1, source_target_pairs={{0,20},{16,1},{1,16},{17,5},{5,17},{21,9},{9,21},{25,13},{13,25},{... | collective-permute-start | bytes 786440 | tf_op jit(solution)/shard_map/ppermute | solution.py:156
  76.3 14.4 %collective-permute-start.5 = (bf16[512,256]{1,0:T(8,128)(2,1)S(1)}, bf16[512,256]{1,0:T(8,128)(2,1)S(1)}, u32[]{:S(2)}, u32[]{:S(2)}) collective-permute-start(bf16[512,256]{1,0:T(8,128)(2,1)S(1)} %shard_map.59.own_ref), channel_id=1, source_target_pairs={{0,16},{16,0},{32,48},{48,32},{64,80},{80,64},{96,112},{112,96},{1... | collective-permute-start | bytes 786440 | tf_op jit(solution)/shard_map/ppermute | solution.py:157
  89.6 5.8 %collective-permute-start.6 = (bf16[512,256]{1,0:T(8,128)(2,1)S(1)}, bf16[512,256]{1,0:T(8,128)(2,1)S(1)}, u32[]{:S(2)}, u32[]{:S(2)}) collective-permute-start(bf16[512,256]{1,0:T(8,128)(2,1)S(1)} %shard_map.59.own_ref), channel_id=1, source_target_pairs={{0,20},{16,1},{1,16},{17,5},{5,17},{21,9},{9,21},{25,13},{13,25},{... | collective-permute-start | bytes 786440 | tf_op jit(solution)/shard_map/ppermute | solution.py:156
  96.2 5.8 %collective-permute-start.8 = (bf16[512,256]{1,0:T(8,128)(2,1)S(1)}, bf16[512,256]{1,0:T(8,128)(2,1)S(1)}, u32[]{:S(2)}, u32[]{:S(2)}) collective-permute-start(bf16[512,256]{1,0:T(8,128)(2,1)S(1)} %shard_map.61.own_ref), channel_id=1, source_target_pairs={{0,20},{16,1},{1,16},{17,5},{5,17},{21,9},{9,21},{25,13},{13,25},{... | collective-permute-start | bytes 786440 | tf_op jit(solution)/shard_map/ppermute | solution.py:156
  102.7 5.9 %collective-permute-start.10 = (bf16[512,256]{1,0:T(8,128)(2,1)S(1)}, bf16[512,256]{1,0:T(8,128)(2,1)S(1)}, u32[]{:S(2)}, u32[]{:S(2)}) collective-permute-start(bf16[512,256]{1,0:T(8,128)(2,1)S(1)} %shard_map.63.own_ref), channel_id=1, source_target_pairs={{0,20},{16,1},{1,16},{17,5},{5,17},{21,9},{9,21},{25,13},{13,25},{... | collective-permute-start | bytes 786440 | tf_op jit(solution)/shard_map/ppermute | solution.py:156
  102.8 5.8 %collective-permute-start.9 = (bf16[512,256]{1,0:T(8,128)(2,1)S(1)}, bf16[512,256]{1,0:T(8,128)(2,1)S(1)}, u32[]{:S(2)}, u32[]{:S(2)}) collective-permute-start(bf16[512,256]{1,0:T(8,128)(2,1)S(1)} %shard_map.63.own_ref), channel_id=1, source_target_pairs={{0,16},{16,0},{32,48},{48,32},{64,80},{80,64},{96,112},{112,96},{1... | collective-permute-start | bytes 786440 | tf_op jit(solution)/shard_map/ppermute | solution.py:157
  109.2 1.6 collective-permute-start.11
  109.7 5.8 %collective-permute-start.12 = (bf16[512,256]{1,0:T(8,128)(2,1)S(1)}, bf16[512,256]{1,0:T(8,128)(2,1)S(1)}, u32[]{:S(2)}, u32[]{:S(2)}) collective-permute-start(bf16[512,256]{1,0:T(8,128)(2,1)S(1)} %shard_map.65.own_ref), channel_id=1, source_target_pairs={{0,20},{16,1},{1,16},{17,5},{5,17},{21,9},{9,21},{25,13},{13,25},{... | collective-permute-start | bytes 786440 | tf_op jit(solution)/shard_map/ppermute | solution.py:156
  116.1 1.8 collective-permute-start.13
  116.5 5.8 %collective-permute-start.14 = (bf16[512,256]{1,0:T(8,128)(2,1)S(1)}, bf16[512,256]{1,0:T(8,128)(2,1)S(1)}, u32[]{:S(2)}, u32[]{:S(2)}) collective-permute-start(bf16[512,256]{1,0:T(8,128)(2,1)S(1)} %shard_map.67.own_ref), channel_id=1, source_target_pairs={{0,20},{16,1},{1,16},{17,5},{5,17},{21,9},{9,21},{25,13},{13,25},{... | collective-permute-start | bytes 786440 | tf_op jit(solution)/shard_map/ppermute | solution.py:156
  123.0 1.6 collective-permute-start.15
  123.5 5.8 %collective-permute-start.16 = (bf16[512,256]{1,0:T(8,128)(2,1)S(1)}, bf16[512,256]{1,0:T(8,128)(2,1)S(1)}, u32[]{:S(2)}, u32[]{:S(2)}) collective-permute-start(bf16[512,256]{1,0:T(8,128)(2,1)S(1)} %shard_map.69.own_ref), channel_id=1, source_target_pairs={{0,20},{16,1},{1,16},{17,5},{5,17},{21,9},{9,21},{25,13},{13,25},{... | collective-permute-start | bytes 786440 | tf_op jit(solution)/shard_map/ppermute | solution.py:156
  130.1 5.8 %collective-permute-start.18 = (bf16[512,256]{1,0:T(8,128)(2,1)S(1)}, bf16[512,256]{1,0:T(8,128)(2,1)S(1)}, u32[]{:S(2)}, u32[]{:S(2)}) collective-permute-start(bf16[512,256]{1,0:T(8,128)(2,1)S(1)} %shard_map.71.own_ref), channel_id=1, source_target_pairs={{0,20},{16,1},{1,16},{17,5},{5,17},{21,9},{9,21},{25,13},{13,25},{... | collective-permute-start | bytes 786440 | tf_op jit(solution)/shard_map/ppermute | solution.py:156
  136.6 1.6 collective-permute-start.19
  137.0 5.8 %collective-permute-start.20 = (bf16[512,256]{1,0:T(8,128)(2,1)S(1)}, bf16[512,256]{1,0:T(8,128)(2,1)S(1)}, u32[]{:S(2)}, u32[]{:S(2)}) collective-permute-start(bf16[512,256]{1,0:T(8,128)(2,1)S(1)} %shard_map.73.own_ref), channel_id=1, source_target_pairs={{0,20},{16,1},{1,16},{17,5},{5,17},{21,9},{9,21},{25,13},{13,25},{... | collective-permute-start | bytes 786440 | tf_op jit(solution)/shard_map/ppermute | solution.py:156
  143.7 5.8 %collective-permute-start.22 = (bf16[512,256]{1,0:T(8,128)(2,1)S(1)}, bf16[512,256]{1,0:T(8,128)(2,1)S(1)}, u32[]{:S(2)}, u32[]{:S(2)}) collective-permute-start(bf16[512,256]{1,0:T(8,128)(2,1)S(1)} %shard_map.75.own_ref), channel_id=1, source_target_pairs={{0,20},{16,1},{1,16},{17,5},{5,17},{21,9},{9,21},{25,13},{13,25},{... | collective-permute-start | bytes 786440 | tf_op jit(solution)/shard_map/ppermute | solution.py:156
  150.1 1.6 collective-permute-start.23
  150.6 5.8 %collective-permute-start.24 = (bf16[512,256]{1,0:T(8,128)(2,1)S(1)}, bf16[512,256]{1,0:T(8,128)(2,1)S(1)}, u32[]{:S(2)}, u32[]{:S(2)}) collective-permute-start(bf16[512,256]{1,0:T(8,128)(2,1)S(1)} %shard_map.77.own_ref), channel_id=1, source_target_pairs={{0,20},{16,1},{1,16},{17,5},{5,17},{21,9},{9,21},{25,13},{13,25},{... | collective-permute-start | bytes 786440 | tf_op jit(solution)/shard_map/ppermute | solution.py:156
  157.3 5.8 %collective-permute-start.26 = (bf16[512,256]{1,0:T(8,128)(2,1)S(1)}, bf16[512,256]{1,0:T(8,128)(2,1)S(1)}, u32[]{:S(2)}, u32[]{:S(2)}) collective-permute-start(bf16[512,256]{1,0:T(8,128)(2,1)S(1)} %shard_map.79.own_ref), channel_id=1, source_target_pairs={{0,20},{16,1},{1,16},{17,5},{5,17},{21,9},{9,21},{25,13},{13,25},{... | collective-permute-start | bytes 786440 | tf_op jit(solution)/shard_map/ppermute | solution.py:156
  163.7 1.9 collective-permute-start.27
  164.4 5.8 %collective-permute-start.28 = (bf16[512,256]{1,0:T(8,128)(2,1)S(1)}, bf16[512,256]{1,0:T(8,128)(2,1)S(1)}, u32[]{:S(2)}, u32[]{:S(2)}) collective-permute-start(bf16[512,256]{1,0:T(8,128)(2,1)S(1)} %shard_map.81.own_ref), channel_id=1, source_target_pairs={{0,20},{16,1},{1,16},{17,5},{5,17},{21,9},{9,21},{25,13},{13,25},{... | collective-permute-start | bytes 786440 | tf_op jit(solution)/shard_map/ppermute | solution.py:156
  171.6 2.0 collective-permute-start.29
  171.7 6.1 %collective-permute-start.30 = (bf16[512,256]{1,0:T(8,128)(2,1)}, bf16[512,256]{1,0:T(8,128)(2,1)}, u32[]{:S(2)}, u32[]{:S(2)}) collective-permute-start(bf16[512,256]{1,0:T(8,128)(2,1)} %shard_map.83.own_ref), channel_id=1, source_target_pairs={{0,20},{16,1},{1,16},{17,5},{5,17},{21,9},{9,21},{25,13},{13,25},{... | collective-permute-start | bytes 786440 | tf_op jit(solution)/shard_map/ppermute | solution.py:156
  181.5 6.1 %collective-permute-start.32 = (bf16[512,256]{1,0:T(8,128)(2,1)S(1)}, bf16[512,256]{1,0:T(8,128)(2,1)S(1)}, u32[]{:S(2)}, u32[]{:S(2)}) collective-permute-start(bf16[512,256]{1,0:T(8,128)(2,1)S(1)} %shard_map.85.own_ref), channel_id=1, source_target_pairs={{0,16},{16,0},{32,48},{48,32},{64,80},{80,64},{96,112},{112,96},{1... | collective-permute-start | bytes 786440 | tf_op jit(solution)/shard_map/ppermute | solution.py:157
  182.0 5.8 %collective-permute-start.33 = (bf16[512,256]{1,0:T(8,128)(2,1)S(1)}, bf16[512,256]{1,0:T(8,128)(2,1)S(1)}, u32[]{:S(2)}, u32[]{:S(2)}) collective-permute-start(bf16[512,256]{1,0:T(8,128)(2,1)S(1)} %shard_map.85.own_ref), channel_id=1, source_target_pairs={{0,20},{16,1},{1,16},{17,5},{5,17},{21,9},{9,21},{25,13},{13,25},{... | collective-permute-start | bytes 786440 | tf_op jit(solution)/shard_map/ppermute | solution.py:156
  183.1 10.5 %collective-permute-start.31 = (bf16[512,256]{1,0:T(8,128)(2,1)}, bf16[512,256]{1,0:T(8,128)(2,1)}, u32[]{:S(2)}, u32[]{:S(2)}) collective-permute-start(bf16[512,256]{1,0:T(8,128)(2,1)} %select_select_fusion.1), channel_id=1, source_target_pairs={{0,0},{16,1},{1,2},{17,3},{5,4},{21,5},{9,6},{25,7},{13,8},{29,9},... | collective-permute-start | bytes 786440 | tf_op jit(solution)/shard_map/ppermute | solution.py:162
  188.8 9.9 %collective-permute-start.34 = (bf16[512,256]{1,0:T(8,128)(2,1)S(1)}, bf16[512,256]{1,0:T(8,128)(2,1)S(1)}, u32[]{:S(2)}, u32[]{:S(2)}) collective-permute-start(bf16[512,256]{1,0:T(8,128)(2,1)S(1)} %select_select_fusion), channel_id=1, source_target_pairs={{0,0},{16,1},{1,2},{17,3},{5,4},{21,5},{9,6},{25,7},{13,8},{29,9},... | collective-permute-start | bytes 786440 | tf_op jit(solution)/shard_map/ppermute | solution.py:162
  (44 other events, 280.9 us)
Sparse Core Ops, SparseCore 0:
  9.2 43.9 all-gather.1

commit v4 on v3

--- a/solution.py
+++ b/solution.py
@@ -95,12 +95,15 @@
     )(to_before, to_after, part, before, after, initial, weight)
 
 
-RING = ((0, 0), (0, 1), (1, 1), (2, 1), (3, 1), (3, 0), (2, 0), (1, 0))
+RINGS = (
+    ((1, 0), (0, 0), (0, 1), (1, 1), (2, 1), (3, 1), (3, 0), (2, 0)),
+    ((1, 2), (0, 2), (0, 3), (1, 3), (2, 3), (3, 3), (3, 2), (2, 2)),
+)
 
 
 def ring_node(span, pair):
-    y, x = RING[pair % len(RING)]
-    return y * 4 + x + 2 * span
+    y, x = RINGS[span][pair % 8]
+    return y * 4 + x
 
 
 def on_device(features, tiles, tile_cols, tile_count, weights):

time: 212 us -> 187 us (0.88); the launches traced: 209 us -> 186 us
  starting transfers between devices: 62.1 us -> 41.3 us
    ppermute x16, starting transfers between devices: 32.3 us -> 5.49 us  [on_device(): beside = lax.ppermute(hidden, 'segment', swap)]
    ppermute x1, waiting for transfers between devices: 14.6 us -> 28.4 us  [on_device(): bundle = lax.ppermute(bundle, both, gather)]
    ppermute x16, waiting for transfers between devices: 61.6 us -> 50.5 us  [on_device(): across = lax.ppermute(hidden, both, across_pairs)]
    ppermute x16, waiting for transfers between devices: 5.88 us -> 0.04 us  [on_device(): beside = lax.ppermute(hidden, 'segment', swap)]
    ppermute x16, starting transfers between devices: 15.8 us -> 20.6 us  [on_device(): across = lax.ppermute(hidden, both, across_pairs)]
  transfers between devices with their start and end apart: 37 -> 37, of which waited for: 32 -> 19; matrix products, arithmetic and copies ran while one was open for 3% -> 3% of each run, Pallas kernels for 8% -> 8%
where the time goes in v4:
time: 187 us; the launch traced here: 186 us
  waiting for transfers between devices  91.4 us (49%)
  starting transfers between devices  41.3 us (22%)
  Pallas kernels  28.1 us (15%)
  between operations  14.3 us (8%)
  local copies, waits for them, and re-layouts  8.04 us (4%)
  other arithmetic  3.39 us (2%)
    ppermute x16, waiting for transfers between devices, on_device(): across = lax.ppermute(hidden, both, across_pairs)  50.5 us
    ppermute x1, waiting for transfers between devices, on_device(): bundle = lax.ppermute(bundle, both, gather)  28.4 us
    ppermute x16, starting transfers between devices, on_device(): across = lax.ppermute(hidden, both, across_pairs)  20.6 us
    pallas_call x16, Pallas kernels, own_part(): pl.pallas_call(own_kernel, out_shape=jax.ShapeDtypeStruct(own.shape, jnp....  13.2 us
    pallas_call x16, Pallas kernels, layer(): pl.pallas_call(lambda *refs: layer_kernel(beta, *refs), out_shape=jax.Sha...  13 us
    ppermute x2, waiting for transfers between devices, on_device(): arrived = [lax.ppermute(value, both, scatter) for value in kept]  7.31 us
    ppermute x1, starting transfers between devices, on_device(): bundle = lax.ppermute(bundle, both, gather)  7.05 us
    ppermute x2, starting transfers between devices, on_device(): arrived = [lax.ppermute(value, both, scatter) for value in kept]  7.02 us
  transfers between devices with their start and end apart: 37, of which 19 were waited for; matrix products, arithmetic and copies ran while one was open for 3% of the time, Pallas kernels for 8%

profile of v4, /device:TPU:1, one launch (start us, length us, event | category | flops | bytes accessed | tf_op | source)
XLA Modules:
  0.0 186.5 jit_solution(3234261905923114837)
XLA Ops:
  9.3 7.1 %collective-permute-start = (bf16[5136,128]{1,0:T(8,128)(2,1)S(1)}, bf16[5136,128]{1,0:T(8,128)(2,1)S(1)}, u32[]{:S(2)}, u32[]{:S(2)}) collective-permute-start(bf16[5136,128]{1,0:T(8,128)(2,1)S(1)} %fusion.1), channel_id=1, source_target_pairs={{0,4},{1,20},{2,0},{3,16},{4,1},{5,17},{6,5},{7,21},{8,9},{9,25},{... | collective-permute-start | bytes 3944456 | tf_op jit(solution)/shard_map/ppermute | solution.py:143
  16.3 28.4 %collective-permute-done = bf16[5136,128]{1,0:T(8,128)(2,1)S(1)} collective-permute-done((bf16[5136,128]{1,0:T(8,128)(2,1)S(1)}, bf16[5136,128]{1,0:T(8,128)(2,1)S(1)}, u32[]{:S(2)}, u32[]{:S(2)}) %collective-permute-start) | collective-permute-done | bytes 1314848 | tf_op jit(solution)/shard_map/ppermute | solution.py:143
  45.6 1.8 shard_map.55
  49.8 3.2 %all-gather.2.cloned.1.call-done = bf16[16,256,256]{2,1,0:T(8,128)(2,1)} async-done(((bf16[1,256,256]{2,1,0:T(8,128)(2,1)}), bf16[16,256,256]{2,1,0:T(8,128)(2,1)}) %all-gather.2.cloned.1.call-update) | async-done | bytes 2097168 | tf_op jit(solution)/shard_map/all_gather | solution.py:129
  53.0 2.5 %slice_bitcast_fusion = (bf16[256,256]{1,0:T(8,128)(2,1)S(1)}, bf16[256,256]{1,0:T(8,128)(2,1)}, bf16[256,256]{1,0:T(8,128)(2,1)S(1)}, bf16[256,256]{1,0:T(8,128...) fusion(bf16[16,256,256]{2,1,0:T(8,128)(2,1)} %all-gather.2.clon, ...), kind=kLoop, calls=%fused_computation.12 | loop fusion | bytes 4194304 | tf_op jit(solution)/shard_map/squeeze | solution.py:162
  55.6 1.7 shard_map.57.own_ref
  59.7 3.7 %collective-permute-done.4.refs_4_ = bf16[512,256]{1,0:T(8,128)(2,1)S(1)} collective-permute-done((bf16[512,256]{1,0:T(8,128)(2,1)S(1)}, bf16[512,256]{1,0:T(8,128)(2,1)S(1)}, u32[]{:S(2)}, u32[]{:S(2)}) %collective-permute-start.4) | collective-permute-done | bytes 262176 | tf_op jit(solution)/shard_map/ppermute | solution.py:159
  66.5 3.7 %collective-permute-done.6.refs_4_ = bf16[512,256]{1,0:T(8,128)(2,1)S(1)} collective-permute-done((bf16[512,256]{1,0:T(8,128)(2,1)S(1)}, bf16[512,256]{1,0:T(8,128)(2,1)S(1)}, u32[]{:S(2)}, u32[]{:S(2)}) %collective-permute-start.6) | collective-permute-done | bytes 262176 | tf_op jit(solution)/shard_map/ppermute | solution.py:159
  73.3 3.7 %collective-permute-done.8.refs_4_ = bf16[512,256]{1,0:T(8,128)(2,1)S(1)} collective-permute-done((bf16[512,256]{1,0:T(8,128)(2,1)S(1)}, bf16[512,256]{1,0:T(8,128)(2,1)S(1)}, u32[]{:S(2)}, u32[]{:S(2)}) %collective-permute-start.8) | collective-permute-done | bytes 262176 | tf_op jit(solution)/shard_map/ppermute | solution.py:159
  77.6 1.4 collective-permute-start.10
  80.1 3.4 %collective-permute-done.10.refs_4_ = bf16[512,256]{1,0:T(8,128)(2,1)S(1)} collective-permute-done((bf16[512,256]{1,0:T(8,128)(2,1)S(1)}, bf16[512,256]{1,0:T(8,128)(2,1)S(1)}, u32[]{:S(2)}, u32[]{:S(2)}) %collective-permute-start.10) | collective-permute-done | bytes 262176 | tf_op jit(solution)/shard_map/ppermute | solution.py:159
  86.6 3.7 %collective-permute-done.12.refs_4_ = bf16[512,256]{1,0:T(8,128)(2,1)S(1)} collective-permute-done((bf16[512,256]{1,0:T(8,128)(2,1)S(1)}, bf16[512,256]{1,0:T(8,128)(2,1)S(1)}, u32[]{:S(2)}, u32[]{:S(2)}) %collective-permute-start.12) | collective-permute-done | bytes 262176 | tf_op jit(solution)/shard_map/ppermute | solution.py:159
  93.6 3.7 %collective-permute-done.14.refs_4_ = bf16[512,256]{1,0:T(8,128)(2,1)S(1)} collective-permute-done((bf16[512,256]{1,0:T(8,128)(2,1)S(1)}, bf16[512,256]{1,0:T(8,128)(2,1)S(1)}, u32[]{:S(2)}, u32[]{:S(2)}) %collective-permute-start.14) | collective-permute-done | bytes 262176 | tf_op jit(solution)/shard_map/ppermute | solution.py:159
  100.4 3.7 %collective-permute-done.16.refs_4_ = bf16[512,256]{1,0:T(8,128)(2,1)S(1)} collective-permute-done((bf16[512,256]{1,0:T(8,128)(2,1)S(1)}, bf16[512,256]{1,0:T(8,128)(2,1)S(1)}, u32[]{:S(2)}, u32[]{:S(2)}) %collective-permute-start.16) | collective-permute-done | bytes 262176 | tf_op jit(solution)/shard_map/ppermute | solution.py:159
  107.2 3.7 %collective-permute-done.18.refs_4_ = bf16[512,256]{1,0:T(8,128)(2,1)S(1)} collective-permute-done((bf16[512,256]{1,0:T(8,128)(2,1)S(1)}, bf16[512,256]{1,0:T(8,128)(2,1)S(1)}, u32[]{:S(2)}, u32[]{:S(2)}) %collective-permute-start.18) | collective-permute-done | bytes 262176 | tf_op jit(solution)/shard_map/ppermute | solution.py:159
  111.8 1.3 collective-permute-start.20
  114.0 3.7 %collective-permute-done.20.refs_4_ = bf16[512,256]{1,0:T(8,128)(2,1)S(1)} collective-permute-done((bf16[512,256]{1,0:T(8,128)(2,1)S(1)}, bf16[512,256]{1,0:T(8,128)(2,1)S(1)}, u32[]{:S(2)}, u32[]{:S(2)}) %collective-permute-start.20) | collective-permute-done | bytes 262176 | tf_op jit(solution)/shard_map/ppermute | solution.py:159
  118.6 1.3 collective-permute-start.22
  120.7 3.7 %collective-permute-done.22.refs_4_ = bf16[512,256]{1,0:T(8,128)(2,1)S(1)} collective-permute-done((bf16[512,256]{1,0:T(8,128)(2,1)S(1)}, bf16[512,256]{1,0:T(8,128)(2,1)S(1)}, u32[]{:S(2)}, u32[]{:S(2)}) %collective-permute-start.22) | collective-permute-done | bytes 262176 | tf_op jit(solution)/shard_map/ppermute | solution.py:159
  127.5 3.7 %collective-permute-done.24.refs_4_ = bf16[512,256]{1,0:T(8,128)(2,1)S(1)} collective-permute-done((bf16[512,256]{1,0:T(8,128)(2,1)S(1)}, bf16[512,256]{1,0:T(8,128)(2,1)S(1)}, u32[]{:S(2)}, u32[]{:S(2)}) %collective-permute-start.24) | collective-permute-done | bytes 262176 | tf_op jit(solution)/shard_map/ppermute | solution.py:159
  134.3 3.7 %collective-permute-done.26.refs_4_ = bf16[512,256]{1,0:T(8,128)(2,1)S(1)} collective-permute-done((bf16[512,256]{1,0:T(8,128)(2,1)S(1)}, bf16[512,256]{1,0:T(8,128)(2,1)S(1)}, u32[]{:S(2)}, u32[]{:S(2)}) %collective-permute-start.26) | collective-permute-done | bytes 262176 | tf_op jit(solution)/shard_map/ppermute | solution.py:159
  139.2 1.3 collective-permute-start.28
  141.3 3.7 %collective-permute-done.28.refs_4_ = bf16[512,256]{1,0:T(8,128)(2,1)S(1)} collective-permute-done((bf16[512,256]{1,0:T(8,128)(2,1)S(1)}, bf16[512,256]{1,0:T(8,128)(2,1)S(1)}, u32[]{:S(2)}, u32[]{:S(2)}) %collective-permute-start.28) | collective-permute-done | bytes 262176 | tf_op jit(solution)/shard_map/ppermute | solution.py:159
  145.0 1.4 shard_map.83.own_ref
  148.0 1.8 shard_map.84.refs_2_
  149.8 2.9 %collective-permute-done.30.refs_4_ = bf16[512,256]{1,0:T(8,128)(2,1)} collective-permute-done((bf16[512,256]{1,0:T(8,128)(2,1)}, bf16[512,256]{1,0:T(8,128)(2,1)}, u32[]{:S(2)}, u32[]{:S(2)}) %collective-permute-start.30) | collective-permute-done | bytes 262176 | tf_op jit(solution)/shard_map/ppermute | solution.py:159
  154.7 1.7 shard_map.85.own_ref
  156.8 1.3 collective-permute-start.33
  159.2 4.1 %collective-permute-start.31 = (bf16[512,256]{1,0:T(8,128)(2,1)}, bf16[512,256]{1,0:T(8,128)(2,1)}, u32[]{:S(2)}, u32[]{:S(2)}) collective-permute-start(bf16[512,256]{1,0:T(8,128)(2,1)} %select_select_fusion.1), channel_id=1, source_target_pairs={{4,0},{20,1},{0,2},{16,3},{1,4},{17,5},{5,6},{21,7},{9,8},{25,9},{... | collective-permute-start | bytes 786440 | tf_op jit(solution)/shard_map/ppermute | solution.py:165
  165.2 2.9 %collective-permute-start.34 = (bf16[512,256]{1,0:T(8,128)(2,1)S(1)}, bf16[512,256]{1,0:T(8,128)(2,1)S(1)}, u32[]{:S(2)}, u32[]{:S(2)}) collective-permute-start(bf16[512,256]{1,0:T(8,128)(2,1)S(1)} %select_select_fusion), channel_id=1, source_target_pairs={{4,0},{20,1},{0,2},{16,3},{1,4},{17,5},{5,6},{21,7},{9,8},{25,9},{... | collective-permute-start | bytes 786440 | tf_op jit(solution)/shard_map/ppermute | solution.py:165
  168.1 1.8 collective-permute-done.31
  169.9 5.5 %collective-permute-done.34 = bf16[512,256]{1,0:T(8,128)(2,1)S(1)} collective-permute-done((bf16[512,256]{1,0:T(8,128)(2,1)S(1)}, bf16[512,256]{1,0:T(8,128)(2,1)S(1)}, u32[]{:S(2)}, u32[]{:S(2)}) %collective-permute-start.34) | collective-permute-done | bytes 262176 | tf_op jit(solution)/shard_map/ppermute | solution.py:165
  (170 shorter events, 50.9 us)
Async XLA Ops:
  6.5 46.5 %all-gather.2.cloned.1.call-start = ((), (), s32[]{:S(2)}) async-start(), calls=%async_computation | async-start | bytes 2228224 | tf_op jit(solution)/shard_map/all_gather | solution.py:129
  9.3 35.5 %collective-permute-start = (bf16[5136,128]{1,0:T(8,128)(2,1)S(1)}, bf16[5136,128]{1,0:T(8,128)(2,1)S(1)}, u32[]{:S(2)}, u32[]{:S(2)}) collective-permute-start(bf16[5136,128]{1,0:T(8,128)(2,1)S(1)} %fusion.1), channel_id=1, source_target_pairs={{0,4},{1,20},{2,0},{3,16},{4,1},{5,17},{6,5},{7,21},{8,9},{9,25},{... | collective-permute-start | bytes 3944456 | tf_op jit(solution)/shard_map/ppermute | solution.py:143
  44.8 10.7 %collective-permute-start.1 = (bf16[512,256]{1,0:T(8,128)(2,1)S(1)}, bf16[512,256]{1,0:T(8,128)(2,1)}, u32[]{:S(2)}, u32[]{:S(2)}) collective-permute-start(bf16[512,256]{1,0:T(8,128)(2,1)S(1)} %pad_maximum_fusion.own_ref.refs_5_), channel_id=1, source_target_pairs={{0,16},{16,0},{32,48},{48,32},{64,80},{80,64},{96,112},{112,96},{1... | collective-permute-start | bytes 786440 | tf_op jit(solution)/shard_map/ppermute | solution.py:160
  44.9 10.6 %collective-permute-start.2 = (bf16[512,256]{1,0:T(8,128)(2,1)S(1)}, bf16[512,256]{1,0:T(8,128)(2,1)}, u32[]{:S(2)}, u32[]{:S(2)}) collective-permute-start(bf16[512,256]{1,0:T(8,128)(2,1)S(1)} %pad_maximum_fusion.own_ref.refs_5_), channel_id=1, source_target_pairs={{4,24},{20,0},{0,20},{16,1},{1,16},{17,5},{5,17},{21,9},{9,21},{25... | collective-permute-start | bytes 786440 | tf_op jit(solution)/shard_map/ppermute | solution.py:159
  57.6 5.8 %collective-permute-start.4 = (bf16[512,256]{1,0:T(8,128)(2,1)S(1)}, bf16[512,256]{1,0:T(8,128)(2,1)S(1)}, u32[]{:S(2)}, u32[]{:S(2)}) collective-permute-start(bf16[512,256]{1,0:T(8,128)(2,1)S(1)} %shard_map.57.own_ref), channel_id=1, source_target_pairs={{4,24},{20,0},{0,20},{16,1},{1,16},{17,5},{5,17},{21,9},{9,21},{25... | collective-permute-start | bytes 786440 | tf_op jit(solution)/shard_map/ppermute | solution.py:159
  64.4 5.8 %collective-permute-start.6 = (bf16[512,256]{1,0:T(8,128)(2,1)S(1)}, bf16[512,256]{1,0:T(8,128)(2,1)S(1)}, u32[]{:S(2)}, u32[]{:S(2)}) collective-permute-start(bf16[512,256]{1,0:T(8,128)(2,1)S(1)} %shard_map.59.own_ref), channel_id=1, source_target_pairs={{4,24},{20,0},{0,20},{16,1},{1,16},{17,5},{5,17},{21,9},{9,21},{25... | collective-permute-start | bytes 786440 | tf_op jit(solution)/shard_map/ppermute | solution.py:159
  71.2 5.8 %collective-permute-start.8 = (bf16[512,256]{1,0:T(8,128)(2,1)S(1)}, bf16[512,256]{1,0:T(8,128)(2,1)S(1)}, u32[]{:S(2)}, u32[]{:S(2)}) collective-permute-start(bf16[512,256]{1,0:T(8,128)(2,1)S(1)} %shard_map.61.own_ref), channel_id=1, source_target_pairs={{4,24},{20,0},{0,20},{16,1},{1,16},{17,5},{5,17},{21,9},{9,21},{25... | collective-permute-start | bytes 786440 | tf_op jit(solution)/shard_map/ppermute | solution.py:159
  77.6 5.9 %collective-permute-start.10 = (bf16[512,256]{1,0:T(8,128)(2,1)S(1)}, bf16[512,256]{1,0:T(8,128)(2,1)S(1)}, u32[]{:S(2)}, u32[]{:S(2)}) collective-permute-start(bf16[512,256]{1,0:T(8,128)(2,1)S(1)} %shard_map.63.own_ref), channel_id=1, source_target_pairs={{4,24},{20,0},{0,20},{16,1},{1,16},{17,5},{5,17},{21,9},{9,21},{25... | collective-permute-start | bytes 786440 | tf_op jit(solution)/shard_map/ppermute | solution.py:159
  79.0 4.5 %collective-permute-start.9 = (bf16[512,256]{1,0:T(8,128)(2,1)S(1)}, bf16[512,256]{1,0:T(8,128)(2,1)S(1)}, u32[]{:S(2)}, u32[]{:S(2)}) collective-permute-start(bf16[512,256]{1,0:T(8,128)(2,1)S(1)} %shard_map.63.own_ref), channel_id=1, source_target_pairs={{0,16},{16,0},{32,48},{48,32},{64,80},{80,64},{96,112},{112,96},{1... | collective-permute-start | bytes 786440 | tf_op jit(solution)/shard_map/ppermute | solution.py:160
  84.2 2.5 %collective-permute-start.11 = (bf16[512,256]{1,0:T(8,128)(2,1)S(1)}, bf16[512,256]{1,0:T(8,128)(2,1)S(1)}, u32[]{:S(2)}, u32[]{:S(2)}) collective-permute-start(bf16[512,256]{1,0:T(8,128)(2,1)S(1)} %shard_map.65.own_ref), channel_id=1, source_target_pairs={{0,16},{16,0},{32,48},{48,32},{64,80},{80,64},{96,112},{112,96},{1... | collective-permute-start | bytes 786440 | tf_op jit(solution)/shard_map/ppermute | solution.py:160
  84.5 5.8 %collective-permute-start.12 = (bf16[512,256]{1,0:T(8,128)(2,1)S(1)}, bf16[512,256]{1,0:T(8,128)(2,1)S(1)}, u32[]{:S(2)}, u32[]{:S(2)}) collective-permute-start(bf16[512,256]{1,0:T(8,128)(2,1)S(1)} %shard_map.65.own_ref), channel_id=1, source_target_pairs={{4,24},{20,0},{0,20},{16,1},{1,16},{17,5},{5,17},{21,9},{9,21},{25... | collective-permute-start | bytes 786440 | tf_op jit(solution)/shard_map/ppermute | solution.py:159
  90.9 2.6 %collective-permute-start.13 = (bf16[512,256]{1,0:T(8,128)(2,1)S(1)}, bf16[512,256]{1,0:T(8,128)(2,1)S(1)}, u32[]{:S(2)}, u32[]{:S(2)}) collective-permute-start(bf16[512,256]{1,0:T(8,128)(2,1)S(1)} %shard_map.67.own_ref), channel_id=1, source_target_pairs={{0,16},{16,0},{32,48},{48,32},{64,80},{80,64},{96,112},{112,96},{1... | collective-permute-start | bytes 786440 | tf_op jit(solution)/shard_map/ppermute | solution.py:160
  91.5 5.8 %collective-permute-start.14 = (bf16[512,256]{1,0:T(8,128)(2,1)S(1)}, bf16[512,256]{1,0:T(8,128)(2,1)S(1)}, u32[]{:S(2)}, u32[]{:S(2)}) collective-permute-start(bf16[512,256]{1,0:T(8,128)(2,1)S(1)} %shard_map.67.own_ref), channel_id=1, source_target_pairs={{4,24},{20,0},{0,20},{16,1},{1,16},{17,5},{5,17},{21,9},{9,21},{25... | collective-permute-start | bytes 786440 | tf_op jit(solution)/shard_map/ppermute | solution.py:159
  97.9 2.5 %collective-permute-start.15 = (bf16[512,256]{1,0:T(8,128)(2,1)S(1)}, bf16[512,256]{1,0:T(8,128)(2,1)S(1)}, u32[]{:S(2)}, u32[]{:S(2)}) collective-permute-start(bf16[512,256]{1,0:T(8,128)(2,1)S(1)} %shard_map.69.own_ref), channel_id=1, source_target_pairs={{0,16},{16,0},{32,48},{48,32},{64,80},{80,64},{96,112},{112,96},{1... | collective-permute-start | bytes 786440 | tf_op jit(solution)/shard_map/ppermute | solution.py:160
  98.3 5.8 %collective-permute-start.16 = (bf16[512,256]{1,0:T(8,128)(2,1)S(1)}, bf16[512,256]{1,0:T(8,128)(2,1)S(1)}, u32[]{:S(2)}, u32[]{:S(2)}) collective-permute-start(bf16[512,256]{1,0:T(8,128)(2,1)S(1)} %shard_map.69.own_ref), channel_id=1, source_target_pairs={{4,24},{20,0},{0,20},{16,1},{1,16},{17,5},{5,17},{21,9},{9,21},{25... | collective-permute-start | bytes 786440 | tf_op jit(solution)/shard_map/ppermute | solution.py:159
  105.0 5.8 %collective-permute-start.18 = (bf16[512,256]{1,0:T(8,128)(2,1)S(1)}, bf16[512,256]{1,0:T(8,128)(2,1)S(1)}, u32[]{:S(2)}, u32[]{:S(2)}) collective-permute-start(bf16[512,256]{1,0:T(8,128)(2,1)S(1)} %shard_map.71.own_ref), channel_id=1, source_target_pairs={{4,24},{20,0},{0,20},{16,1},{1,16},{17,5},{5,17},{21,9},{9,21},{25... | collective-permute-start | bytes 786440 | tf_op jit(solution)/shard_map/ppermute | solution.py:159
  111.5 2.5 %collective-permute-start.19 = (bf16[512,256]{1,0:T(8,128)(2,1)S(1)}, bf16[512,256]{1,0:T(8,128)(2,1)S(1)}, u32[]{:S(2)}, u32[]{:S(2)}) collective-permute-start(bf16[512,256]{1,0:T(8,128)(2,1)S(1)} %shard_map.73.own_ref), channel_id=1, source_target_pairs={{0,16},{16,0},{32,48},{48,32},{64,80},{80,64},{96,112},{112,96},{1... | collective-permute-start | bytes 786440 | tf_op jit(solution)/shard_map/ppermute | solution.py:160
  111.8 5.8 %collective-permute-start.20 = (bf16[512,256]{1,0:T(8,128)(2,1)S(1)}, bf16[512,256]{1,0:T(8,128)(2,1)S(1)}, u32[]{:S(2)}, u32[]{:S(2)}) collective-permute-start(bf16[512,256]{1,0:T(8,128)(2,1)S(1)} %shard_map.73.own_ref), channel_id=1, source_target_pairs={{4,24},{20,0},{0,20},{16,1},{1,16},{17,5},{5,17},{21,9},{9,21},{25... | collective-permute-start | bytes 786440 | tf_op jit(solution)/shard_map/ppermute | solution.py:159
  118.3 2.5 %collective-permute-start.21 = (bf16[512,256]{1,0:T(8,128)(2,1)S(1)}, bf16[512,256]{1,0:T(8,128)(2,1)S(1)}, u32[]{:S(2)}, u32[]{:S(2)}) collective-permute-start(bf16[512,256]{1,0:T(8,128)(2,1)S(1)} %shard_map.75.own_ref), channel_id=1, source_target_pairs={{0,16},{16,0},{32,48},{48,32},{64,80},{80,64},{96,112},{112,96},{1... | collective-permute-start | bytes 786440 | tf_op jit(solution)/shard_map/ppermute | solution.py:160
  118.6 5.8 %collective-permute-start.22 = (bf16[512,256]{1,0:T(8,128)(2,1)S(1)}, bf16[512,256]{1,0:T(8,128)(2,1)S(1)}, u32[]{:S(2)}, u32[]{:S(2)}) collective-permute-start(bf16[512,256]{1,0:T(8,128)(2,1)S(1)} %shard_map.75.own_ref), channel_id=1, source_target_pairs={{4,24},{20,0},{0,20},{16,1},{1,16},{17,5},{5,17},{21,9},{9,21},{25... | collective-permute-start | bytes 786440 | tf_op jit(solution)/shard_map/ppermute | solution.py:159
  125.1 2.5 %collective-permute-start.23 = (bf16[512,256]{1,0:T(8,128)(2,1)S(1)}, bf16[512,256]{1,0:T(8,128)(2,1)S(1)}, u32[]{:S(2)}, u32[]{:S(2)}) collective-permute-start(bf16[512,256]{1,0:T(8,128)(2,1)S(1)} %shard_map.77.own_ref), channel_id=1, source_target_pairs={{0,16},{16,0},{32,48},{48,32},{64,80},{80,64},{96,112},{112,96},{1... | collective-permute-start | bytes 786440 | tf_op jit(solution)/shard_map/ppermute | solution.py:160
  125.4 5.8 %collective-permute-start.24 = (bf16[512,256]{1,0:T(8,128)(2,1)S(1)}, bf16[512,256]{1,0:T(8,128)(2,1)S(1)}, u32[]{:S(2)}, u32[]{:S(2)}) collective-permute-start(bf16[512,256]{1,0:T(8,128)(2,1)S(1)} %shard_map.77.own_ref), channel_id=1, source_target_pairs={{4,24},{20,0},{0,20},{16,1},{1,16},{17,5},{5,17},{21,9},{9,21},{25... | collective-permute-start | bytes 786440 | tf_op jit(solution)/shard_map/ppermute | solution.py:159
  131.9 2.4 %collective-permute-start.25 = (bf16[512,256]{1,0:T(8,128)(2,1)S(1)}, bf16[512,256]{1,0:T(8,128)(2,1)S(1)}, u32[]{:S(2)}, u32[]{:S(2)}) collective-permute-start(bf16[512,256]{1,0:T(8,128)(2,1)S(1)} %shard_map.79.own_ref), channel_id=1, source_target_pairs={{0,16},{16,0},{32,48},{48,32},{64,80},{80,64},{96,112},{112,96},{1... | collective-permute-start | bytes 786440 | tf_op jit(solution)/shard_map/ppermute | solution.py:160
  132.2 5.8 %collective-permute-start.26 = (bf16[512,256]{1,0:T(8,128)(2,1)S(1)}, bf16[512,256]{1,0:T(8,128)(2,1)S(1)}, u32[]{:S(2)}, u32[]{:S(2)}) collective-permute-start(bf16[512,256]{1,0:T(8,128)(2,1)S(1)} %shard_map.79.own_ref), channel_id=1, source_target_pairs={{4,24},{20,0},{0,20},{16,1},{1,16},{17,5},{5,17},{21,9},{9,21},{25... | collective-permute-start | bytes 786440 | tf_op jit(solution)/shard_map/ppermute | solution.py:159
  138.6 2.7 %collective-permute-start.27 = (bf16[512,256]{1,0:T(8,128)(2,1)S(1)}, bf16[512,256]{1,0:T(8,128)(2,1)S(1)}, u32[]{:S(2)}, u32[]{:S(2)}) collective-permute-start(bf16[512,256]{1,0:T(8,128)(2,1)S(1)} %shard_map.81.own_ref), channel_id=1, source_target_pairs={{0,16},{16,0},{32,48},{48,32},{64,80},{80,64},{96,112},{112,96},{1... | collective-permute-start | bytes 786440 | tf_op jit(solution)/shard_map/ppermute | solution.py:160
  139.2 5.8 %collective-permute-start.28 = (bf16[512,256]{1,0:T(8,128)(2,1)S(1)}, bf16[512,256]{1,0:T(8,128)(2,1)S(1)}, u32[]{:S(2)}, u32[]{:S(2)}) collective-permute-start(bf16[512,256]{1,0:T(8,128)(2,1)S(1)} %shard_map.81.own_ref), channel_id=1, source_target_pairs={{4,24},{20,0},{0,20},{16,1},{1,16},{17,5},{5,17},{21,9},{9,21},{25... | collective-permute-start | bytes 786440 | tf_op jit(solution)/shard_map/ppermute | solution.py:159
  146.4 3.4 %collective-permute-start.29 = (bf16[512,256]{1,0:T(8,128)(2,1)}, bf16[512,256]{1,0:T(8,128)(2,1)}, u32[]{:S(2)}, u32[]{:S(2)}) collective-permute-start(bf16[512,256]{1,0:T(8,128)(2,1)} %shard_map.83.own_ref), channel_id=1, source_target_pairs={{0,16},{16,0},{32,48},{48,32},{64,80},{80,64},{96,112},{112,96},{1... | collective-permute-start | bytes 786440 | tf_op jit(solution)/shard_map/ppermute | solution.py:160
  146.6 6.1 %collective-permute-start.30 = (bf16[512,256]{1,0:T(8,128)(2,1)}, bf16[512,256]{1,0:T(8,128)(2,1)}, u32[]{:S(2)}, u32[]{:S(2)}) collective-permute-start(bf16[512,256]{1,0:T(8,128)(2,1)} %shard_map.83.own_ref), channel_id=1, source_target_pairs={{4,24},{20,0},{0,20},{16,1},{1,16},{17,5},{5,17},{21,9},{9,21},{25... | collective-permute-start | bytes 786440 | tf_op jit(solution)/shard_map/ppermute | solution.py:159
  156.5 7.7 %collective-permute-start.32 = (bf16[512,256]{1,0:T(8,128)(2,1)S(1)}, bf16[512,256]{1,0:T(8,128)(2,1)S(1)}, u32[]{:S(2)}, u32[]{:S(2)}) collective-permute-start(bf16[512,256]{1,0:T(8,128)(2,1)S(1)} %shard_map.85.own_ref), channel_id=1, source_target_pairs={{0,16},{16,0},{32,48},{48,32},{64,80},{80,64},{96,112},{112,96},{1... | collective-permute-start | bytes 786440 | tf_op jit(solution)/shard_map/ppermute | solution.py:160
  156.8 7.4 %collective-permute-start.33 = (bf16[512,256]{1,0:T(8,128)(2,1)S(1)}, bf16[512,256]{1,0:T(8,128)(2,1)S(1)}, u32[]{:S(2)}, u32[]{:S(2)}) collective-permute-start(bf16[512,256]{1,0:T(8,128)(2,1)S(1)} %shard_map.85.own_ref), channel_id=1, source_target_pairs={{4,24},{20,0},{0,20},{16,1},{1,16},{17,5},{5,17},{21,9},{9,21},{25... | collective-permute-start | bytes 786440 | tf_op jit(solution)/shard_map/ppermute | solution.py:159
  159.2 10.6 %collective-permute-start.31 = (bf16[512,256]{1,0:T(8,128)(2,1)}, bf16[512,256]{1,0:T(8,128)(2,1)}, u32[]{:S(2)}, u32[]{:S(2)}) collective-permute-start(bf16[512,256]{1,0:T(8,128)(2,1)} %select_select_fusion.1), channel_id=1, source_target_pairs={{4,0},{20,1},{0,2},{16,3},{1,4},{17,5},{5,6},{21,7},{9,8},{25,9},{... | collective-permute-start | bytes 786440 | tf_op jit(solution)/shard_map/ppermute | solution.py:165
  165.2 10.2 %collective-permute-start.34 = (bf16[512,256]{1,0:T(8,128)(2,1)S(1)}, bf16[512,256]{1,0:T(8,128)(2,1)S(1)}, u32[]{:S(2)}, u32[]{:S(2)}) collective-permute-start(bf16[512,256]{1,0:T(8,128)(2,1)S(1)} %select_select_fusion), channel_id=1, source_target_pairs={{4,0},{20,1},{0,2},{16,3},{1,4},{17,5},{5,6},{21,7},{9,8},{25,9},{... | collective-permute-start | bytes 786440 | tf_op jit(solution)/shard_map/ppermute | solution.py:165
  (44 other events, 249.5 us)
Sparse Core Ops, SparseCore 0:
  9.2 43.7 all-gather.1

commit v5 on v4

--- a/solution.py
+++ b/solution.py
@@ -57,42 +57,41 @@
     return first + second
 
 
-def own_kernel(dense_ref, own_ref, part_ref):
+def near_kernel(to_own_ref, to_beside_ref, own_ref, beside_ref, part_ref):
     @pl.loop(0, 4)
     def _(r):
         rows = pl.ds(pl.multiple_of(r * BLOCK, BLOCK), BLOCK)
-        part_ref[rows, :] = product(dense_ref, own_ref, rows)
+        part_ref[rows, :] = product(to_own_ref, own_ref, rows) + product(to_beside_ref, beside_ref, rows)
 
 
-def own_part(dense, own):
+def near_part(to_own, to_beside, own, beside):
     return pl.pallas_call(
-        own_kernel,
+        near_kernel,
         out_shape=jax.ShapeDtypeStruct(own.shape, jnp.float32),
-        in_specs=[VMEM, VMEM],
+        in_specs=[VMEM] * 4,
         out_specs=VMEM,
-        compiler_params=pltpu.CompilerParams(vmem_limit_bytes=12 << 20),
-        cost_estimate=pl.CostEstimate(flops=2 * 512 * 512 * 256, bytes_accessed=1 << 20, transcendentals=0),
-    )(dense, own)
+        compiler_params=pltpu.CompilerParams(vmem_limit_bytes=8 << 20),
+        cost_estimate=pl.CostEstimate(flops=2 * 512 * 1024 * 256, bytes_accessed=2 << 20, transcendentals=0),
+    )(to_own, to_beside, own, beside)
 
 
-def layer_kernel(beta, to_before_ref, to_after_ref, part_ref, before_ref, after_ref, initial_ref, weight_ref, out_ref):
-    aggregate = part_ref[...] + product(to_before_ref, before_ref)
-    aggregate = aggregate + product(to_after_ref, after_ref)
+def layer_kernel(beta, to_across_ref, part_ref, across_ref, initial_ref, weight_ref, out_ref):
+    aggregate = part_ref[...] + product(to_across_ref, across_ref)
     support = (0.9 * aggregate + 0.1 * initial_ref[...].astype(jnp.float32)).astype(jnp.bfloat16)
     branch = jnp.dot(support, weight_ref[...], preferred_element_type=jnp.float32)
     combined = (1.0 - beta) * support.astype(jnp.float32) + beta * branch
     out_ref[...] = jnp.maximum(combined, 0.0).astype(jnp.bfloat16)
 
 
-def layer(beta, to_before, to_after, part, before, after, initial, weight):
+def layer(beta, to_across, part, across, initial, weight):
     return pl.pallas_call(
         lambda *refs: layer_kernel(beta, *refs),
         out_shape=jax.ShapeDtypeStruct(initial.shape, jnp.bfloat16),
-        in_specs=[VMEM] * 7,
+        in_specs=[VMEM] * 5,
         out_specs=VMEM,
-        compiler_params=pltpu.CompilerParams(vmem_limit_bytes=12 << 20),
-        cost_estimate=pl.CostEstimate(flops=2 * 512 * 1280 * 256, bytes_accessed=2 << 20, transcendentals=0),
-    )(to_before, to_after, part, before, after, initial, weight)
+        compiler_params=pltpu.CompilerParams(vmem_limit_bytes=8 << 20),
+        cost_estimate=pl.CostEstimate(flops=2 * 512 * 768 * 256, bytes_accessed=2 << 20, transcendentals=0),
+    )(to_across, part, across, initial, weight)
 
 
 RINGS = (
@@ -137,18 +136,13 @@
     places = jnp.where(jnp.arange(slots, dtype=jnp.int32)[None, :] < count[:, None], places, 12)
     note = jnp.zeros((16, BLOCK), jnp.bfloat16).at[0:per_group, 0:slots].set(places.astype(jnp.bfloat16))
 
-    mine = lax.dynamic_index_in_dim(features, core, 0, keepdims=False)
+    initial = lax.ppermute(lax.dynamic_index_in_dim(features, core, 0, keepdims=False), both, gather)
     mine_tiles = lax.dynamic_index_in_dim(tiles, core, 0, keepdims=False).reshape(-1, BLOCK)
-    bundle = jnp.concatenate([mine_tiles, mine[:, :BLOCK], mine[:, BLOCK:], note], axis=0)
-    bundle = lax.ppermute(bundle, both, gather)
+    bundle = lax.ppermute(jnp.concatenate([mine_tiles, note], axis=0), both, gather)
 
     tile_rows = mine_tiles.shape[0]
-    rows = mine.shape[0]
     held_tiles = bundle[:tile_rows].reshape(-1, BLOCK, BLOCK)
-    initial = jnp.concatenate(
-        [bundle[tile_rows : tile_rows + rows], bundle[tile_rows + rows : tile_rows + 2 * rows]], axis=1
-    )
-    held_places = bundle[tile_rows + 2 * rows :][0:per_group, 0:slots].astype(jnp.int32)
+    held_places = bundle[tile_rows:][0:per_group, 0:slots].astype(jnp.int32)
     to_own, to_beside, to_across = dense_adjacency(held_places, held_tiles)
 
     hidden = initial
@@ -156,19 +150,20 @@
     low = seg - core
     for step in range(layers):
         beta = math.log(0.5 / (step + 1) + 1.0)
+        all_weights, hidden = lax.optimization_barrier((all_weights, hidden)) if step else (all_weights, hidden)
         across = lax.ppermute(hidden, both, across_pairs)
         beside = lax.ppermute(hidden, "segment", swap)
-        part = own_part(to_own, hidden)
-        hidden = layer(beta, to_beside, to_across, part, beside, across, initial, all_weights[step])
+        part = near_part(to_own, to_beside, hidden, beside)
+        hidden = layer(beta, to_across, part, across, initial, all_weights[step])
         kept[step % 2] = jnp.where(low == step - step % 2, hidden, kept[step % 2])
 
     arrived = [lax.ppermute(value, both, scatter) for value in kept]
     mine_out = jnp.where(core == 0, arrived[0], arrived[1])
     give = jnp.where(core == 0, arrived[1], arrived[0])
     other = lax.ppermute(give, "segment", swap)
-    first = jnp.where(core == 0, mine_out, other)
-    second = jnp.where(core == 0, other, mine_out)
-    return jnp.stack([first, second])[None]
+    result = jnp.zeros((1,) + features.shape, jnp.bfloat16)
+    result = lax.dynamic_update_slice(result, mine_out[None, None], (0, core, 0, 0))
+    return lax.dynamic_update_slice(result, other[None, None], (0, 1 - core, 0, 0))
 
 
 def solution(mesh):

time: 187 us -> 183 us (0.979)
  waiting for transfers between devices: 91.4 us -> 73.4 us
  local copies, waits for them, and re-layouts: 8.04 us -> 20.3 us
    ppermute x16, waiting for transfers between devices: 50.5 us -> 34.1 us  [on_device(): across = lax.ppermute(hidden, both, across_pairs)]
    squeeze x2 -> x17, local copies, waits for them, and re-layouts: 3.48 us -> 14.7 us  [the longest x16 14.7 us: on_device(): hidden = layer(beta, to_across, part, across, initial, all_weights[step])]
    pallas_call x16, Pallas kernels: 13.2 us -> 16.5 us  [near_part(): pl.pallas_call(near_kernel, out_shape=jax.ShapeDtypeStruct(own.shape, jnp...]
    ppermute x1 -> x2, starting transfers between devices: 7.05 us -> 9.5 us  [the longest x1 7.05 us: on_device(): lax.ppermute(jnp.concatenate([mine_tiles, note], axis=0), both, gather)]
    ppermute x1 -> x2, waiting for transfers between devices: 28.4 us -> 26 us  [the longest x1 26 us: on_device(): lax.ppermute(lax.dynamic_index_in_dim(features, core, 0, keepdims=False),...]
    pallas_call x16, Pallas kernels: 13 us -> 10.6 us  [layer(): pl.pallas_call(lambda *refs: layer_kernel(beta, *refs), out_shape=jax.Sha...]
    unnamed x78 -> x72, local copies, waits for them, and re-layouts: 3.66 us -> 3.96 us
  transfers between devices with their start and end apart: 37 -> 38, of which waited for: 19 -> 19; matrix products, arithmetic and copies ran while one was open for 3% -> 9% of each run, Pallas kernels for 8% -> 10%
where the time goes in v5:
time: 183 us; the launch traced here: 182 us
  waiting for transfers between devices  73.4 us (40%)
  starting transfers between devices  42.9 us (23%)
  Pallas kernels  28.9 us (16%)
  local copies, waits for them, and re-layouts  20.3 us (11%)
  between operations  14.4 us (8%)
  other arithmetic  2.14 us (1%)
    ppermute x16, waiting for transfers between devices, on_device(): across = lax.ppermute(hidden, both, across_pairs)  34.1 us
    ppermute x1, waiting for transfers between devices, on_device(): lax.ppermute(lax.dynamic_index_in_dim(features, core, 0, keepdims=False),...  26 us
    ppermute x16, starting transfers between devices, on_device(): across = lax.ppermute(hidden, both, across_pairs)  20.4 us
    pallas_call x16, Pallas kernels, near_part(): pl.pallas_call(near_kernel, out_shape=jax.ShapeDtypeStruct(own.shape, jnp...  16.5 us
    squeeze x16, local copies, waits for them, and re-layouts, on_device(): hidden = layer(beta, to_across, part, across, initial, all_weights[step])  14.7 us
    pallas_call x16, Pallas kernels, layer(): pl.pallas_call(lambda *refs: layer_kernel(beta, *refs), out_shape=jax.Sha...  10.6 us
    ppermute x2, waiting for transfers between devices, on_device(): arrived = [lax.ppermute(value, both, scatter) for value in kept]  7.43 us
    ppermute x1, starting transfers between devices, on_device(): lax.ppermute(jnp.concatenate([mine_tiles, note], axis=0), both, gather)  7.05 us
  transfers between devices with their start and end apart: 38, of which 19 were waited for; matrix products, arithmetic and copies ran while one was open for 9% of the time, Pallas kernels for 10%

profile of v5, /device:TPU:1, one launch (start us, length us, event | category | flops | bytes accessed | tf_op | source)
XLA Modules:
  0.0 182.0 jit_solution(2006011862485388576)
XLA Ops:
  8.4 7.1 %collective-permute-start = (bf16[4112,128]{1,0:T(8,128)(2,1)S(1)}, bf16[4112,128]{1,0:T(8,128)(2,1)S(1)}, u32[]{:S(2)}, u32[]{:S(2)}) collective-permute-start(bf16[4112,128]{1,0:T(8,128)(2,1)S(1)} %fusion.1), channel_id=1, source_target_pairs={{0,4},{1,20},{2,0},{3,16},{4,1},{5,17},{6,5},{7,21},{8,9},{9,25},{... | collective-permute-start | bytes 3158024 | tf_op jit(solution)/shard_map/ppermute | solution.py:141
  15.5 2.4 %collective-permute-start.1 = (bf16[512,256]{1,0:T(8,128)(2,1)S(1)}, bf16[512,256]{1,0:T(8,128)(2,1)S(1)}, u32[]{:S(2)}, u32[]{:S(2)}) collective-permute-start(bf16[512,256]{1,0:T(8,128)(2,1)S(1)} %dynamic-slice_bitcast_fusion), channel_id=1, source_target_pairs={{0,4},{1,20},{2,0},{3,16},{4,1},{5,17},{6,5},{7,21},{8,9},{9,25},{... | collective-permute-start | bytes 786440 | tf_op jit(solution)/shard_map/ppermute | solution.py:139
  18.0 26.0 %collective-permute-done.1.own_ref.refs_3_ = bf16[512,256]{1,0:T(8,128)(2,1)S(1)} collective-permute-done((bf16[512,256]{1,0:T(8,128)(2,1)S(1)}, bf16[512,256]{1,0:T(8,128)(2,1)S(1)}, u32[]{:S(2)}, u32[]{:S(2)}) %collective-permute-start.1) | collective-permute-done | bytes 262176 | tf_op jit(solution)/shard_map/ppermute | solution.py:139
  44.5 1.8 %shard_map.55 = (bf16[2,512,256]{2,1,0:T(8,128)(2,1)S(1)}, bf16[2,512,256]{2,1,0:T(8,128)(2,1)S(1)}, bf16[2,512,256]{2,1,0:T(8,128)(2,1)S(1)}) custom-call(s32[4,8]{1,0:T(4,128)S(1)} %slice_convert_fusion.places_ref, bf16[32,128,128]{2,1,0:T(8,128)(2,1)S(1)} %bitcast.46), custom_call_target="tpu_custom_call" | custom-call | tf_op jit(solution)/shard_map/pallas_call | solution.py:44
  48.9 4.1 %all-gather.2.cloned.1.call-done = bf16[16,256,256]{2,1,0:T(8,128)(2,1)} async-done(((bf16[1,256,256]{2,1,0:T(8,128)(2,1)}), bf16[16,256,256]{2,1,0:T(8,128)(2,1)}) %all-gather.2.cloned.1.call-update) | async-done | bytes 2097168 | tf_op jit(solution)/shard_map/all_gather | solution.py:128
  55.0 1.4 shard_map.57.own_ref
  60.1 2.6 %collective-permute-done.5.refs_2_ = bf16[512,256]{1,0:T(8,128)(2,1)S(1)} collective-permute-done((bf16[512,256]{1,0:T(8,128)(2,1)S(1)}, bf16[512,256]{1,0:T(8,128)(2,1)S(1)}, u32[]{:S(2)}, u32[]{:S(2)}) %collective-permute-start.5) | collective-permute-done | bytes 262176 | tf_op jit(solution)/shard_map/ppermute | solution.py:154
  63.5 1.3 collective-permute-start.7
  66.7 2.6 %collective-permute-done.7.refs_2_ = bf16[512,256]{1,0:T(8,128)(2,1)S(1)} collective-permute-done((bf16[512,256]{1,0:T(8,128)(2,1)S(1)}, bf16[512,256]{1,0:T(8,128)(2,1)S(1)}, u32[]{:S(2)}, u32[]{:S(2)}) %collective-permute-start.7) | collective-permute-done | bytes 262176 | tf_op jit(solution)/shard_map/ppermute | solution.py:154
  73.4 2.6 %collective-permute-done.9.refs_2_ = bf16[512,256]{1,0:T(8,128)(2,1)S(1)} collective-permute-done((bf16[512,256]{1,0:T(8,128)(2,1)S(1)}, bf16[512,256]{1,0:T(8,128)(2,1)S(1)}, u32[]{:S(2)}, u32[]{:S(2)}) %collective-permute-start.9) | collective-permute-done | bytes 262176 | tf_op jit(solution)/shard_map/ppermute | solution.py:154
  76.8 1.3 collective-permute-start.11
  80.1 2.6 %collective-permute-done.11.refs_2_ = bf16[512,256]{1,0:T(8,128)(2,1)S(1)} collective-permute-done((bf16[512,256]{1,0:T(8,128)(2,1)S(1)}, bf16[512,256]{1,0:T(8,128)(2,1)S(1)}, u32[]{:S(2)}, u32[]{:S(2)}) %collective-permute-start.11) | collective-permute-done | bytes 262176 | tf_op jit(solution)/shard_map/ppermute | solution.py:154
  86.7 2.6 %collective-permute-done.13.refs_2_ = bf16[512,256]{1,0:T(8,128)(2,1)S(1)} collective-permute-done((bf16[512,256]{1,0:T(8,128)(2,1)S(1)}, bf16[512,256]{1,0:T(8,128)(2,1)S(1)}, u32[]{:S(2)}, u32[]{:S(2)}) %collective-permute-start.13) | collective-permute-done | bytes 262176 | tf_op jit(solution)/shard_map/ppermute | solution.py:154
  90.2 1.4 collective-permute-start.15
  93.4 2.6 %collective-permute-done.15.refs_2_ = bf16[512,256]{1,0:T(8,128)(2,1)S(1)} collective-permute-done((bf16[512,256]{1,0:T(8,128)(2,1)S(1)}, bf16[512,256]{1,0:T(8,128)(2,1)S(1)}, u32[]{:S(2)}, u32[]{:S(2)}) %collective-permute-start.15) | collective-permute-done | bytes 262176 | tf_op jit(solution)/shard_map/ppermute | solution.py:154
  96.9 1.3 collective-permute-start.17
  100.1 2.6 %collective-permute-done.17.refs_2_ = bf16[512,256]{1,0:T(8,128)(2,1)S(1)} collective-permute-done((bf16[512,256]{1,0:T(8,128)(2,1)S(1)}, bf16[512,256]{1,0:T(8,128)(2,1)S(1)}, u32[]{:S(2)}, u32[]{:S(2)}) %collective-permute-start.17) | collective-permute-done | bytes 262176 | tf_op jit(solution)/shard_map/ppermute | solution.py:154
  106.7 2.6 %collective-permute-done.19.refs_2_ = bf16[512,256]{1,0:T(8,128)(2,1)S(1)} collective-permute-done((bf16[512,256]{1,0:T(8,128)(2,1)S(1)}, bf16[512,256]{1,0:T(8,128)(2,1)S(1)}, u32[]{:S(2)}, u32[]{:S(2)}) %collective-permute-start.19) | collective-permute-done | bytes 262176 | tf_op jit(solution)/shard_map/ppermute | solution.py:154
  110.2 1.3 collective-permute-start.21
  113.4 2.6 %collective-permute-done.21.refs_2_ = bf16[512,256]{1,0:T(8,128)(2,1)S(1)} collective-permute-done((bf16[512,256]{1,0:T(8,128)(2,1)S(1)}, bf16[512,256]{1,0:T(8,128)(2,1)S(1)}, u32[]{:S(2)}, u32[]{:S(2)}) %collective-permute-start.21) | collective-permute-done | bytes 262176 | tf_op jit(solution)/shard_map/ppermute | solution.py:154
  120.1 2.6 %collective-permute-done.23.refs_2_ = bf16[512,256]{1,0:T(8,128)(2,1)S(1)} collective-permute-done((bf16[512,256]{1,0:T(8,128)(2,1)S(1)}, bf16[512,256]{1,0:T(8,128)(2,1)S(1)}, u32[]{:S(2)}, u32[]{:S(2)}) %collective-permute-start.23) | collective-permute-done | bytes 262176 | tf_op jit(solution)/shard_map/ppermute | solution.py:154
  123.5 1.3 collective-permute-start.25
  126.7 2.6 %collective-permute-done.25.refs_2_ = bf16[512,256]{1,0:T(8,128)(2,1)S(1)} collective-permute-done((bf16[512,256]{1,0:T(8,128)(2,1)S(1)}, bf16[512,256]{1,0:T(8,128)(2,1)S(1)}, u32[]{:S(2)}, u32[]{:S(2)}) %collective-permute-start.25) | collective-permute-done | bytes 262176 | tf_op jit(solution)/shard_map/ppermute | solution.py:154
  133.4 2.6 %collective-permute-done.27.refs_2_ = bf16[512,256]{1,0:T(8,128)(2,1)S(1)} collective-permute-done((bf16[512,256]{1,0:T(8,128)(2,1)S(1)}, bf16[512,256]{1,0:T(8,128)(2,1)S(1)}, u32[]{:S(2)}, u32[]{:S(2)}) %collective-permute-start.27) | collective-permute-done | bytes 262176 | tf_op jit(solution)/shard_map/ppermute | solution.py:154
  136.9 1.4 collective-permute-start.29
  140.1 2.6 %collective-permute-done.29.refs_2_ = bf16[512,256]{1,0:T(8,128)(2,1)S(1)} collective-permute-done((bf16[512,256]{1,0:T(8,128)(2,1)S(1)}, bf16[512,256]{1,0:T(8,128)(2,1)S(1)}, u32[]{:S(2)}, u32[]{:S(2)}) %collective-permute-start.29) | collective-permute-done | bytes 262176 | tf_op jit(solution)/shard_map/ppermute | solution.py:154
  144.2 1.3 collective-permute-start.31
  147.5 2.1 %shard_map.84.refs_1_ = f32[512,256]{1,0:T(8,128)S(1)} custom-call(bf16[2,512,256]{2,1,0:T(8,128)(2,1)S(1)} %get-tuple-element.51.to_own_ref, bf16[2,512,256]{2,1,0:T(8,128)(2,1)S(1)} %copy-done.3, bf16[512,256]{1,0:T(8,128)(2,1)} %shard_map.83.own_ref, bf16[512,256]{1,0:T(8,128)(2,1)} %collective-permute-done.30.beside_ref), custom_call_target="tpu_custom_call" | custom-call | flops 268435456 | bytes 2097152 | tf_op jit(solution)/shard_map/pallas_call | solution.py:68
  150.3 1.4 shard_map.85.own_ref
  154.3 4.0 %collective-permute-start.32 = (bf16[512,256]{1,0:T(8,128)(2,1)}, bf16[512,256]{1,0:T(8,128)(2,1)}, u32[]{:S(2)}, u32[]{:S(2)}) collective-permute-start(bf16[512,256]{1,0:T(8,128)(2,1)} %select_select_fusion.1), channel_id=1, source_target_pairs={{4,0},{20,1},{0,2},{16,3},{1,4},{17,5},{5,6},{21,7},{9,8},{25,9},{... | collective-permute-start | bytes 786440 | tf_op jit(solution)/shard_map/ppermute | solution.py:160
  161.0 2.8 %collective-permute-start.35 = (bf16[512,256]{1,0:T(8,128)(2,1)S(1)}, bf16[512,256]{1,0:T(8,128)(2,1)S(1)}, u32[]{:S(2)}, u32[]{:S(2)}) collective-permute-start(bf16[512,256]{1,0:T(8,128)(2,1)S(1)} %select_select_fusion), channel_id=1, source_target_pairs={{4,0},{20,1},{0,2},{16,3},{1,4},{17,5},{5,6},{21,7},{9,8},{25,9},{... | collective-permute-start | bytes 786440 | tf_op jit(solution)/shard_map/ppermute | solution.py:160
  164.8 6.4 %collective-permute-done.35 = bf16[512,256]{1,0:T(8,128)(2,1)S(1)} collective-permute-done((bf16[512,256]{1,0:T(8,128)(2,1)S(1)}, bf16[512,256]{1,0:T(8,128)(2,1)S(1)}, u32[]{:S(2)}, u32[]{:S(2)}) %collective-permute-start.35) | collective-permute-done | bytes 262176 | tf_op jit(solution)/shard_map/ppermute | solution.py:160
  (179 shorter events, 63.9 us)
Async XLA Ops:
  6.5 46.5 %all-gather.2.cloned.1.call-start = ((), (), s32[]{:S(2)}) async-start(), calls=%async_computation | async-start | bytes 2228224 | tf_op jit(solution)/shard_map/all_gather | solution.py:128
  8.4 36.0 %collective-permute-start = (bf16[4112,128]{1,0:T(8,128)(2,1)S(1)}, bf16[4112,128]{1,0:T(8,128)(2,1)S(1)}, u32[]{:S(2)}, u32[]{:S(2)}) collective-permute-start(bf16[4112,128]{1,0:T(8,128)(2,1)S(1)} %fusion.1), channel_id=1, source_target_pairs={{0,4},{1,20},{2,0},{3,16},{4,1},{5,17},{6,5},{7,21},{8,9},{9,25},{... | collective-permute-start | bytes 3158024 | tf_op jit(solution)/shard_map/ppermute | solution.py:141
  15.5 28.5 %collective-permute-start.1 = (bf16[512,256]{1,0:T(8,128)(2,1)S(1)}, bf16[512,256]{1,0:T(8,128)(2,1)S(1)}, u32[]{:S(2)}, u32[]{:S(2)}) collective-permute-start(bf16[512,256]{1,0:T(8,128)(2,1)S(1)} %dynamic-slice_bitcast_fusion), channel_id=1, source_target_pairs={{0,4},{1,20},{2,0},{3,16},{4,1},{5,17},{6,5},{7,21},{8,9},{9,25},{... | collective-permute-start | bytes 786440 | tf_op jit(solution)/shard_map/ppermute | solution.py:139
  44.0 10.0 %collective-permute-start.3 = (bf16[512,256]{1,0:T(8,128)(2,1)S(1)}, bf16[512,256]{1,0:T(8,128)(2,1)}, u32[]{:S(2)}, u32[]{:S(2)}) collective-permute-start(bf16[512,256]{1,0:T(8,128)(2,1)S(1)} %collective-permute-done.1.own_ref.refs_3_), channel_id=1, source_target_pairs={{4,24},{20,0},{0,20},{16,1},{1,16},{17,5},{5,17},{21,9},{9,21},{25... | collective-permute-start | bytes 786440 | tf_op jit(solution)/shard_map/ppermute | solution.py:154
  56.5 2.6 %collective-permute-start.4 = (bf16[512,256]{1,0:T(8,128)(2,1)S(1)}, bf16[512,256]{1,0:T(8,128)(2,1)S(1)}, u32[]{:S(2)}, u32[]{:S(2)}) collective-permute-start(bf16[512,256]{1,0:T(8,128)(2,1)S(1)} %shard_map.57.own_ref), channel_id=1, source_target_pairs={{0,16},{16,0},{32,48},{48,32},{64,80},{80,64},{96,112},{112,96},{1... | collective-permute-start | bytes 786440 | tf_op jit(solution)/shard_map/ppermute | solution.py:155
  56.8 5.8 %collective-permute-start.5 = (bf16[512,256]{1,0:T(8,128)(2,1)S(1)}, bf16[512,256]{1,0:T(8,128)(2,1)S(1)}, u32[]{:S(2)}, u32[]{:S(2)}) collective-permute-start(bf16[512,256]{1,0:T(8,128)(2,1)S(1)} %shard_map.57.own_ref), channel_id=1, source_target_pairs={{4,24},{20,0},{0,20},{16,1},{1,16},{17,5},{5,17},{21,9},{9,21},{25... | collective-permute-start | bytes 786440 | tf_op jit(solution)/shard_map/ppermute | solution.py:154
  63.2 2.6 %collective-permute-start.6 = (bf16[512,256]{1,0:T(8,128)(2,1)S(1)}, bf16[512,256]{1,0:T(8,128)(2,1)S(1)}, u32[]{:S(2)}, u32[]{:S(2)}) collective-permute-start(bf16[512,256]{1,0:T(8,128)(2,1)S(1)} %shard_map.59.own_ref), channel_id=1, source_target_pairs={{0,16},{16,0},{32,48},{48,32},{64,80},{80,64},{96,112},{112,96},{1... | collective-permute-start | bytes 786440 | tf_op jit(solution)/shard_map/ppermute | solution.py:155
  63.5 5.8 %collective-permute-start.7 = (bf16[512,256]{1,0:T(8,128)(2,1)S(1)}, bf16[512,256]{1,0:T(8,128)(2,1)S(1)}, u32[]{:S(2)}, u32[]{:S(2)}) collective-permute-start(bf16[512,256]{1,0:T(8,128)(2,1)S(1)} %shard_map.59.own_ref), channel_id=1, source_target_pairs={{4,24},{20,0},{0,20},{16,1},{1,16},{17,5},{5,17},{21,9},{9,21},{25... | collective-permute-start | bytes 786440 | tf_op jit(solution)/shard_map/ppermute | solution.py:154
  69.8 2.6 %collective-permute-start.8 = (bf16[512,256]{1,0:T(8,128)(2,1)S(1)}, bf16[512,256]{1,0:T(8,128)(2,1)S(1)}, u32[]{:S(2)}, u32[]{:S(2)}) collective-permute-start(bf16[512,256]{1,0:T(8,128)(2,1)S(1)} %shard_map.61.own_ref), channel_id=1, source_target_pairs={{0,16},{16,0},{32,48},{48,32},{64,80},{80,64},{96,112},{112,96},{1... | collective-permute-start | bytes 786440 | tf_op jit(solution)/shard_map/ppermute | solution.py:155
  70.2 5.8 %collective-permute-start.9 = (bf16[512,256]{1,0:T(8,128)(2,1)S(1)}, bf16[512,256]{1,0:T(8,128)(2,1)S(1)}, u32[]{:S(2)}, u32[]{:S(2)}) collective-permute-start(bf16[512,256]{1,0:T(8,128)(2,1)S(1)} %shard_map.61.own_ref), channel_id=1, source_target_pairs={{4,24},{20,0},{0,20},{16,1},{1,16},{17,5},{5,17},{21,9},{9,21},{25... | collective-permute-start | bytes 786440 | tf_op jit(solution)/shard_map/ppermute | solution.py:154
  76.5 2.6 %collective-permute-start.10 = (bf16[512,256]{1,0:T(8,128)(2,1)S(1)}, bf16[512,256]{1,0:T(8,128)(2,1)S(1)}, u32[]{:S(2)}, u32[]{:S(2)}) collective-permute-start(bf16[512,256]{1,0:T(8,128)(2,1)S(1)} %shard_map.63.own_ref), channel_id=1, source_target_pairs={{0,16},{16,0},{32,48},{48,32},{64,80},{80,64},{96,112},{112,96},{1... | collective-permute-start | bytes 786440 | tf_op jit(solution)/shard_map/ppermute | solution.py:155
  76.8 5.8 %collective-permute-start.11 = (bf16[512,256]{1,0:T(8,128)(2,1)S(1)}, bf16[512,256]{1,0:T(8,128)(2,1)S(1)}, u32[]{:S(2)}, u32[]{:S(2)}) collective-permute-start(bf16[512,256]{1,0:T(8,128)(2,1)S(1)} %shard_map.63.own_ref), channel_id=1, source_target_pairs={{4,24},{20,0},{0,20},{16,1},{1,16},{17,5},{5,17},{21,9},{9,21},{25... | collective-permute-start | bytes 786440 | tf_op jit(solution)/shard_map/ppermute | solution.py:154
  83.2 2.6 %collective-permute-start.12 = (bf16[512,256]{1,0:T(8,128)(2,1)S(1)}, bf16[512,256]{1,0:T(8,128)(2,1)S(1)}, u32[]{:S(2)}, u32[]{:S(2)}) collective-permute-start(bf16[512,256]{1,0:T(8,128)(2,1)S(1)} %shard_map.65.own_ref), channel_id=1, source_target_pairs={{0,16},{16,0},{32,48},{48,32},{64,80},{80,64},{96,112},{112,96},{1... | collective-permute-start | bytes 786440 | tf_op jit(solution)/shard_map/ppermute | solution.py:155
  83.5 5.8 %collective-permute-start.13 = (bf16[512,256]{1,0:T(8,128)(2,1)S(1)}, bf16[512,256]{1,0:T(8,128)(2,1)S(1)}, u32[]{:S(2)}, u32[]{:S(2)}) collective-permute-start(bf16[512,256]{1,0:T(8,128)(2,1)S(1)} %shard_map.65.own_ref), channel_id=1, source_target_pairs={{4,24},{20,0},{0,20},{16,1},{1,16},{17,5},{5,17},{21,9},{9,21},{25... | collective-permute-start | bytes 786440 | tf_op jit(solution)/shard_map/ppermute | solution.py:154
  89.8 2.6 %collective-permute-start.14 = (bf16[512,256]{1,0:T(8,128)(2,1)S(1)}, bf16[512,256]{1,0:T(8,128)(2,1)S(1)}, u32[]{:S(2)}, u32[]{:S(2)}) collective-permute-start(bf16[512,256]{1,0:T(8,128)(2,1)S(1)} %shard_map.67.own_ref), channel_id=1, source_target_pairs={{0,16},{16,0},{32,48},{48,32},{64,80},{80,64},{96,112},{112,96},{1... | collective-permute-start | bytes 786440 | tf_op jit(solution)/shard_map/ppermute | solution.py:155
  90.2 5.8 %collective-permute-start.15 = (bf16[512,256]{1,0:T(8,128)(2,1)S(1)}, bf16[512,256]{1,0:T(8,128)(2,1)S(1)}, u32[]{:S(2)}, u32[]{:S(2)}) collective-permute-start(bf16[512,256]{1,0:T(8,128)(2,1)S(1)} %shard_map.67.own_ref), channel_id=1, source_target_pairs={{4,24},{20,0},{0,20},{16,1},{1,16},{17,5},{5,17},{21,9},{9,21},{25... | collective-permute-start | bytes 786440 | tf_op jit(solution)/shard_map/ppermute | solution.py:154
  96.9 5.8 %collective-permute-start.17 = (bf16[512,256]{1,0:T(8,128)(2,1)S(1)}, bf16[512,256]{1,0:T(8,128)(2,1)S(1)}, u32[]{:S(2)}, u32[]{:S(2)}) collective-permute-start(bf16[512,256]{1,0:T(8,128)(2,1)S(1)} %shard_map.69.own_ref), channel_id=1, source_target_pairs={{4,24},{20,0},{0,20},{16,1},{1,16},{17,5},{5,17},{21,9},{9,21},{25... | collective-permute-start | bytes 786440 | tf_op jit(solution)/shard_map/ppermute | solution.py:154
  103.2 2.6 %collective-permute-start.18 = (bf16[512,256]{1,0:T(8,128)(2,1)S(1)}, bf16[512,256]{1,0:T(8,128)(2,1)S(1)}, u32[]{:S(2)}, u32[]{:S(2)}) collective-permute-start(bf16[512,256]{1,0:T(8,128)(2,1)S(1)} %shard_map.71.own_ref), channel_id=1, source_target_pairs={{0,16},{16,0},{32,48},{48,32},{64,80},{80,64},{96,112},{112,96},{1... | collective-permute-start | bytes 786440 | tf_op jit(solution)/shard_map/ppermute | solution.py:155
  103.5 5.8 %collective-permute-start.19 = (bf16[512,256]{1,0:T(8,128)(2,1)S(1)}, bf16[512,256]{1,0:T(8,128)(2,1)S(1)}, u32[]{:S(2)}, u32[]{:S(2)}) collective-permute-start(bf16[512,256]{1,0:T(8,128)(2,1)S(1)} %shard_map.71.own_ref), channel_id=1, source_target_pairs={{4,24},{20,0},{0,20},{16,1},{1,16},{17,5},{5,17},{21,9},{9,21},{25... | collective-permute-start | bytes 786440 | tf_op jit(solution)/shard_map/ppermute | solution.py:154
  110.2 5.8 %collective-permute-start.21 = (bf16[512,256]{1,0:T(8,128)(2,1)S(1)}, bf16[512,256]{1,0:T(8,128)(2,1)S(1)}, u32[]{:S(2)}, u32[]{:S(2)}) collective-permute-start(bf16[512,256]{1,0:T(8,128)(2,1)S(1)} %shard_map.73.own_ref), channel_id=1, source_target_pairs={{4,24},{20,0},{0,20},{16,1},{1,16},{17,5},{5,17},{21,9},{9,21},{25... | collective-permute-start | bytes 786440 | tf_op jit(solution)/shard_map/ppermute | solution.py:154
  116.5 2.6 %collective-permute-start.22 = (bf16[512,256]{1,0:T(8,128)(2,1)S(1)}, bf16[512,256]{1,0:T(8,128)(2,1)S(1)}, u32[]{:S(2)}, u32[]{:S(2)}) collective-permute-start(bf16[512,256]{1,0:T(8,128)(2,1)S(1)} %shard_map.75.own_ref), channel_id=1, source_target_pairs={{0,16},{16,0},{32,48},{48,32},{64,80},{80,64},{96,112},{112,96},{1... | collective-permute-start | bytes 786440 | tf_op jit(solution)/shard_map/ppermute | solution.py:155
  116.9 5.8 %collective-permute-start.23 = (bf16[512,256]{1,0:T(8,128)(2,1)S(1)}, bf16[512,256]{1,0:T(8,128)(2,1)S(1)}, u32[]{:S(2)}, u32[]{:S(2)}) collective-permute-start(bf16[512,256]{1,0:T(8,128)(2,1)S(1)} %shard_map.75.own_ref), channel_id=1, source_target_pairs={{4,24},{20,0},{0,20},{16,1},{1,16},{17,5},{5,17},{21,9},{9,21},{25... | collective-permute-start | bytes 786440 | tf_op jit(solution)/shard_map/ppermute | solution.py:154
  123.5 5.8 %collective-permute-start.25 = (bf16[512,256]{1,0:T(8,128)(2,1)S(1)}, bf16[512,256]{1,0:T(8,128)(2,1)S(1)}, u32[]{:S(2)}, u32[]{:S(2)}) collective-permute-start(bf16[512,256]{1,0:T(8,128)(2,1)S(1)} %shard_map.77.own_ref), channel_id=1, source_target_pairs={{4,24},{20,0},{0,20},{16,1},{1,16},{17,5},{5,17},{21,9},{9,21},{25... | collective-permute-start | bytes 786440 | tf_op jit(solution)/shard_map/ppermute | solution.py:154
  129.8 2.6 %collective-permute-start.26 = (bf16[512,256]{1,0:T(8,128)(2,1)S(1)}, bf16[512,256]{1,0:T(8,128)(2,1)S(1)}, u32[]{:S(2)}, u32[]{:S(2)}) collective-permute-start(bf16[512,256]{1,0:T(8,128)(2,1)S(1)} %shard_map.79.own_ref), channel_id=1, source_target_pairs={{0,16},{16,0},{32,48},{48,32},{64,80},{80,64},{96,112},{112,96},{1... | collective-permute-start | bytes 786440 | tf_op jit(solution)/shard_map/ppermute | solution.py:155
  130.2 5.8 %collective-permute-start.27 = (bf16[512,256]{1,0:T(8,128)(2,1)S(1)}, bf16[512,256]{1,0:T(8,128)(2,1)S(1)}, u32[]{:S(2)}, u32[]{:S(2)}) collective-permute-start(bf16[512,256]{1,0:T(8,128)(2,1)S(1)} %shard_map.79.own_ref), channel_id=1, source_target_pairs={{4,24},{20,0},{0,20},{16,1},{1,16},{17,5},{5,17},{21,9},{9,21},{25... | collective-permute-start | bytes 786440 | tf_op jit(solution)/shard_map/ppermute | solution.py:154
  136.5 2.7 %collective-permute-start.28 = (bf16[512,256]{1,0:T(8,128)(2,1)S(1)}, bf16[512,256]{1,0:T(8,128)(2,1)S(1)}, u32[]{:S(2)}, u32[]{:S(2)}) collective-permute-start(bf16[512,256]{1,0:T(8,128)(2,1)S(1)} %shard_map.81.own_ref), channel_id=1, source_target_pairs={{0,16},{16,0},{32,48},{48,32},{64,80},{80,64},{96,112},{112,96},{1... | collective-permute-start | bytes 786440 | tf_op jit(solution)/shard_map/ppermute | solution.py:155
  136.9 5.9 %collective-permute-start.29 = (bf16[512,256]{1,0:T(8,128)(2,1)S(1)}, bf16[512,256]{1,0:T(8,128)(2,1)S(1)}, u32[]{:S(2)}, u32[]{:S(2)}) collective-permute-start(bf16[512,256]{1,0:T(8,128)(2,1)S(1)} %shard_map.81.own_ref), channel_id=1, source_target_pairs={{4,24},{20,0},{0,20},{16,1},{1,16},{17,5},{5,17},{21,9},{9,21},{25... | collective-permute-start | bytes 786440 | tf_op jit(solution)/shard_map/ppermute | solution.py:154
  144.2 6.1 %collective-permute-start.31 = (bf16[512,256]{1,0:T(8,128)(2,1)}, bf16[512,256]{1,0:T(8,128)(2,1)}, u32[]{:S(2)}, u32[]{:S(2)}) collective-permute-start(bf16[512,256]{1,0:T(8,128)(2,1)} %shard_map.83.own_ref), channel_id=1, source_target_pairs={{4,24},{20,0},{0,20},{16,1},{1,16},{17,5},{5,17},{21,9},{9,21},{25... | collective-permute-start | bytes 786440 | tf_op jit(solution)/shard_map/ppermute | solution.py:154
  151.8 7.5 %collective-permute-start.33 = (bf16[512,256]{1,0:T(8,128)(2,1)S(1)}, bf16[512,256]{1,0:T(8,128)(2,1)S(1)}, u32[]{:S(2)}, u32[]{:S(2)}) collective-permute-start(bf16[512,256]{1,0:T(8,128)(2,1)S(1)} %shard_map.85.own_ref), channel_id=1, source_target_pairs={{0,16},{16,0},{32,48},{48,32},{64,80},{80,64},{96,112},{112,96},{1... | collective-permute-start | bytes 786440 | tf_op jit(solution)/shard_map/ppermute | solution.py:155
  152.1 8.1 %collective-permute-start.34 = (bf16[512,256]{1,0:T(8,128)(2,1)S(1)}, bf16[512,256]{1,0:T(8,128)(2,1)S(1)}, u32[]{:S(2)}, u32[]{:S(2)}) collective-permute-start(bf16[512,256]{1,0:T(8,128)(2,1)S(1)} %shard_map.85.own_ref), channel_id=1, source_target_pairs={{4,24},{20,0},{0,20},{16,1},{1,16},{17,5},{5,17},{21,9},{9,21},{25... | collective-permute-start | bytes 786440 | tf_op jit(solution)/shard_map/ppermute | solution.py:154
  154.3 10.5 %collective-permute-start.32 = (bf16[512,256]{1,0:T(8,128)(2,1)}, bf16[512,256]{1,0:T(8,128)(2,1)}, u32[]{:S(2)}, u32[]{:S(2)}) collective-permute-start(bf16[512,256]{1,0:T(8,128)(2,1)} %select_select_fusion.1), channel_id=1, source_target_pairs={{4,0},{20,1},{0,2},{16,3},{1,4},{17,5},{5,6},{21,7},{9,8},{25,9},{... | collective-permute-start | bytes 786440 | tf_op jit(solution)/shard_map/ppermute | solution.py:160
  161.0 10.2 %collective-permute-start.35 = (bf16[512,256]{1,0:T(8,128)(2,1)S(1)}, bf16[512,256]{1,0:T(8,128)(2,1)S(1)}, u32[]{:S(2)}, u32[]{:S(2)}) collective-permute-start(bf16[512,256]{1,0:T(8,128)(2,1)S(1)} %select_select_fusion), channel_id=1, source_target_pairs={{4,0},{20,1},{0,2},{16,3},{1,4},{17,5},{5,6},{21,7},{9,8},{25,9},{... | collective-permute-start | bytes 786440 | tf_op jit(solution)/shard_map/ppermute | solution.py:160
  (42 other events, 181.2 us)
Sparse Core Ops, SparseCore 0:
  9.2 43.7 all-gather.1
